TPU v7x, 128 devices: a whole 4x4x4 slice. The times are simulated.
128 devices in a mesh: dp: 4 (over z), sy: 8 (over x, core), sx: 4 (over y).
Axes of the slice: x: 4, y: 4, z: 4, core: 2. Of those that a mesh axis runs over, the one named last changes fastest.
Arguments:
- input_gates: bfloat16 [4, 3, 64, 128, 1024], P('dp', None, 'sy', 'sx'), may hold values from -6 to 6
- recur_weight: bfloat16 [2304, 1024], replicated, may hold values from -0.125 to 0.125
- hidden_init: bfloat16 [4, 64, 128, 256], P('dp', 'sy', 'sx'), may hold values from -3 to 3
- cell_init: float32 [4, 64, 128, 256], P('dp', 'sy', 'sx'), may hold values from -5 to 5
- hidden_cot: bfloat16 [4, 3, 64, 128, 256], P('dp', None, 'sy', 'sx'), may hold values from -6 to 6
- frame_count: int32 [4], P('dp'), may hold values from 1 to 3, as said below
Outputs:
- hidden_seq: bfloat16 [4, 3, 64, 128, 256], P('dp', None, 'sy', 'sx')
- weight_grad: float32 [2304, 1024], P(None, ('dp', 'sy', 'sx'))
- gate_grad: bfloat16 [4, 3, 64, 128, 1024], P('dp', None, 'sy', 'sx')
- hidden_grad: bfloat16 [4, 64, 128, 256], P('dp', 'sy', 'sx')
- cell_grad: float32 [4, 64, 128, 256], P('dp', 'sy', 'sx')
Inputs may be any that keep to these rules, and one draw needn't show every extreme that they name: `frame_count`: each sample's count of valid frames; some sample has all 3.
All inputs are finite; a program needn't handle non-finite values.
Results may differ from a plain program's by a relative error of at most 0.015.
Values may be sent and summed in bfloat16 or wider, within the bound.
No kernel may reach another device: no remote copies, remote signals or barrier semaphores. Data moves between devices by JAX's collectives and lax.ppermute only.
A program may use at most 64 MiB of HBM per device.

v0:
```python
import jax
import jax.numpy as jnp
from jax import lax
from jax.sharding import PartitionSpec as P


def with_halo(value, sides, width):
    for axis, dim in sides:
        size, length = (lax.axis_size(axis), value.shape[dim])
        up = [(i, (i + 1) % size) for i in range(size - 1)]
        down = [(j, i) for i, j in up]
        last = lax.slice_in_dim(value, length - width, length, axis=dim)
        leading = lax.slice_in_dim(value, 0, width, axis=dim)
        before = lax.ppermute(last, axis, up)
        after = lax.ppermute(leading, axis, down)
        value = jnp.concatenate([before, value, after], axis=dim)
    return value


def in_blocks(value, dim, size):
    before, after = (value.shape[:dim], value.shape[dim + 1 :])
    return jnp.moveaxis(value.reshape(*before, size, -1, *after), dim, 0)


def summed_on_arrival(value, axis, dim):
    size = lax.axis_size(axis)
    parts = lax.all_to_all(in_blocks(value, dim, size), axis, 0, 0, tiled=True)
    return jnp.sum(parts.astype(jnp.float32), axis=0)


def patch_rows(padded, rows, cols, width):
    slabs = [
        padded[row_off : row_off + rows, col_off : col_off + cols]
        for row_off in range(3)
        for col_off in range(3)
    ]
    return jnp.concatenate(slabs, axis=-1).reshape(rows * cols, 9 * width)


def state_border(hidden):
    return with_halo(hidden, (("sy", 0), ("sx", 1)), 1)


def gate_border(dgates):
    return with_halo(dgates, (("sy", 0), ("sx", 1)), 1)


def back_conv(padded_grad, recur_weight, rows, cols, width):
    total = jnp.zeros((rows * cols, width), jnp.float32)
    for row_off in range(3):
        for col_off in range(3):
            block = row_off * 3 + col_off
            slab = padded_grad[
                2 - row_off : 2 - row_off + rows, 2 - col_off : 2 - col_off + cols
            ].reshape(rows * cols, 4 * width)
            weight_block = recur_weight[block * width : (block + 1) * width]
            total = total + lax.dot_general(
                slab, weight_block, (((1,), (1,)), ((), ())), preferred_element_type=jnp.float32
            )
    return total


def body(input_gates, recur_weight, hidden_init, cell_init, hidden_cot, frame_count):
    rows, cols, width = (hidden_init.shape[1], hidden_init.shape[2], hidden_init.shape[3])
    frames = input_gates.shape[1]
    cells = rows * cols
    count = frame_count[0]
    hidden = hidden_init[0].reshape(cells, width)
    cell = cell_init[0].reshape(cells, width)
    saved = []
    outs = []
    for frame in range(frames):
        padded = state_border(hidden.reshape(rows, cols, width))
        patches = patch_rows(padded, rows, cols, width)
        gates = input_gates[0, frame].reshape(cells, 4 * width).astype(jnp.float32) + jnp.dot(
            patches, recur_weight, preferred_element_type=jnp.float32
        )
        sig_i = jax.nn.sigmoid(gates[:, :width])
        sig_f = jax.nn.sigmoid(gates[:, width : 2 * width])
        tan_g = jnp.tanh(gates[:, 2 * width : 3 * width])
        sig_o = jax.nn.sigmoid(gates[:, 3 * width :])
        cell_new = sig_f * cell + sig_i * tan_g
        tan_c = jnp.tanh(cell_new)
        hidden_new = (sig_o * tan_c).astype(jnp.bfloat16)
        valid = frame < count
        saved.append((patches, cell, sig_i, sig_f, tan_g, sig_o, tan_c, valid))
        cell = jnp.where(valid, cell_new, cell)
        hidden = jnp.where(valid, hidden_new, hidden)
        outs.append(hidden.reshape(rows, cols, width))
    grad_h = jnp.zeros((cells, width), jnp.float32)
    grad_c = jnp.zeros((cells, width), jnp.float32)
    w_acc = jnp.zeros((9 * width, 4 * width), jnp.float32)
    gate_list = [None] * frames
    for frame in range(frames - 1, -1, -1):
        patches, cell_prev, sig_i, sig_f, tan_g, sig_o, tan_c, valid = saved[frame]
        grad_h = grad_h + hidden_cot[0, frame].reshape(cells, width).astype(jnp.float32)
        dc_new = grad_c + grad_h * sig_o * (1.0 - tan_c * tan_c)
        d_i = dc_new * tan_g * sig_i * (1.0 - sig_i)
        d_f = dc_new * cell_prev * sig_f * (1.0 - sig_f)
        d_g = dc_new * sig_i * (1.0 - tan_g * tan_g)
        d_o = grad_h * tan_c * sig_o * (1.0 - sig_o)
        dgates = jnp.concatenate([d_i, d_f, d_g, d_o], axis=-1)
        dgates = jnp.where(valid, dgates, 0.0).astype(jnp.bfloat16)
        gate_list[frame] = dgates.reshape(rows, cols, 4 * width)
        w_acc = w_acc + lax.dot_general(
            patches, dgates, (((0,), (0,)), ((), ())), preferred_element_type=jnp.float32
        )
        padded_grad = gate_border(dgates.reshape(rows, cols, 4 * width))
        dh_prev = back_conv(padded_grad, recur_weight, rows, cols, width)
        grad_h = jnp.where(valid, dh_prev, grad_h)
        grad_c = jnp.where(valid, dc_new * sig_f, grad_c)
    partial_sum = lax.psum_scatter(
        w_acc.astype(jnp.bfloat16), "dp", scatter_dimension=1, tiled=True
    )
    weight_grad = summed_on_arrival(partial_sum, ("sy", "sx"), 1)
    hidden_seq = jnp.stack(outs)[None]
    gate_grad = jnp.stack(gate_list)[None]
    hidden_grad = grad_h.astype(jnp.bfloat16).reshape(1, rows, cols, width)
    cell_grad = grad_c.reshape(1, rows, cols, width)
    return (hidden_seq, weight_grad, gate_grad, hidden_grad, cell_grad)


def solution(mesh):
    return jax.shard_map(
        body,
        mesh=mesh,
        in_specs=(
            P("dp", None, "sy", "sx", None),
            P(),
            P("dp", "sy", "sx", None),
            P("dp", "sy", "sx", None),
            P("dp", None, "sy", "sx", None),
            P("dp"),
        ),
        out_specs=(
            P("dp", None, "sy", "sx", None),
            P(None, ("dp", "sy", "sx")),
            P("dp", None, "sy", "sx", None),
            P("dp", "sy", "sx", None),
            P("dp", "sy", "sx", None),
        ),
        check_vma=False,
    )
```

profile of v0, /device:TPU:0, one launch (start us, length us, event | category | flops | bytes accessed | tf_op | source)
XLA Modules:
  0.0 199.6 jit_solution(16109723944541984670)
XLA Ops:
  10.6 1.5 fusion.89
  12.7 1.5 collective-permute-done.1
  15.5 4.5 %collective-permute-start.2 = (bf16[10,1,256]{2,1,0:T(2,128)(2,1)S(1)}, bf16[10,1,256]{2,1,0:T(2,128)(2,1)S(1)}, u32[]{:S(2)}, u32[]{:S(2)}) collective-permute-start(bf16[10,1,256]{2,1,0:T(2,128)(2,1)S(1)} %get-tuple-element.108), channel_id=1, source_target_pairs={{0,1},{1,2},{2,3},{4,5},{5,6},{6,7},{8,9},{9,10},{10,11},{12,13},{... | collective-permute-start | bytes 15368 | tf_op jit(solution)/shard_map/ppermute | solution.py:14
  22.4 1.4 convolution_add_fusion.2
  24.2 4.3 %collective-permute-start.4 = (bf16[1,32,256]{2,1,0:T(8,128)(2,1)S(1)}, bf16[1,32,256]{2,1,0:T(8,128)(2,1)S(1)}, u32[]{:S(2)}, u32[]{:S(2)}) collective-permute-start(bf16[1,32,256]{2,1,0:T(8,128)(2,1)S(1)} %get-tuple-element.115), channel_id=1, source_target_pairs={{0,4},{4,8},{8,12},{12,16},{16,20},{20,24},{24,28},{1,5},{5,9},{9,... | collective-permute-start | bytes 49160 | tf_op jit(solution)/shard_map/ppermute | solution.py:14
  29.8 2.2 %collective-permute-done.5 = bf16[1,32,256]{2,1,0:T(8,128)(2,1)S(1)} collective-permute-done((bf16[1,32,256]{2,1,0:T(8,128)(2,1)S(1)}, bf16[1,32,256]{2,1,0:T(8,128)(2,1)S(1)}, u32[]{:S(2)}, u32[]{:S(2)}) %collective-permute-start.5) | collective-permute-done | bytes 16416 | tf_op jit(solution)/shard_map/ppermute | solution.py:15
  33.3 4.5 %collective-permute-start.6 = (bf16[10,1,256]{2,1,0:T(2,128)(2,1)S(1)}, bf16[10,1,256]{2,1,0:T(2,128)(2,1)S(1)}, u32[]{:S(2)}, u32[]{:S(2)}) collective-permute-start(bf16[10,1,256]{2,1,0:T(2,128)(2,1)S(1)} %get-tuple-element.104), channel_id=1, source_target_pairs={{0,1},{1,2},{2,3},{4,5},{5,6},{6,7},{8,9},{9,10},{10,11},{12,13},{... | collective-permute-start | bytes 15368 | tf_op jit(solution)/shard_map/ppermute | solution.py:14
  39.5 1.4 convolution_add_fusion.1
  41.3 3.2 %collective-permute-start.8 = (bf16[1,32,256]{2,1,0:T(8,128)(2,1)S(1)}, bf16[1,32,256]{2,1,0:T(8,128)(2,1)S(1)}, u32[]{:S(2)}, u32[]{:S(2)}) collective-permute-start(bf16[1,32,256]{2,1,0:T(8,128)(2,1)S(1)} %get-tuple-element.111), channel_id=1, source_target_pairs={{0,4},{4,8},{8,12},{12,16},{16,20},{20,24},{24,28},{1,5},{5,9},{9,... | collective-permute-start | bytes 49160 | tf_op jit(solution)/shard_map/ppermute | solution.py:14
  45.9 2.4 %collective-permute-done.9 = bf16[1,32,256]{2,1,0:T(8,128)(2,1)S(1)} collective-permute-done((bf16[1,32,256]{2,1,0:T(8,128)(2,1)S(1)}, bf16[1,32,256]{2,1,0:T(8,128)(2,1)S(1)}, u32[]{:S(2)}, u32[]{:S(2)}) %collective-permute-start.9) | collective-permute-done | bytes 16416 | tf_op jit(solution)/shard_map/ppermute | solution.py:15
  49.6 4.8 %collective-permute-start.10 = (bf16[10,1,256]{2,1,0:T(2,128)(2,1)S(1)}, bf16[10,1,256]{2,1,0:T(2,128)(2,1)S(1)}, u32[]{:S(2)}, u32[]{:S(2)}) collective-permute-start(bf16[10,1,256]{2,1,0:T(2,128)(2,1)S(1)} %get-tuple-element.100), channel_id=1, source_target_pairs={{0,1},{1,2},{2,3},{4,5},{5,6},{6,7},{8,9},{9,10},{10,11},{12,13},{... | collective-permute-start | bytes 15368 | tf_op jit(solution)/shard_map/ppermute | solution.py:14
  56.2 1.4 convolution_add_fusion
  59.0 1.4 fusion.103
  60.4 3.5 %collective-permute-start.12 = (bf16[1,32,1024]{2,1,0:T(8,128)(2,1)S(1)}, bf16[1,32,1024]{2,1,0:T(8,128)(2,1)S(1)}, u32[]{:S(2)}, u32[]{:S(2)}) collective-permute-start(bf16[1,32,1024]{2,1,0:T(8,128)(2,1)S(1)} %get-tuple-element.74), channel_id=1, source_target_pairs={{0,4},{4,8},{8,12},{12,16},{16,20},{20,24},{24,28},{1,5},{5,9},{9,... | collective-permute-start | bytes 196616 | tf_op jit(solution)/shard_map/ppermute | solution.py:14
  65.4 2.1 %collective-permute-done.13 = bf16[1,32,1024]{2,1,0:T(8,128)(2,1)S(1)} collective-permute-done((bf16[1,32,1024]{2,1,0:T(8,128)(2,1)S(1)}, bf16[1,32,1024]{2,1,0:T(8,128)(2,1)S(1)}, u32[]{:S(2)}, u32[]{:S(2)}) %collective-permute-start.13) | collective-permute-done | bytes 65568 | tf_op jit(solution)/shard_map/ppermute | solution.py:15
  68.8 5.0 %collective-permute-start.15 = (bf16[10,1,1024]{2,1,0:T(2,128)(2,1)S(1)}, bf16[10,1,1024]{2,1,0:T(2,128)(2,1)S(1)}, u32[]{:S(2)}, u32[]{:S(2)}) collective-permute-start(bf16[10,1,1024]{2,1,0:T(2,128)(2,1)S(1)} %get-tuple-element.63), channel_id=1, source_target_pairs={{0,1},{1,2},{2,3},{4,5},{5,6},{6,7},{8,9},{9,10},{10,11},{12,13},{... | collective-permute-start | bytes 61448 | tf_op jit(solution)/shard_map/ppermute | solution.py:14
  79.5 1.4 fusion.104
  81.0 4.0 %collective-permute-start.16 = (bf16[1,32,1024]{2,1,0:T(8,128)(2,1)S(1)}, bf16[1,32,1024]{2,1,0:T(8,128)(2,1)S(1)}, u32[]{:S(2)}, u32[]{:S(2)}) collective-permute-start(bf16[1,32,1024]{2,1,0:T(8,128)(2,1)S(1)} %get-tuple-element.70), channel_id=1, source_target_pairs={{0,4},{4,8},{8,12},{12,16},{16,20},{20,24},{24,28},{1,5},{5,9},{9,... | collective-permute-start | bytes 196616 | tf_op jit(solution)/shard_map/ppermute | solution.py:14
  86.4 2.0 %collective-permute-done.17 = bf16[1,32,1024]{2,1,0:T(8,128)(2,1)S(1)} collective-permute-done((bf16[1,32,1024]{2,1,0:T(8,128)(2,1)S(1)}, bf16[1,32,1024]{2,1,0:T(8,128)(2,1)S(1)}, u32[]{:S(2)}, u32[]{:S(2)}) %collective-permute-start.17) | collective-permute-done | bytes 65568 | tf_op jit(solution)/shard_map/ppermute | solution.py:15
  89.8 4.9 %collective-permute-start.19 = (bf16[10,1,1024]{2,1,0:T(2,128)(2,1)S(1)}, bf16[10,1,1024]{2,1,0:T(2,128)(2,1)S(1)}, u32[]{:S(2)}, u32[]{:S(2)}) collective-permute-start(bf16[10,1,1024]{2,1,0:T(2,128)(2,1)S(1)} %get-tuple-element.59), channel_id=1, source_target_pairs={{0,1},{1,2},{2,3},{4,5},{5,6},{6,7},{8,9},{9,10},{10,11},{12,13},{... | collective-permute-start | bytes 61448 | tf_op jit(solution)/shard_map/ppermute | solution.py:14
  101.6 5.0 %add_convert_fusion = bf16[2304,1024]{1,0:T(8,128)(2,1)} fusion(f32[2304,1024]{1,0:T(8,128)S(1)} %fusion.103, f32[2304,1024]{1,0:T(8,128)S(1)} %fusion.104, bf16[256,2304]{1,0:T(8,128)(2,1)} %copy-done.8, bf16[256,1024]{1,0:T(8,128)(2,1)S(1)} %fusion.13), kind=kOutput, calls=%fused_computation | convolution fusion | flops 1215037440 | bytes 25296896 | tf_op jit(solution)/shard_map/dot_general | solution.py:105
  108.5 4.0 %collective-permute-start.20 = (bf16[1,32,1024]{2,1,0:T(8,128)(2,1)S(1)}, bf16[1,32,1024]{2,1,0:T(8,128)(2,1)S(1)}, u32[]{:S(2)}, u32[]{:S(2)}) collective-permute-start(bf16[1,32,1024]{2,1,0:T(8,128)(2,1)S(1)} %get-tuple-element.66), channel_id=1, source_target_pairs={{0,4},{4,8},{8,12},{12,16},{16,20},{20,24},{24,28},{1,5},{5,9},{9,... | collective-permute-start | bytes 196616 | tf_op jit(solution)/shard_map/ppermute | solution.py:14
  117.4 5.1 %collective-permute-start.23 = (bf16[10,1,1024]{2,1,0:T(2,128)(2,1)S(1)}, bf16[10,1,1024]{2,1,0:T(2,128)(2,1)S(1)}, u32[]{:S(2)}, u32[]{:S(2)}) collective-permute-start(bf16[10,1,1024]{2,1,0:T(2,128)(2,1)S(1)} %get-tuple-element.55), channel_id=1, source_target_pairs={{0,1},{1,2},{2,3},{4,5},{5,6},{6,7},{8,9},{9,10},{10,11},{12,13},{... | collective-permute-start | bytes 61448 | tf_op jit(solution)/shard_map/ppermute | solution.py:14
  122.5 1.4 fusion.42
  128.5 1.4 convolution_add_fusion.7
  129.9 34.2 %reduce-scatter.2.cloned.1.call-done = bf16[2304,256]{1,0:T(8,128)(2,1)} async-done(((bf16[2304,1024]{1,0:T(8,128)(2,1)}), bf16[2304,256]{1,0:T(8,128)(2,1)}) %reduce-scatter.2.cloned.1.call-update) | async-done | bytes 1179664 | tf_op jit(solution)/shard_map/reduce_scatter | solution.py:112
  164.0 2.4 %copy.11 = bf16[2304,256]{0,1:T(8,128)(2,1)} copy(bf16[2304,256]{1,0:T(8,128)(2,1)} %reduce-scatter.2.cloned.1.call-done) | data formatting | bytes 2359296 | tf_op jit(solution)/shard_map/reduce_scatter | solution.py:112
  166.4 7.1 %all-to-all-start = ((bf16[32,2304,8]{1,2,0:T(8,128)(2,1)}), bf16[32,2304,8]{1,2,0:T(8,128)(2,1)S(1)}, u32[]{:S(2)}, u32[]{:S(2)}) async-start(bf16[32,2304,8]{1,2,0:T(8,128)(2,1)} %bitcast.78), calls=%async_computation.1 | async-start | bytes 2359296 | tf_op jit(solution)/shard_map/all_to_all | solution.py:27
  173.5 1.6 fusion.18
  176.6 1.4 convolution_add_fusion.5
  179.4 2.0 %fusion.8 = bf16[256,256]{1,0:T(8,128)(2,1)} fusion(f32[256,256]{1,0:T(8,128)S(1)} %copy-done.10, f32[256,256]{1,0:T(8,128)S(1)} %fusion.18, f32[256,256]{1,0:T(8,128)S(1)} %convolution_add_fusion.4, bf16[256,1024]{1,0:T(8,128)(2,1)S(1)} %bitcast.194, bf16[2304,1024]{1,0:T(8,128)(2,1)} %param.7, pred[]{:T(512)} %bitcast), kind=kOutput, calls=%fused_computation.35 | convolution fusion | flops 134414336 | bytes 1966592 | tf_op jit(solution)/shard_map/dot_general | solution.py:57
  181.4 10.6 %all-to-all-done = bf16[32,2304,8]{1,2,0:T(8,128)(2,1)S(1)} async-done(((bf16[32,2304,8]{1,2,0:T(8,128)(2,1)}), bf16[32,2304,8]{1,2,0:T(8,128)(2,1)S(1)}, u32[]{:S(2)}, u32[]{:S(2)}) %all-to-all-start) | async-done | bytes 1179680 | tf_op jit(solution)/shard_map/all_to_all | solution.py:27
  (163 shorter events, 50.1 us)
Async XLA Ops:
  7.2 7.0 %copy-start.1 = (bf16[1,8,32,256]{3,2,1,0:T(8,128)(2,1)S(1)}, bf16[1,8,32,256]{3,2,1,0:T(8,128)(2,1)}, u32[]{:S(2)}) copy-start(bf16[1,8,32,256]{3,2,1,0:T(8,128)(2,1)} %param.8) | copy-start | bytes 393220
  7.2 156.9 %reduce-scatter.2.cloned.1.call-start = ((), (), s32[]{:S(2)}) async-start(), calls=%async_computation.2 | async-start | bytes 5898240 | tf_op jit(solution)/shard_map/reduce_scatter | solution.py:112
  8.0 4.7 %collective-permute-start = (bf16[1,32,256]{2,1,0:T(8,128)(2,1)S(1)}, bf16[1,32,256]{2,1,0:T(8,128)(2,1)S(1)}, u32[]{:S(2)}, u32[]{:S(2)}) collective-permute-start(bf16[1,32,256]{2,1,0:T(8,128)(2,1)S(1)} %get-tuple-element.119), channel_id=1, source_target_pairs={{0,4},{4,8},{8,12},{12,16},{16,20},{20,24},{24,28},{1,5},{5,9},{9,... | collective-permute-start | bytes 49160 | tf_op jit(solution)/shard_map/ppermute | solution.py:14
  9.3 4.9 %collective-permute-start.1 = (bf16[1,32,256]{2,1,0:T(8,128)(2,1)S(1)}, bf16[1,32,256]{2,1,0:T(8,128)(2,1)S(1)}, u32[]{:S(2)}, u32[]{:S(2)}) collective-permute-start(bf16[1,32,256]{2,1,0:T(8,128)(2,1)S(1)} %get-tuple-element.120), channel_id=1, source_target_pairs={{4,0},{8,4},{12,8},{16,12},{20,16},{24,20},{28,24},{5,1},{9,5},{13... | collective-permute-start | bytes 49160 | tf_op jit(solution)/shard_map/ppermute | solution.py:15
  14.2 5.9 %collective-permute-start.3 = (bf16[10,1,256]{2,1,0:T(2,128)(2,1)S(1)}, bf16[10,1,256]{2,1,0:T(2,128)(2,1)S(1)}, u32[]{:S(2)}, u32[]{:S(2)}) collective-permute-start(bf16[10,1,256]{2,1,0:T(2,128)(2,1)S(1)} %get-tuple-element.107), channel_id=1, source_target_pairs={{1,0},{2,1},{3,2},{5,4},{6,5},{7,6},{9,8},{10,9},{11,10},{13,12},{... | collective-permute-start | bytes 15368 | tf_op jit(solution)/shard_map/ppermute | solution.py:15
  15.5 5.9 %collective-permute-start.2 = (bf16[10,1,256]{2,1,0:T(2,128)(2,1)S(1)}, bf16[10,1,256]{2,1,0:T(2,128)(2,1)S(1)}, u32[]{:S(2)}, u32[]{:S(2)}) collective-permute-start(bf16[10,1,256]{2,1,0:T(2,128)(2,1)S(1)} %get-tuple-element.108), channel_id=1, source_target_pairs={{0,1},{1,2},{2,3},{4,5},{5,6},{6,7},{8,9},{9,10},{10,11},{12,13},{... | collective-permute-start | bytes 15368 | tf_op jit(solution)/shard_map/ppermute | solution.py:14
  24.2 5.6 %collective-permute-start.4 = (bf16[1,32,256]{2,1,0:T(8,128)(2,1)S(1)}, bf16[1,32,256]{2,1,0:T(8,128)(2,1)S(1)}, u32[]{:S(2)}, u32[]{:S(2)}) collective-permute-start(bf16[1,32,256]{2,1,0:T(8,128)(2,1)S(1)} %get-tuple-element.115), channel_id=1, source_target_pairs={{0,4},{4,8},{8,12},{12,16},{16,20},{20,24},{24,28},{1,5},{5,9},{9,... | collective-permute-start | bytes 49160 | tf_op jit(solution)/shard_map/ppermute | solution.py:14
  28.4 3.5 %collective-permute-start.5 = (bf16[1,32,256]{2,1,0:T(8,128)(2,1)S(1)}, bf16[1,32,256]{2,1,0:T(8,128)(2,1)S(1)}, u32[]{:S(2)}, u32[]{:S(2)}) collective-permute-start(bf16[1,32,256]{2,1,0:T(8,128)(2,1)S(1)} %get-tuple-element.116), channel_id=1, source_target_pairs={{4,0},{8,4},{12,8},{16,12},{20,16},{24,20},{28,24},{5,1},{9,5},{13... | collective-permute-start | bytes 49160 | tf_op jit(solution)/shard_map/ppermute | solution.py:15
  32.0 5.9 %collective-permute-start.7 = (bf16[10,1,256]{2,1,0:T(2,128)(2,1)S(1)}, bf16[10,1,256]{2,1,0:T(2,128)(2,1)S(1)}, u32[]{:S(2)}, u32[]{:S(2)}) collective-permute-start(bf16[10,1,256]{2,1,0:T(2,128)(2,1)S(1)} %get-tuple-element.103), channel_id=1, source_target_pairs={{1,0},{2,1},{3,2},{5,4},{6,5},{7,6},{9,8},{10,9},{11,10},{13,12},{... | collective-permute-start | bytes 15368 | tf_op jit(solution)/shard_map/ppermute | solution.py:15
  33.3 5.9 %collective-permute-start.6 = (bf16[10,1,256]{2,1,0:T(2,128)(2,1)S(1)}, bf16[10,1,256]{2,1,0:T(2,128)(2,1)S(1)}, u32[]{:S(2)}, u32[]{:S(2)}) collective-permute-start(bf16[10,1,256]{2,1,0:T(2,128)(2,1)S(1)} %get-tuple-element.104), channel_id=1, source_target_pairs={{0,1},{1,2},{2,3},{4,5},{5,6},{6,7},{8,9},{9,10},{10,11},{12,13},{... | collective-permute-start | bytes 15368 | tf_op jit(solution)/shard_map/ppermute | solution.py:14
  41.0 4.9 %copy-start.12 = (bf16[1,3,8,32,256]{4,3,2,1,0:T(8,128)(2,1)S(1)}, bf16[1,3,8,32,256]{4,3,2,1,0:T(8,128)(2,1)}, u32[]{:S(2)}) copy-start(bf16[1,3,8,32,256]{4,3,2,1,0:T(8,128)(2,1)} %param.10) | copy-start | bytes 1179652
  41.3 4.6 %collective-permute-start.8 = (bf16[1,32,256]{2,1,0:T(8,128)(2,1)S(1)}, bf16[1,32,256]{2,1,0:T(8,128)(2,1)S(1)}, u32[]{:S(2)}, u32[]{:S(2)}) collective-permute-start(bf16[1,32,256]{2,1,0:T(8,128)(2,1)S(1)} %get-tuple-element.111), channel_id=1, source_target_pairs={{0,4},{4,8},{8,12},{12,16},{16,20},{20,24},{24,28},{1,5},{5,9},{9,... | collective-permute-start | bytes 49160 | tf_op jit(solution)/shard_map/ppermute | solution.py:14
  44.5 3.7 %collective-permute-start.9 = (bf16[1,32,256]{2,1,0:T(8,128)(2,1)S(1)}, bf16[1,32,256]{2,1,0:T(8,128)(2,1)S(1)}, u32[]{:S(2)}, u32[]{:S(2)}) collective-permute-start(bf16[1,32,256]{2,1,0:T(8,128)(2,1)S(1)} %get-tuple-element.112), channel_id=1, source_target_pairs={{4,0},{8,4},{12,8},{16,12},{20,16},{24,20},{28,24},{5,1},{9,5},{13... | collective-permute-start | bytes 49160 | tf_op jit(solution)/shard_map/ppermute | solution.py:15
  48.3 6.2 %collective-permute-start.11 = (bf16[10,1,256]{2,1,0:T(2,128)(2,1)S(1)}, bf16[10,1,256]{2,1,0:T(2,128)(2,1)S(1)}, u32[]{:S(2)}, u32[]{:S(2)}) collective-permute-start(bf16[10,1,256]{2,1,0:T(2,128)(2,1)S(1)} %get-tuple-element.99), channel_id=1, source_target_pairs={{1,0},{2,1},{3,2},{5,4},{6,5},{7,6},{9,8},{10,9},{11,10},{13,12},{... | collective-permute-start | bytes 15368 | tf_op jit(solution)/shard_map/ppermute | solution.py:15
  49.6 6.2 %collective-permute-start.10 = (bf16[10,1,256]{2,1,0:T(2,128)(2,1)S(1)}, bf16[10,1,256]{2,1,0:T(2,128)(2,1)S(1)}, u32[]{:S(2)}, u32[]{:S(2)}) collective-permute-start(bf16[10,1,256]{2,1,0:T(2,128)(2,1)S(1)} %get-tuple-element.100), channel_id=1, source_target_pairs={{0,1},{1,2},{2,3},{4,5},{5,6},{6,7},{8,9},{9,10},{10,11},{12,13},{... | collective-permute-start | bytes 15368 | tf_op jit(solution)/shard_map/ppermute | solution.py:14
  58.8 6.4 %copy-start.4 = (bf16[256,256]{1,0:T(8,128)(2,1)}, bf16[256,256]{1,0:T(8,128)(2,1)S(1)}, u32[]{:S(2)}) copy-start(bf16[256,256]{1,0:T(8,128)(2,1)S(1)} %get-tuple-element.27) | copy-start | bytes 393220
  58.8 6.4 %copy-start.6 = (bf16[256,256]{1,0:T(8,128)(2,1)}, bf16[256,256]{1,0:T(8,128)(2,1)S(1)}, u32[]{:S(2)}) copy-start(bf16[256,256]{1,0:T(8,128)(2,1)S(1)} %get-tuple-element.33) | copy-start | bytes 393220
  60.4 5.0 %collective-permute-start.12 = (bf16[1,32,1024]{2,1,0:T(8,128)(2,1)S(1)}, bf16[1,32,1024]{2,1,0:T(8,128)(2,1)S(1)}, u32[]{:S(2)}, u32[]{:S(2)}) collective-permute-start(bf16[1,32,1024]{2,1,0:T(8,128)(2,1)S(1)} %get-tuple-element.74), channel_id=1, source_target_pairs={{0,4},{4,8},{8,12},{12,16},{16,20},{20,24},{24,28},{1,5},{5,9},{9,... | collective-permute-start | bytes 196616 | tf_op jit(solution)/shard_map/ppermute | solution.py:14
  63.9 3.5 %collective-permute-start.13 = (bf16[1,32,1024]{2,1,0:T(8,128)(2,1)S(1)}, bf16[1,32,1024]{2,1,0:T(8,128)(2,1)S(1)}, u32[]{:S(2)}, u32[]{:S(2)}) collective-permute-start(bf16[1,32,1024]{2,1,0:T(8,128)(2,1)S(1)} %get-tuple-element.75), channel_id=1, source_target_pairs={{4,0},{8,4},{12,8},{16,12},{20,16},{24,20},{28,24},{5,1},{9,5},{13... | collective-permute-start | bytes 196616 | tf_op jit(solution)/shard_map/ppermute | solution.py:15
  67.5 6.7 %collective-permute-start.14 = (bf16[10,1,1024]{2,1,0:T(2,128)(2,1)S(1)}, bf16[10,1,1024]{2,1,0:T(2,128)(2,1)S(1)}, u32[]{:S(2)}, u32[]{:S(2)}) collective-permute-start(bf16[10,1,1024]{2,1,0:T(2,128)(2,1)S(1)} %get-tuple-element.62), channel_id=1, source_target_pairs={{1,0},{2,1},{3,2},{5,4},{6,5},{7,6},{9,8},{10,9},{11,10},{13,12},{... | collective-permute-start | bytes 61448 | tf_op jit(solution)/shard_map/ppermute | solution.py:15
  68.8 6.5 %collective-permute-start.15 = (bf16[10,1,1024]{2,1,0:T(2,128)(2,1)S(1)}, bf16[10,1,1024]{2,1,0:T(2,128)(2,1)S(1)}, u32[]{:S(2)}, u32[]{:S(2)}) collective-permute-start(bf16[10,1,1024]{2,1,0:T(2,128)(2,1)S(1)} %get-tuple-element.63), channel_id=1, source_target_pairs={{0,1},{1,2},{2,3},{4,5},{5,6},{6,7},{8,9},{9,10},{10,11},{12,13},{... | collective-permute-start | bytes 61448 | tf_op jit(solution)/shard_map/ppermute | solution.py:14
  81.0 5.4 %collective-permute-start.16 = (bf16[1,32,1024]{2,1,0:T(8,128)(2,1)S(1)}, bf16[1,32,1024]{2,1,0:T(8,128)(2,1)S(1)}, u32[]{:S(2)}, u32[]{:S(2)}) collective-permute-start(bf16[1,32,1024]{2,1,0:T(8,128)(2,1)S(1)} %get-tuple-element.70), channel_id=1, source_target_pairs={{0,4},{4,8},{8,12},{12,16},{16,20},{20,24},{24,28},{1,5},{5,9},{9,... | collective-permute-start | bytes 196616 | tf_op jit(solution)/shard_map/ppermute | solution.py:14
  85.0 3.5 %collective-permute-start.17 = (bf16[1,32,1024]{2,1,0:T(8,128)(2,1)S(1)}, bf16[1,32,1024]{2,1,0:T(8,128)(2,1)S(1)}, u32[]{:S(2)}, u32[]{:S(2)}) collective-permute-start(bf16[1,32,1024]{2,1,0:T(8,128)(2,1)S(1)} %get-tuple-element.71), channel_id=1, source_target_pairs={{4,0},{8,4},{12,8},{16,12},{20,16},{24,20},{28,24},{5,1},{9,5},{13... | collective-permute-start | bytes 196616 | tf_op jit(solution)/shard_map/ppermute | solution.py:15
  88.5 6.6 %collective-permute-start.18 = (bf16[10,1,1024]{2,1,0:T(2,128)(2,1)S(1)}, bf16[10,1,1024]{2,1,0:T(2,128)(2,1)S(1)}, u32[]{:S(2)}, u32[]{:S(2)}) collective-permute-start(bf16[10,1,1024]{2,1,0:T(2,128)(2,1)S(1)} %get-tuple-element.58), channel_id=1, source_target_pairs={{1,0},{2,1},{3,2},{5,4},{6,5},{7,6},{9,8},{10,9},{11,10},{13,12},{... | collective-permute-start | bytes 61448 | tf_op jit(solution)/shard_map/ppermute | solution.py:15
  89.8 6.5 %collective-permute-start.19 = (bf16[10,1,1024]{2,1,0:T(2,128)(2,1)S(1)}, bf16[10,1,1024]{2,1,0:T(2,128)(2,1)S(1)}, u32[]{:S(2)}, u32[]{:S(2)}) collective-permute-start(bf16[10,1,1024]{2,1,0:T(2,128)(2,1)S(1)} %get-tuple-element.59), channel_id=1, source_target_pairs={{0,1},{1,2},{2,3},{4,5},{5,6},{6,7},{8,9},{9,10},{10,11},{12,13},{... | collective-permute-start | bytes 61448 | tf_op jit(solution)/shard_map/ppermute | solution.py:14
  108.5 6.8 %collective-permute-start.20 = (bf16[1,32,1024]{2,1,0:T(8,128)(2,1)S(1)}, bf16[1,32,1024]{2,1,0:T(8,128)(2,1)S(1)}, u32[]{:S(2)}, u32[]{:S(2)}) collective-permute-start(bf16[1,32,1024]{2,1,0:T(8,128)(2,1)S(1)} %get-tuple-element.66), channel_id=1, source_target_pairs={{0,4},{4,8},{8,12},{12,16},{16,20},{20,24},{24,28},{1,5},{5,9},{9,... | collective-permute-start | bytes 196616 | tf_op jit(solution)/shard_map/ppermute | solution.py:14
  112.5 3.5 %collective-permute-start.21 = (bf16[1,32,1024]{2,1,0:T(8,128)(2,1)S(1)}, bf16[1,32,1024]{2,1,0:T(8,128)(2,1)S(1)}, u32[]{:S(2)}, u32[]{:S(2)}) collective-permute-start(bf16[1,32,1024]{2,1,0:T(8,128)(2,1)S(1)} %get-tuple-element.67), channel_id=1, source_target_pairs={{4,0},{8,4},{12,8},{16,12},{20,16},{24,20},{28,24},{5,1},{9,5},{13... | collective-permute-start | bytes 196616 | tf_op jit(solution)/shard_map/ppermute | solution.py:15
  116.1 7.9 %collective-permute-start.22 = (bf16[10,1,1024]{2,1,0:T(2,128)(2,1)S(1)}, bf16[10,1,1024]{2,1,0:T(2,128)(2,1)S(1)}, u32[]{:S(2)}, u32[]{:S(2)}) collective-permute-start(bf16[10,1,1024]{2,1,0:T(2,128)(2,1)S(1)} %get-tuple-element.54), channel_id=1, source_target_pairs={{1,0},{2,1},{3,2},{5,4},{6,5},{7,6},{9,8},{10,9},{11,10},{13,12},{... | collective-permute-start | bytes 61448 | tf_op jit(solution)/shard_map/ppermute | solution.py:15
  117.4 6.6 %collective-permute-start.23 = (bf16[10,1,1024]{2,1,0:T(2,128)(2,1)S(1)}, bf16[10,1,1024]{2,1,0:T(2,128)(2,1)S(1)}, u32[]{:S(2)}, u32[]{:S(2)}) collective-permute-start(bf16[10,1,1024]{2,1,0:T(2,128)(2,1)S(1)} %get-tuple-element.55), channel_id=1, source_target_pairs={{0,1},{1,2},{2,3},{4,5},{5,6},{6,7},{8,9},{9,10},{10,11},{12,13},{... | collective-permute-start | bytes 61448 | tf_op jit(solution)/shard_map/ppermute | solution.py:14
  166.4 25.6 %all-to-all-start = ((bf16[32,2304,8]{1,2,0:T(8,128)(2,1)}), bf16[32,2304,8]{1,2,0:T(8,128)(2,1)S(1)}, u32[]{:S(2)}, u32[]{:S(2)}) async-start(bf16[32,2304,8]{1,2,0:T(8,128)(2,1)} %bitcast.78), calls=%async_computation.1 | async-start | bytes 2359296 | tf_op jit(solution)/shard_map/all_to_all | solution.py:27
  173.5 3.0 %copy-start.3 = (bf16[8,32,1024]{2,1,0:T(8,128)(2,1)S(1)}, bf16[8,32,1024]{2,1,0:T(8,128)(2,1)}, u32[]{:S(2)}) copy-start(bf16[8,32,1024]{2,1,0:T(8,128)(2,1)} %get-tuple-element.37) | copy-start | bytes 1572868
  176.5 2.8 %copy-start.10 = (f32[256,256]{1,0:T(8,128)S(1)}, f32[256,256]{1,0:T(8,128)}, u32[]{:S(2)}) copy-start(f32[256,256]{1,0:T(8,128)} %copy-done.9) | copy-start | bytes 786436
  (7 other events, 10.9 us)
Sparse Core Ops, SparseCore 0:
  106.7 57.2 reduce-scatter.1
where the time goes:
time: 201 us; the launch traced here: 200 us
  starting transfers between devices  71.8 us (36%)
  waiting for transfers between devices  61.8 us (31%)
  matrix products  32.5 us (16%)
  between operations  15.9 us (8%)
  local copies, waits for them, and re-layouts  9.43 us (5%)
  other arithmetic  8.23 us (4%)
    ppermute x12, starting transfers between devices, with_halo(): before = lax.ppermute(last, axis, up)  49.2 us
    reduce_scatter x1, waiting for transfers between devices, body(): lax.psum_scatter(w_acc.astype(jnp.bfloat16), 'dp', scatter_dimension=1, t...  34.2 us
    dot_general x27, matrix products, back_conv(): lax.dot_general(slab, weight_block, (((1,), (1,)), ((), ())), preferred_e...  20.5 us
    ppermute x12, starting transfers between devices, with_halo(): after = lax.ppermute(leading, axis, down)  15.5 us
    ppermute x12, waiting for transfers between devices, with_halo(): after = lax.ppermute(leading, axis, down)  10.8 us
    all_to_all x1, waiting for transfers between devices, summed_on_arrival(): parts = lax.all_to_all(in_blocks(value, dim, size), axis, 0, 0, tiled=True)  10.6 us
    dot_general x3, matrix products, body(): lax.dot_general(patches, dgates, (((0,), (0,)), ((), ())), preferred_elem...  7.84 us
    all_to_all x1, starting transfers between devices, summed_on_arrival(): parts = lax.all_to_all(in_blocks(value, dim, size), axis, 0, 0, tiled=True)  7.11 us
  transfers between devices with their start and end apart: 26, of which 13 were waited for; matrix products, arithmetic and copies ran while one was open for 10% of the time, Pallas kernels for 0%

commit v1 on v0

--- a/solution.py
+++ b/solution.py
@@ -1,31 +1,25 @@
 import jax
 import jax.numpy as jnp
 from jax import lax
-from jax.sharding import PartitionSpec as P
+from jax.sharding import Mesh, PartitionSpec as P
 
 
-def with_halo(value, sides, width):
-    for axis, dim in sides:
-        size, length = (lax.axis_size(axis), value.shape[dim])
-        up = [(i, (i + 1) % size) for i in range(size - 1)]
-        down = [(j, i) for i, j in up]
-        last = lax.slice_in_dim(value, length - width, length, axis=dim)
-        leading = lax.slice_in_dim(value, 0, width, axis=dim)
-        before = lax.ppermute(last, axis, up)
-        after = lax.ppermute(leading, axis, down)
-        value = jnp.concatenate([before, value, after], axis=dim)
-    return value
+def ring_pairs(size, phase):
+    pairs = [(i, (i + 1) % size) for i in range(phase, size, 2)]
+    return [edge for a, b in pairs for edge in ((a, b), (b, a))]
 
 
-def in_blocks(value, dim, size):
-    before, after = (value.shape[:dim], value.shape[dim + 1 :])
-    return jnp.moveaxis(value.reshape(*before, size, -1, *after), dim, 0)
-
-
-def summed_on_arrival(value, axis, dim):
-    size = lax.axis_size(axis)
-    parts = lax.all_to_all(in_blocks(value, dim, size), axis, 0, 0, tiled=True)
-    return jnp.sum(parts.astype(jnp.float32), axis=0)
+def with_halo(value, axis, size, dim):
+    me = lax.axis_index(axis)
+    odd = me % 2 == 1
+    length = value.shape[dim]
+    first = lax.slice_in_dim(value, 0, 1, axis=dim)
+    last = lax.slice_in_dim(value, length - 1, length, axis=dim)
+    near = lax.ppermute(jnp.where(odd, first, last), axis, ring_pairs(size, 0))
+    far = lax.ppermute(jnp.where(odd, last, first), axis, ring_pairs(size, 1))
+    before = jnp.where(me == 0, 0, jnp.where(odd, near, far))
+    after = jnp.where(me == size - 1, 0, jnp.where(odd, far, near))
+    return jnp.concatenate([before, value, after], axis=dim)
 
 
 def patch_rows(padded, rows, cols, width):
@@ -38,11 +32,11 @@
 
 
 def state_border(hidden):
-    return with_halo(hidden, (("sy", 0), ("sx", 1)), 1)
+    return with_halo(with_halo(hidden, ("x", "core"), 8, 0), "sx", 4, 1)
 
 
 def gate_border(dgates):
-    return with_halo(dgates, (("sy", 0), ("sx", 1)), 1)
+    return with_halo(with_halo(dgates, ("x", "core"), 8, 0), "sx", 4, 1)
 
 
 def back_conv(padded_grad, recur_weight, rows, cols, width):
@@ -89,7 +83,7 @@
         outs.append(hidden.reshape(rows, cols, width))
     grad_h = jnp.zeros((cells, width), jnp.float32)
     grad_c = jnp.zeros((cells, width), jnp.float32)
-    w_acc = jnp.zeros((9 * width, 4 * width), jnp.float32)
+    all_patches, all_grads = ([], [])
     gate_list = [None] * frames
     for frame in range(frames - 1, -1, -1):
         patches, cell_prev, sig_i, sig_f, tan_g, sig_o, tan_c, valid = saved[frame]
@@ -102,17 +96,25 @@
         dgates = jnp.concatenate([d_i, d_f, d_g, d_o], axis=-1)
         dgates = jnp.where(valid, dgates, 0.0).astype(jnp.bfloat16)
         gate_list[frame] = dgates.reshape(rows, cols, 4 * width)
-        w_acc = w_acc + lax.dot_general(
-            patches, dgates, (((0,), (0,)), ((), ())), preferred_element_type=jnp.float32
-        )
+        all_patches.append(patches)
+        all_grads.append(dgates)
         padded_grad = gate_border(dgates.reshape(rows, cols, 4 * width))
         dh_prev = back_conv(padded_grad, recur_weight, rows, cols, width)
         grad_h = jnp.where(valid, dh_prev, grad_h)
         grad_c = jnp.where(valid, dc_new * sig_f, grad_c)
-    partial_sum = lax.psum_scatter(
-        w_acc.astype(jnp.bfloat16), "dp", scatter_dimension=1, tiled=True
-    )
-    weight_grad = summed_on_arrival(partial_sum, ("sy", "sx"), 1)
+    weight_t = lax.dot_general(
+        jnp.concatenate(all_grads),
+        jnp.concatenate(all_patches),
+        (((0,), (0,)), ((), ())),
+        preferred_element_type=jnp.float32,
+    ).reshape(16, 2, 32, 9 * width)
+    core = lax.axis_index("core")
+    mine = jnp.where(core == 0, weight_t[:, 0], weight_t[:, 1])
+    theirs = jnp.where(core == 0, weight_t[:, 1], weight_t[:, 0]).astype(jnp.bfloat16)
+    got = lax.ppermute(theirs, "core", [(0, 1), (1, 0)])
+    chip_sum = (mine + got.astype(jnp.float32)).astype(jnp.bfloat16).reshape(512, 9 * width)
+    parts = lax.all_to_all(chip_sum, ("dp", "x", "sx"), 0, 0, tiled=True)
+    weight_grad = jnp.sum(parts.reshape(64, 8, 9 * width).astype(jnp.float32), axis=0).T
     hidden_seq = jnp.stack(outs)[None]
     gate_grad = jnp.stack(gate_list)[None]
     hidden_grad = grad_h.astype(jnp.bfloat16).reshape(1, rows, cols, width)
@@ -121,23 +123,26 @@
 
 
 def solution(mesh):
-    return jax.shard_map(
+    split = Mesh(mesh.devices.reshape(4, 4, 2, 4), ("dp", "x", "core", "sx"))
+    sy = ("x", "core")
+    step = jax.shard_map(
         body,
-        mesh=mesh,
+        mesh=split,
         in_specs=(
-            P("dp", None, "sy", "sx", None),
+            P("dp", None, sy, "sx", None),
             P(),
-            P("dp", "sy", "sx", None),
-            P("dp", "sy", "sx", None),
-            P("dp", None, "sy", "sx", None),
+            P("dp", sy, "sx", None),
+            P("dp", sy, "sx", None),
+            P("dp", None, sy, "sx", None),
             P("dp"),
         ),
         out_specs=(
-            P("dp", None, "sy", "sx", None),
-            P(None, ("dp", "sy", "sx")),
-            P("dp", None, "sy", "sx", None),
-            P("dp", "sy", "sx", None),
-            P("dp", "sy", "sx", None),
+            P("dp", None, sy, "sx", None),
+            P(None, ("dp", "x", "core", "sx")),
+            P("dp", None, sy, "sx", None),
+            P("dp", sy, "sx", None),
+            P("dp", sy, "sx", None),
         ),
         check_vma=False,
     )
+    return step

time: 201 us -> 142 us (0.71)
  starting transfers between devices: 71.8 us -> 27.1 us
  between operations: 15.9 us -> 2.48 us
  other arithmetic: 8.23 us -> 14.4 us
  waiting for transfers between devices: 61.8 us -> 57.1 us
  matrix products: 32.5 us -> 30.1 us
    ppermute x24 -> x25, starting transfers between devices: 64.7 us -> 19.9 us  [the longest x12 16.4 us: with_halo(): far = lax.ppermute(jnp.where(odd, last, first), axis, ring_pairs(size, 1))]
    reduce_scatter x1 -> x0, waiting for transfers between devices: 34.2 us -> none  [body(): lax.psum_scatter(w_acc.astype(jnp.bfloat16), 'dp', scatter_dimension=1, t...]
    ppermute x24 -> x25, waiting for transfers between devices: 17 us -> 38.3 us  [the longest x12 30 us: with_halo(): far = lax.ppermute(jnp.where(odd, last, first), axis, ring_pairs(size, 1))]
    all_to_all x1, waiting for transfers between devices: 10.6 us -> 18.9 us  [body(): parts = lax.all_to_all(chip_sum, ('dp', 'x', 'sx'), 0, 0, tiled=True)]
    dot_general x3 -> x1, matrix products: 7.84 us -> 4 us  [body(): lax.dot_general(jnp.concatenate(all_grads), jnp.concatenate(all_patches),...]
    select_n x0 -> x30, other arithmetic: none -> 3.22 us  [the longest x12 1.75 us: with_halo(): near = lax.ppermute(jnp.where(odd, first, last), axis, ring_pairs(size, 0))]
    convert_element_type x0 -> x2, other arithmetic: none -> 2.79 us  [the longest x1 2.38 us: body(): (mine + got.astype(jnp.float32)).astype(jnp.bfloat16)]
    reduce_scatter x1 -> x0, local copies, waits for them, and re-layouts: 2.37 us -> none  [body(): lax.psum_scatter(w_acc.astype(jnp.bfloat16), 'dp', scatter_dimension=1, t...]
  transfers between devices with their start and end apart: 26 -> 26, of which waited for: 13 -> 21; matrix products, arithmetic and copies ran while one was open for 10% -> 15% of each run, Pallas kernels for 0% -> 0%
where the time goes in v1:
time: 142 us; the launch traced here: 141 us
  waiting for transfers between devices  57.1 us (40%)
  matrix products  30.1 us (21%)
  starting transfers between devices  27.1 us (19%)
  other arithmetic  14.4 us (10%)
  local copies, waits for them, and re-layouts  9.71 us (7%)
  between operations  2.48 us (2%)
    ppermute x12, waiting for transfers between devices, with_halo(): far = lax.ppermute(jnp.where(odd, last, first), axis, ring_pairs(size, 1))  30 us
    dot_general x27, matrix products, back_conv(): lax.dot_general(slab, weight_block, (((1,), (1,)), ((), ())), preferred_e...  19.5 us
    all_to_all x1, waiting for transfers between devices, body(): parts = lax.all_to_all(chip_sum, ('dp', 'x', 'sx'), 0, 0, tiled=True)  18.9 us
    ppermute x12, starting transfers between devices, with_halo(): far = lax.ppermute(jnp.where(odd, last, first), axis, ring_pairs(size, 1))  16.4 us
    ppermute x12, waiting for transfers between devices, with_halo(): near = lax.ppermute(jnp.where(odd, first, last), axis, ring_pairs(size, 0))  8.27 us
    all_to_all x1, starting transfers between devices, body(): parts = lax.all_to_all(chip_sum, ('dp', 'x', 'sx'), 0, 0, tiled=True)  7.2 us
    dot_general x3, matrix products, body(): jnp.dot(patches, recur_weight, preferred_element_type=jnp.float32)  6.54 us
    unnamed x66, local copies, waits for them, and re-layouts  4.02 us
  transfers between devices with their start and end apart: 26, of which 21 were waited for; matrix products, arithmetic and copies ran while one was open for 15% of the time, Pallas kernels for 0%

profile of v1, /device:TPU:0, one launch (start us, length us, event | category | flops | bytes accessed | tf_op | source)
XLA Modules:
  0.0 140.9 jit_solution(10559921382068279763)
XLA Ops:
  1.5 3.0 %collective-permute-start.1 = (bf16[1,32,256]{2,1,0:T(8,128)(2,1)S(1)}, bf16[1,32,256]{2,1,0:T(8,128)(2,1)S(1)}, u32[]{:S(2)}, u32[]{:S(2)}) collective-permute-start(bf16[1,32,256]{2,1,0:T(8,128)(2,1)S(1)} %get-tuple-element.132), channel_id=1, source_target_pairs={{4,8},{8,4},{12,16},{16,12},{20,24},{24,20},{28,0},{0,28},{5,9},{9... | collective-permute-start | bytes 49160 | tf_op jit(solution)/shard_map/ppermute | solution.py:19
  4.5 2.5 %fusion.99 = (bf16[1,1,8,32,1024]{4,3,2,1,0:T(8,128)(2,1)}, bf16[1,1,8,32,1024]{4,3,2,1,0:T(8,128)(2,1)S(1)}, bf16[1,1,8,32,1024]{4,3,2,1,0:T(8,128)(2,1)}) fusion(bf16[1,3,8,32,1024]{4,3,2,1,0:T(8,128)(2,1)} %param.6), kind=kLoop, calls=%fused_computation.305 | loop fusion | bytes 3145728 | tf_op jit(solution)/shard_map/slice | solution.py:69
  7.7 1.7 %collective-permute-start.2 = (bf16[10,1,256]{2,1,0:T(2,128)(2,1)S(1)}, bf16[10,1,256]{2,1,0:T(2,128)(2,1)S(1)}, u32[]{:S(2)}, u32[]{:S(2)}) collective-permute-start(bf16[10,1,256]{2,1,0:T(2,128)(2,1)S(1)} %broadcast_select_fusion.33), channel_id=1, source_target_pairs={{0,1},{1,0},{2,3},{3,2},{4,5},{5,4},{6,7},{7,6},{8,9},{9,8},{10,11... | collective-permute-start | bytes 15368 | tf_op jit(solution)/shard_map/ppermute | solution.py:18
  9.4 2.2 %collective-permute-start.3 = (bf16[10,1,256]{2,1,0:T(2,128)(2,1)S(1)}, bf16[10,1,256]{2,1,0:T(2,128)(2,1)S(1)}, u32[]{:S(2)}, u32[]{:S(2)}) collective-permute-start(bf16[10,1,256]{2,1,0:T(2,128)(2,1)S(1)} %get-tuple-element.32), channel_id=1, source_target_pairs={{1,2},{2,1},{3,0},{0,3},{5,6},{6,5},{7,4},{4,7},{9,10},{10,9},{11,... | collective-permute-start | bytes 15368 | tf_op jit(solution)/shard_map/ppermute | solution.py:19
  11.6 2.7 %collective-permute-done.3 = bf16[10,1,256]{2,1,0:T(2,128)(2,1)S(1)} collective-permute-done((bf16[10,1,256]{2,1,0:T(2,128)(2,1)S(1)}, bf16[10,1,256]{2,1,0:T(2,128)(2,1)S(1)}, u32[]{:S(2)}, u32[]{:S(2)}) %collective-permute-start.3) | collective-permute-done | bytes 5152 | tf_op jit(solution)/shard_map/ppermute | solution.py:19
  14.7 1.4 convolution_add_fusion.2
  17.7 3.3 %collective-permute-done.5 = bf16[1,32,256]{2,1,0:T(8,128)(2,1)S(1)} collective-permute-done((bf16[1,32,256]{2,1,0:T(8,128)(2,1)S(1)}, bf16[1,32,256]{2,1,0:T(8,128)(2,1)S(1)}, u32[]{:S(2)}, u32[]{:S(2)}) %collective-permute-start.5) | collective-permute-done | bytes 16416 | tf_op jit(solution)/shard_map/ppermute | solution.py:19
  21.1 2.3 %collective-permute-start.7 = (bf16[10,1,256]{2,1,0:T(2,128)(2,1)S(1)}, bf16[10,1,256]{2,1,0:T(2,128)(2,1)S(1)}, u32[]{:S(2)}, u32[]{:S(2)}) collective-permute-start(bf16[10,1,256]{2,1,0:T(2,128)(2,1)S(1)} %get-tuple-element.27), channel_id=1, source_target_pairs={{1,2},{2,1},{3,0},{0,3},{5,6},{6,5},{7,4},{4,7},{9,10},{10,9},{11,... | collective-permute-start | bytes 15368 | tf_op jit(solution)/shard_map/ppermute | solution.py:19
  31.0 3.3 %collective-permute-done.9 = bf16[1,32,256]{2,1,0:T(8,128)(2,1)} collective-permute-done((bf16[1,32,256]{2,1,0:T(8,128)(2,1)}, bf16[1,32,256]{2,1,0:T(8,128)(2,1)}, u32[]{:S(2)}, u32[]{:S(2)}) %collective-permute-start.9) | collective-permute-done | bytes 16416 | tf_op jit(solution)/shard_map/ppermute | solution.py:19
  35.9 2.2 %collective-permute-start.11 = (bf16[10,1,256]{2,1,0:T(2,128)(2,1)S(1)}, bf16[10,1,256]{2,1,0:T(2,128)(2,1)S(1)}, u32[]{:S(2)}, u32[]{:S(2)}) collective-permute-start(bf16[10,1,256]{2,1,0:T(2,128)(2,1)S(1)} %get-tuple-element.21), channel_id=1, source_target_pairs={{1,2},{2,1},{3,0},{0,3},{5,6},{6,5},{7,4},{4,7},{9,10},{10,9},{11,... | collective-permute-start | bytes 15368 | tf_op jit(solution)/shard_map/ppermute | solution.py:19
  38.9 1.9 %collective-permute-done.11 = bf16[10,1,256]{2,1,0:T(2,128)(2,1)S(1)} collective-permute-done((bf16[10,1,256]{2,1,0:T(2,128)(2,1)S(1)}, bf16[10,1,256]{2,1,0:T(2,128)(2,1)S(1)}, u32[]{:S(2)}, u32[]{:S(2)}) %collective-permute-start.11) | collective-permute-done | bytes 5152 | tf_op jit(solution)/shard_map/ppermute | solution.py:19
  42.0 3.8 %convolution_add_fusion = f32[256,1024]{1,0:T(8,128)S(1)} fusion(bf16[256,2304]{1,0:T(8,128)(2,1)S(1)} %constant_dynamic-update-slice_fusion.18, bf16[2304,1024]{1,0:T(8,128)(2,1)} %param.7, bf16[256,1024]{1,0:T(8,128)(2,1)S(1)} %bitcast.288), kind=kOutput, calls=%fused_computation.19 | convolution fusion | flops 1208483840 | bytes 7471104 | tf_op jit(solution)/shard_map/dot_general | solution.py:69
  47.9 3.7 %collective-permute-done.13 = bf16[1,32,1024]{2,1,0:T(8,128)(2,1)S(1)} collective-permute-done((bf16[1,32,1024]{2,1,0:T(8,128)(2,1)S(1)}, bf16[1,32,1024]{2,1,0:T(8,128)(2,1)S(1)}, u32[]{:S(2)}, u32[]{:S(2)}) %collective-permute-start.13) | collective-permute-done | bytes 65568 | tf_op jit(solution)/shard_map/ppermute | solution.py:19
  51.8 2.3 %collective-permute-start.14 = (bf16[10,1,1024]{2,1,0:T(2,128)(2,1)S(1)}, bf16[10,1,1024]{2,1,0:T(2,128)(2,1)S(1)}, u32[]{:S(2)}, u32[]{:S(2)}) collective-permute-start(bf16[10,1,1024]{2,1,0:T(2,128)(2,1)S(1)} %broadcast_select_fusion.15), channel_id=1, source_target_pairs={{1,2},{2,1},{3,0},{0,3},{5,6},{6,5},{7,4},{4,7},{9,10},{10,9},{11,... | collective-permute-start | bytes 61448 | tf_op jit(solution)/shard_map/ppermute | solution.py:19
  54.2 2.9 %collective-permute-done.14 = bf16[10,1,1024]{2,1,0:T(2,128)(2,1)S(1)} collective-permute-done((bf16[10,1,1024]{2,1,0:T(2,128)(2,1)S(1)}, bf16[10,1,1024]{2,1,0:T(2,128)(2,1)S(1)}, u32[]{:S(2)}, u32[]{:S(2)}) %collective-permute-start.14) | collective-permute-done | bytes 20512 | tf_op jit(solution)/shard_map/ppermute | solution.py:19
  64.6 3.7 %collective-permute-done.17 = bf16[1,32,1024]{2,1,0:T(8,128)(2,1)S(1)} collective-permute-done((bf16[1,32,1024]{2,1,0:T(8,128)(2,1)S(1)}, bf16[1,32,1024]{2,1,0:T(8,128)(2,1)S(1)}, u32[]{:S(2)}, u32[]{:S(2)}) %collective-permute-start.17) | collective-permute-done | bytes 65568 | tf_op jit(solution)/shard_map/ppermute | solution.py:19
  69.9 3.9 %collective-permute-done.18 = bf16[10,1,1024]{2,1,0:T(2,128)(2,1)S(1)} collective-permute-done((bf16[10,1,1024]{2,1,0:T(2,128)(2,1)S(1)}, bf16[10,1,1024]{2,1,0:T(2,128)(2,1)S(1)}, u32[]{:S(2)}, u32[]{:S(2)}) %collective-permute-start.18) | collective-permute-done | bytes 20512 | tf_op jit(solution)/shard_map/ppermute | solution.py:19
  80.5 4.0 %fusion.3 = f32[1024,2304]{1,0:T(8,128)S(1)} fusion(bf16[256,2304]{1,0:T(8,128)(2,1)S(1)} %copy-done.16, bf16[256,2304]{1,0:T(8,128)(2,1)S(1)} %copy-done.18, bf16[256,2304]{1,0:T(8,128)(2,1)S(1)} %constant_dynamic-update-slice_fusion.18, bf16[256,1024]{1,0:T(8,128)(2,1)S(1)} %fusion.25, bf16[256,1024]{1,0:T(8,128)(2,1)S(1)} %fusion.23, ...), kind=kOutput, calls=%fused_computation.6 | convolution fusion | flops 3639214080 | bytes 14548992 | tf_op jit(solution)/shard_map/dot_general | solution.py:105
  87.3 2.4 %collective-permute-done.21 = bf16[1,32,1024]{2,1,0:T(8,128)(2,1)S(1)} collective-permute-done((bf16[1,32,1024]{2,1,0:T(8,128)(2,1)S(1)}, bf16[1,32,1024]{2,1,0:T(8,128)(2,1)S(1)}, u32[]{:S(2)}, u32[]{:S(2)}) %collective-permute-start.21) | collective-permute-done | bytes 65568 | tf_op jit(solution)/shard_map/ppermute | solution.py:18
  90.8 2.1 %collective-permute-start.23 = (bf16[10,1,1024]{2,1,0:T(2,128)(2,1)S(1)}, bf16[10,1,1024]{2,1,0:T(2,128)(2,1)S(1)}, u32[]{:S(2)}, u32[]{:S(2)}) collective-permute-start(bf16[10,1,1024]{2,1,0:T(2,128)(2,1)S(1)} %broadcast_select_fusion.7), channel_id=1, source_target_pairs={{1,2},{2,1},{3,0},{0,3},{5,6},{6,5},{7,4},{4,7},{9,10},{10,9},{11,... | collective-permute-start | bytes 61448 | tf_op jit(solution)/shard_map/ppermute | solution.py:19
  94.0 2.2 %collective-permute-done.23 = bf16[10,1,1024]{2,1,0:T(2,128)(2,1)S(1)} collective-permute-done((bf16[10,1,1024]{2,1,0:T(2,128)(2,1)S(1)}, bf16[10,1,1024]{2,1,0:T(2,128)(2,1)S(1)}, u32[]{:S(2)}, u32[]{:S(2)}) %collective-permute-start.23) | collective-permute-done | bytes 20512 | tf_op jit(solution)/shard_map/ppermute | solution.py:19
  99.0 2.4 %fusion.2 = bf16[16,32,2304]{2,1,0:T(8,128)(2,1)} fusion(bf16[16,32,2304]{2,1,0:T(8,128)(2,1)S(1)} %collective-permute-done.20, f32[16,2,32,2304]{3,2,1,0:T(8,128)S(1)} %bitcast.203, pred[]{:T(512)S(6)} %eq.33), kind=kLoop, calls=%fused_computation.3 | loop fusion | flops 4718592 | bytes 14155777 | tf_op jit(solution)/shard_map/convert_element_type | solution.py:115
  101.3 7.2 %all-to-all-start = ((bf16[64,8,2304]{2,1,0:T(8,128)(2,1)}), bf16[64,8,2304]{2,1,0:T(8,128)(2,1)S(1)}, u32[]{:S(2)}, u32[]{:S(2)}) async-start(bf16[64,8,2304]{2,1,0:T(8,128)(2,1)} %bitcast.204), calls=%async_computation | async-start | bytes 4718592 | tf_op jit(solution)/shard_map/all_to_all | solution.py:116
  108.5 1.5 %convolution_add_fusion.10 = f32[256,256]{1,0:T(8,128)S(1)} fusion(f32[256,256]{1,0:T(8,128)S(1)} %fusion.54, bf16[256,1024]{1,0:T(8,128)(2,1)} %bitcast.220, bf16[2304,1024]{1,0:T(8,128)(2,1)} %param.7), kind=kOutput, calls=%fused_computation.29 | convolution fusion | flops 134283264 | bytes 1572864 | tf_op jit(solution)/shard_map/dot_general | solution.py:51
  110.3 1.4 %convolution_add_fusion.9 = f32[256,256]{1,0:T(8,128)S(1)} fusion(f32[256,256]{1,0:T(8,128)S(1)} %convolution_add_fusion.10, bf16[256,1024]{1,0:T(8,128)(2,1)S(1)} %bitcast.234, bf16[2304,1024]{1,0:T(8,128)(2,1)} %param.7), kind=kOutput, calls=%fused_computation.28 | convolution fusion | flops 134283264 | bytes 1572864 | tf_op jit(solution)/shard_map/dot_general | solution.py:51
  111.8 1.4 convolution_add_fusion.8
  113.2 1.4 %convolution_add_fusion.7 = f32[256,256]{1,0:T(8,128)S(1)} fusion(f32[256,256]{1,0:T(8,128)S(1)} %convolution_add_fusion.8, bf16[256,1024]{1,0:T(8,128)(2,1)S(1)} %copy-done.3, bf16[2304,1024]{1,0:T(8,128)(2,1)} %param.7), kind=kOutput, calls=%fused_computation.26 | convolution fusion | flops 134283264 | bytes 1572864 | tf_op jit(solution)/shard_map/dot_general | solution.py:51
  114.6 1.4 %convolution_add_fusion.6 = f32[256,256]{1,0:T(8,128)S(1)} fusion(f32[256,256]{1,0:T(8,128)S(1)} %convolution_add_fusion.7, bf16[256,1024]{1,0:T(8,128)(2,1)S(1)} %bitcast.231, bf16[2304,1024]{1,0:T(8,128)(2,1)} %param.7), kind=kOutput, calls=%fused_computation.25 | convolution fusion | flops 134283264 | bytes 1572864 | tf_op jit(solution)/shard_map/dot_general | solution.py:51
  116.1 1.4 %convolution_add_fusion.5 = f32[256,256]{1,0:T(8,128)S(1)} fusion(f32[256,256]{1,0:T(8,128)S(1)} %convolution_add_fusion.6, bf16[256,1024]{1,0:T(8,128)(2,1)S(1)} %bitcast.223, bf16[2304,1024]{1,0:T(8,128)(2,1)} %param.7), kind=kOutput, calls=%fused_computation.24 | convolution fusion | flops 134283264 | bytes 1572864 | tf_op jit(solution)/shard_map/dot_general | solution.py:51
  117.5 1.4 convolution_add_fusion.4
  118.9 2.1 %fusion.20 = bf16[256,256]{1,0:T(8,128)(2,1)} fusion(f32[256,256]{1,0:T(8,128)S(1)} %copy-done.9, f32[256,256]{1,0:T(8,128)S(1)} %convolution_add_fusion.4, bf16[256,1024]{1,0:T(8,128)(2,1)S(1)} %bitcast.235, bf16[2304,1024]{1,0:T(8,128)(2,1)} %param.7, pred[]{:T(512)} %bitcast), kind=kOutput, calls=%fused_computation.51 | convolution fusion | flops 134348800 | bytes 1704448 | tf_op jit(solution)/shard_map/dot_general | solution.py:51
  121.0 18.9 %all-to-all-done = bf16[64,8,2304]{2,1,0:T(8,128)(2,1)S(1)} async-done(((bf16[64,8,2304]{2,1,0:T(8,128)(2,1)}), bf16[64,8,2304]{2,1,0:T(8,128)(2,1)S(1)}, u32[]{:S(2)}, u32[]{:S(2)}) %all-to-all-start) | async-done | bytes 2359328 | tf_op jit(solution)/shard_map/all_to_all | solution.py:116
  (196 shorter events, 40.5 us)
Async XLA Ops:
  1.4 6.3 %copy-start.1 = (bf16[1,8,32,256]{3,2,1,0:T(8,128)(2,1)S(1)}, bf16[1,8,32,256]{3,2,1,0:T(8,128)(2,1)}, u32[]{:S(2)}) copy-start(bf16[1,8,32,256]{3,2,1,0:T(8,128)(2,1)} %param.8) | copy-start | bytes 393220
  1.4 6.2 %collective-permute-start = (bf16[1,32,256]{2,1,0:T(8,128)(2,1)S(1)}, bf16[1,32,256]{2,1,0:T(8,128)(2,1)S(1)}, u32[]{:S(2)}, u32[]{:S(2)}) collective-permute-start(bf16[1,32,256]{2,1,0:T(8,128)(2,1)S(1)} %get-tuple-element.131), channel_id=1, source_target_pairs={{0,4},{4,0},{8,12},{12,8},{16,20},{20,16},{24,28},{28,24},{1,5},{5... | collective-permute-start | bytes 49160 | tf_op jit(solution)/shard_map/ppermute | solution.py:18
  1.5 6.2 %collective-permute-start.1 = (bf16[1,32,256]{2,1,0:T(8,128)(2,1)S(1)}, bf16[1,32,256]{2,1,0:T(8,128)(2,1)S(1)}, u32[]{:S(2)}, u32[]{:S(2)}) collective-permute-start(bf16[1,32,256]{2,1,0:T(8,128)(2,1)S(1)} %get-tuple-element.132), channel_id=1, source_target_pairs={{4,8},{8,4},{12,16},{16,12},{20,24},{24,20},{28,0},{0,28},{5,9},{9... | collective-permute-start | bytes 49160 | tf_op jit(solution)/shard_map/ppermute | solution.py:19
  7.7 3.9 %collective-permute-start.2 = (bf16[10,1,256]{2,1,0:T(2,128)(2,1)S(1)}, bf16[10,1,256]{2,1,0:T(2,128)(2,1)S(1)}, u32[]{:S(2)}, u32[]{:S(2)}) collective-permute-start(bf16[10,1,256]{2,1,0:T(2,128)(2,1)S(1)} %broadcast_select_fusion.33), channel_id=1, source_target_pairs={{0,1},{1,0},{2,3},{3,2},{4,5},{5,4},{6,7},{7,6},{8,9},{9,8},{10,11... | collective-permute-start | bytes 15368 | tf_op jit(solution)/shard_map/ppermute | solution.py:18
  9.4 4.9 %collective-permute-start.3 = (bf16[10,1,256]{2,1,0:T(2,128)(2,1)S(1)}, bf16[10,1,256]{2,1,0:T(2,128)(2,1)S(1)}, u32[]{:S(2)}, u32[]{:S(2)}) collective-permute-start(bf16[10,1,256]{2,1,0:T(2,128)(2,1)S(1)} %get-tuple-element.32), channel_id=1, source_target_pairs={{1,2},{2,1},{3,0},{0,3},{5,6},{6,5},{7,4},{4,7},{9,10},{10,9},{11,... | collective-permute-start | bytes 15368 | tf_op jit(solution)/shard_map/ppermute | solution.py:19
  11.6 3.1 %copy-start = (bf16[2304,1024]{1,0:T(8,128)(2,1)S(1)}, bf16[2304,1024]{1,0:T(8,128)(2,1)}, u32[]{:S(2)}) copy-start(bf16[2304,1024]{1,0:T(8,128)(2,1)} %param.7) | copy-start | bytes 14155780
  16.4 1.3 collective-permute-start.4
  16.5 4.5 %collective-permute-start.5 = (bf16[1,32,256]{2,1,0:T(8,128)(2,1)S(1)}, bf16[1,32,256]{2,1,0:T(8,128)(2,1)S(1)}, u32[]{:S(2)}, u32[]{:S(2)}) collective-permute-start(bf16[1,32,256]{2,1,0:T(8,128)(2,1)S(1)} %get-tuple-element.128), channel_id=1, source_target_pairs={{4,8},{8,4},{12,16},{16,12},{20,24},{24,20},{28,0},{0,28},{5,9},{9... | collective-permute-start | bytes 49160 | tf_op jit(solution)/shard_map/ppermute | solution.py:19
  21.0 3.8 %collective-permute-start.6 = (bf16[10,1,256]{2,1,0:T(2,128)(2,1)S(1)}, bf16[10,1,256]{2,1,0:T(2,128)(2,1)S(1)}, u32[]{:S(2)}, u32[]{:S(2)}) collective-permute-start(bf16[10,1,256]{2,1,0:T(2,128)(2,1)S(1)} %broadcast_select_fusion.29), channel_id=1, source_target_pairs={{0,1},{1,0},{2,3},{3,2},{4,5},{5,4},{6,7},{7,6},{8,9},{9,8},{10,11... | collective-permute-start | bytes 15368 | tf_op jit(solution)/shard_map/ppermute | solution.py:18
  21.1 5.0 %collective-permute-start.7 = (bf16[10,1,256]{2,1,0:T(2,128)(2,1)S(1)}, bf16[10,1,256]{2,1,0:T(2,128)(2,1)S(1)}, u32[]{:S(2)}, u32[]{:S(2)}) collective-permute-start(bf16[10,1,256]{2,1,0:T(2,128)(2,1)S(1)} %get-tuple-element.27), channel_id=1, source_target_pairs={{1,2},{2,1},{3,0},{0,3},{5,6},{6,5},{7,4},{4,7},{9,10},{10,9},{11,... | collective-permute-start | bytes 15368 | tf_op jit(solution)/shard_map/ppermute | solution.py:19
  29.6 1.4 collective-permute-start.8
  29.6 4.7 %collective-permute-start.9 = (bf16[1,32,256]{2,1,0:T(8,128)(2,1)}, bf16[1,32,256]{2,1,0:T(8,128)(2,1)}, u32[]{:S(2)}, u32[]{:S(2)}) collective-permute-start(bf16[1,32,256]{2,1,0:T(8,128)(2,1)} %get-tuple-element.124), channel_id=1, source_target_pairs={{4,8},{8,4},{12,16},{16,12},{20,24},{24,20},{28,0},{0,28},{5,9},{9... | collective-permute-start | bytes 49160 | tf_op jit(solution)/shard_map/ppermute | solution.py:19
  35.1 3.8 %collective-permute-start.10 = (bf16[10,1,256]{2,1,0:T(2,128)(2,1)S(1)}, bf16[10,1,256]{2,1,0:T(2,128)(2,1)S(1)}, u32[]{:S(2)}, u32[]{:S(2)}) collective-permute-start(bf16[10,1,256]{2,1,0:T(2,128)(2,1)S(1)} %broadcast_select_fusion.25), channel_id=1, source_target_pairs={{0,1},{1,0},{2,3},{3,2},{4,5},{5,4},{6,7},{7,6},{8,9},{9,8},{10,11... | collective-permute-start | bytes 15368 | tf_op jit(solution)/shard_map/ppermute | solution.py:18
  35.9 4.9 %collective-permute-start.11 = (bf16[10,1,256]{2,1,0:T(2,128)(2,1)S(1)}, bf16[10,1,256]{2,1,0:T(2,128)(2,1)S(1)}, u32[]{:S(2)}, u32[]{:S(2)}) collective-permute-start(bf16[10,1,256]{2,1,0:T(2,128)(2,1)S(1)} %get-tuple-element.21), channel_id=1, source_target_pairs={{1,2},{2,1},{3,0},{0,3},{5,6},{6,5},{7,4},{4,7},{9,10},{10,9},{11,... | collective-permute-start | bytes 15368 | tf_op jit(solution)/shard_map/ppermute | solution.py:19
  46.6 1.3 collective-permute-start.12
  46.7 5.0 %collective-permute-start.13 = (bf16[1,32,1024]{2,1,0:T(8,128)(2,1)S(1)}, bf16[1,32,1024]{2,1,0:T(8,128)(2,1)S(1)}, u32[]{:S(2)}, u32[]{:S(2)}) collective-permute-start(bf16[1,32,1024]{2,1,0:T(8,128)(2,1)S(1)} %get-tuple-element.87), channel_id=1, source_target_pairs={{4,8},{8,4},{12,16},{16,12},{20,24},{24,20},{28,0},{0,28},{5,9},{9... | collective-permute-start | bytes 196616 | tf_op jit(solution)/shard_map/ppermute | solution.py:19
  46.9 12.1 %slice-start = ((s8[4718592]{0:T(1024)(128)(4,1)}), s8[4194304]{0:T(1024)(128)(4,1)S(1)}, s32[]{:S(2)}) async-start(s8[4718592]{0:T(1024)(128)(4,1)} %bitcast.200), calls=%async_computation.1 | async-start | bytes 8388608
  51.8 5.3 %collective-permute-start.14 = (bf16[10,1,1024]{2,1,0:T(2,128)(2,1)S(1)}, bf16[10,1,1024]{2,1,0:T(2,128)(2,1)S(1)}, u32[]{:S(2)}, u32[]{:S(2)}) collective-permute-start(bf16[10,1,1024]{2,1,0:T(2,128)(2,1)S(1)} %broadcast_select_fusion.15), channel_id=1, source_target_pairs={{1,2},{2,1},{3,0},{0,3},{5,6},{6,5},{7,4},{4,7},{9,10},{10,9},{11,... | collective-permute-start | bytes 61448 | tf_op jit(solution)/shard_map/ppermute | solution.py:19
  54.1 4.0 %collective-permute-start.15 = (bf16[10,1,1024]{2,1,0:T(2,128)(2,1)S(1)}, bf16[10,1,1024]{2,1,0:T(2,128)(2,1)S(1)}, u32[]{:S(2)}, u32[]{:S(2)}) collective-permute-start(bf16[10,1,1024]{2,1,0:T(2,128)(2,1)S(1)} %get-tuple-element.15), channel_id=1, source_target_pairs={{0,1},{1,0},{2,3},{3,2},{4,5},{5,4},{6,7},{7,6},{8,9},{9,8},{10,11... | collective-permute-start | bytes 61448 | tf_op jit(solution)/shard_map/ppermute | solution.py:18
  63.2 1.3 collective-permute-start.16
  63.3 5.0 %collective-permute-start.17 = (bf16[1,32,1024]{2,1,0:T(8,128)(2,1)S(1)}, bf16[1,32,1024]{2,1,0:T(8,128)(2,1)S(1)}, u32[]{:S(2)}, u32[]{:S(2)}) collective-permute-start(bf16[1,32,1024]{2,1,0:T(8,128)(2,1)S(1)} %get-tuple-element.83), channel_id=1, source_target_pairs={{4,8},{8,4},{12,16},{16,12},{20,24},{24,20},{28,0},{0,28},{5,9},{9... | collective-permute-start | bytes 196616 | tf_op jit(solution)/shard_map/ppermute | solution.py:19
  68.5 5.3 %collective-permute-start.18 = (bf16[10,1,1024]{2,1,0:T(2,128)(2,1)S(1)}, bf16[10,1,1024]{2,1,0:T(2,128)(2,1)S(1)}, u32[]{:S(2)}, u32[]{:S(2)}) collective-permute-start(bf16[10,1,1024]{2,1,0:T(2,128)(2,1)S(1)} %broadcast_select_fusion.11), channel_id=1, source_target_pairs={{1,2},{2,1},{3,0},{0,3},{5,6},{6,5},{7,4},{4,7},{9,10},{10,9},{11,... | collective-permute-start | bytes 61448 | tf_op jit(solution)/shard_map/ppermute | solution.py:19
  69.8 4.0 %collective-permute-start.19 = (bf16[10,1,1024]{2,1,0:T(2,128)(2,1)S(1)}, bf16[10,1,1024]{2,1,0:T(2,128)(2,1)S(1)}, u32[]{:S(2)}, u32[]{:S(2)}) collective-permute-start(bf16[10,1,1024]{2,1,0:T(2,128)(2,1)S(1)} %get-tuple-element.12), channel_id=1, source_target_pairs={{0,1},{1,0},{2,3},{3,2},{4,5},{5,4},{6,7},{7,6},{8,9},{9,8},{10,11... | collective-permute-start | bytes 61448 | tf_op jit(solution)/shard_map/ppermute | solution.py:18
  80.5 4.6 %copy-start.2 = (bf16[256,1024]{1,0:T(8,128)(2,1)}, bf16[256,1024]{1,0:T(8,128)(2,1)S(1)}, u32[]{:S(2)}) copy-start(bf16[256,1024]{1,0:T(8,128)(2,1)S(1)} %fusion.25) | copy-start | bytes 1572868
  84.9 14.0 %collective-permute-start.20 = (bf16[16,32,2304]{2,1,0:T(8,128)(2,1)S(1)}, bf16[16,32,2304]{2,1,0:T(8,128)(2,1)S(1)}, u32[]{:S(2)}, u32[]{:S(2)}) collective-permute-start(bf16[16,32,2304]{2,1,0:T(8,128)(2,1)S(1)} %fusion.9), channel_id=1, source_target_pairs={{0,4},{4,0},{1,5},{5,1},{2,6},{6,2},{3,7},{7,3},{8,12},{12,8},{9,1... | collective-permute-start | bytes 7077896 | tf_op jit(solution)/shard_map/ppermute | solution.py:114
  85.2 4.5 %collective-permute-start.21 = (bf16[1,32,1024]{2,1,0:T(8,128)(2,1)S(1)}, bf16[1,32,1024]{2,1,0:T(8,128)(2,1)S(1)}, u32[]{:S(2)}, u32[]{:S(2)}) collective-permute-start(bf16[1,32,1024]{2,1,0:T(8,128)(2,1)S(1)} %get-tuple-element.78), channel_id=1, source_target_pairs={{0,4},{4,0},{8,12},{12,8},{16,20},{20,16},{24,28},{28,24},{1,5},{5... | collective-permute-start | bytes 196616 | tf_op jit(solution)/shard_map/ppermute | solution.py:18
  85.7 4.9 %collective-permute-start.22 = (bf16[1,32,1024]{2,1,0:T(8,128)(2,1)S(1)}, bf16[1,32,1024]{2,1,0:T(8,128)(2,1)S(1)}, u32[]{:S(2)}, u32[]{:S(2)}) collective-permute-start(bf16[1,32,1024]{2,1,0:T(8,128)(2,1)S(1)} %get-tuple-element.79), channel_id=1, source_target_pairs={{4,8},{8,4},{12,16},{16,12},{20,24},{24,20},{28,0},{0,28},{5,9},{9... | collective-permute-start | bytes 196616 | tf_op jit(solution)/shard_map/ppermute | solution.py:19
  90.8 5.3 %collective-permute-start.23 = (bf16[10,1,1024]{2,1,0:T(2,128)(2,1)S(1)}, bf16[10,1,1024]{2,1,0:T(2,128)(2,1)S(1)}, u32[]{:S(2)}, u32[]{:S(2)}) collective-permute-start(bf16[10,1,1024]{2,1,0:T(2,128)(2,1)S(1)} %broadcast_select_fusion.7), channel_id=1, source_target_pairs={{1,2},{2,1},{3,0},{0,3},{5,6},{6,5},{7,4},{4,7},{9,10},{10,9},{11,... | collective-permute-start | bytes 61448 | tf_op jit(solution)/shard_map/ppermute | solution.py:19
  92.9 4.0 %collective-permute-start.24 = (bf16[10,1,1024]{2,1,0:T(2,128)(2,1)S(1)}, bf16[10,1,1024]{2,1,0:T(2,128)(2,1)S(1)}, u32[]{:S(2)}, u32[]{:S(2)}) collective-permute-start(bf16[10,1,1024]{2,1,0:T(2,128)(2,1)S(1)} %get-tuple-element.7), channel_id=1, source_target_pairs={{0,1},{1,0},{2,3},{3,2},{4,5},{5,4},{6,7},{7,6},{8,9},{9,8},{10,11... | collective-permute-start | bytes 61448 | tf_op jit(solution)/shard_map/ppermute | solution.py:18
  101.3 38.5 %all-to-all-start = ((bf16[64,8,2304]{2,1,0:T(8,128)(2,1)}), bf16[64,8,2304]{2,1,0:T(8,128)(2,1)S(1)}, u32[]{:S(2)}, u32[]{:S(2)}) async-start(bf16[64,8,2304]{2,1,0:T(8,128)(2,1)} %bitcast.204), calls=%async_computation | async-start | bytes 4718592 | tf_op jit(solution)/shard_map/all_to_all | solution.py:116
  113.2 2.9 %copy-start.6 = (bf16[8,32,1024]{2,1,0:T(8,128)(2,1)S(1)}, bf16[8,32,1024]{2,1,0:T(8,128)(2,1)}, u32[]{:S(2)}) copy-start(bf16[8,32,1024]{2,1,0:T(8,128)(2,1)} %get-tuple-element.55) | copy-start | bytes 1572868
  114.6 2.9 %copy-start.5 = (bf16[8,32,1024]{2,1,0:T(8,128)(2,1)S(1)}, bf16[8,32,1024]{2,1,0:T(8,128)(2,1)}, u32[]{:S(2)}) copy-start(bf16[8,32,1024]{2,1,0:T(8,128)(2,1)} %get-tuple-element.76) | copy-start | bytes 1572868
  (15 other events, 22.2 us)

commit v2 on v1

v2 whole, which is shorter than its diff:
```python
import functools

import jax
import jax.numpy as jnp
from jax import lax
from jax.experimental import pallas as pl
from jax.experimental.pallas import tpu as pltpu
from jax.sharding import Mesh, PartitionSpec as P


def ring_pairs(size, phase):
    pairs = [(i, (i + 1) % size) for i in range(phase, size, 2)]
    return [edge for a, b in pairs for edge in ((a, b), (b, a))]


BF = jnp.bfloat16
F32 = jnp.float32
R, L, C = 8, 32, 256
W = 48
ROWS_A = (("h", 3, 1), ("c", 2, 1), ("x0", 2, 4), ("x1", 1, 4), ("t1", 1, 1))
ROWS_B = (("g", 2, 4), ("q", 1, 1))
ROWS_C = (("g", 1, 4),)


def row_offsets(spec):
    table, at = {}, 0
    for name, width, parts in spec:
        for row in range(width):
            for part in range(parts):
                table[name, row, part] = at
                at += 1
    return table, at


def col_offsets(spec):
    table, at = {}, 0
    for name, width, parts in spec:
        for part in range(parts):
            for row in range(R + 2 * width):
                table[name, row, part] = at
                at += width
    return table, -(-at // 16) * 16


def quarter(part):
    return slice(part * C, (part + 1) * C)


def parities():
    return lax.axis_index("core"), lax.axis_index("sx") % 2


def arranged(odd, near, far, before, after):
    @pl.when(odd == 1)
    def _():
        before[...] = near[...]
        after[...] = far[...]

    @pl.when(odd == 0)
    def _():
        before[...] = far[...]
        after[...] = near[...]


def pack_columns(spec, own, above, below, odd, near, far, left, right):
    rows, _ = row_offsets(spec)
    cols, _ = col_offsets(spec)
    for name, width, parts in spec:
        for row in range(R + 2 * width):
            for part in range(parts):
                at = cols[name, row, part]
                if row < width:
                    unit = rows[name, row, part]
                    first, last = above[unit, 0:8, :], above[unit, 24:32, :]
                elif row >= R + width:
                    unit = rows[name, row - R - width, part]
                    first, last = below[unit, 0:8, :], below[unit, 24:32, :]
                else:
                    first, last = own(name, row - width, slice(0, 8), part), own(name, row - width, slice(24, 32), part)
                left[at : at + width, :] = first.astype(F32)[0:width]
                right[at : at + width, :] = last.astype(F32)[8 - width : 8]

    @pl.when(odd == 1)
    def _():
        near[...] = left[...].astype(BF)
        far[...] = right[...].astype(BF)

    @pl.when(odd == 0)
    def _():
        near[...] = right[...].astype(BF)
        far[...] = left[...].astype(BF)


def rows_a_kernel(h_ref, c_ref, x_ref, t_ref, near, far):
    odd, _ = parities()
    rows, _ = row_offsets(ROWS_A)
    for name, width, parts in ROWS_A:
        first = jnp.where(odd == 1, 0, R - width)
        last = jnp.where(odd == 1, R - width, 0)
        for row in range(width):
            for part in range(parts):
                unit = rows[name, row, part]
                for start, out in ((first, near), (last, far)):
                    at = start + row
                    if name == "h":
                        value = h_ref[0, at]
                    elif name == "c":
                        value = c_ref[0, at].astype(BF)
                    elif name == "t1":
                        value = t_ref[0, 0, at]
                    else:
                        value = x_ref[0, int(name[1]), at, :, quarter(part)]
                    out[unit] = value


def cols_a_kernel(h_ref, c_ref, x_ref, t_ref, near_r, far_r, near, far, above, below, left, right):
    row_odd, col_odd = parities()
    arranged(row_odd, near_r, far_r, above, below)

    def own(name, row, cells, part):
        if name == "h":
            return h_ref[0, row, cells]
        if name == "c":
            return c_ref[0, row, cells]
        if name == "t1":
            return t_ref[0, 0, row, cells]
        return x_ref[0, int(name[1]), row, cells, quarter(part)]

    pack_columns(ROWS_A, own, above, below, col_odd, near, far, left, right)


def cols_b_kernel(g_ref, q_ref, near_r, far_r, near, far, above, below, left, right):
    row_odd, col_odd = parities()
    arranged(row_odd, near_r, far_r, above, below)

    def own(name, row, cells, part):
        if name == "q":
            return q_ref[row, cells]
        return g_ref[row, cells, quarter(part)]

    pack_columns(ROWS_B, own, above, below, col_odd, near, far, left, right)


def cols_c_kernel(g_ref, near_r, far_r, near, far, above, below, left, right):
    row_odd, col_odd = parities()
    arranged(row_odd, near_r, far_r, above, below)

    def own(name, row, cells, part):
        return g_ref[row, cells, quarter(part)]

    pack_columns(ROWS_C, own, above, below, col_odd, near, far, left, right)


def unpack_columns(odd, near, far, left, right):
    @pl.when(odd == 1)
    def _():
        left[...] = near[...].astype(F32)
        right[...] = far[...].astype(F32)

    @pl.when(odd == 0)
    def _():
        left[...] = far[...].astype(F32)
        right[...] = near[...].astype(F32)


def border(at, width, left, right):
    cell = lax.broadcasted_iota(jnp.int32, (16, C), 0)
    out = jnp.zeros((16, C), F32)
    for i in range(width):
        out = jnp.where(cell == i, jnp.broadcast_to(right[at + i : at + i + 1, :], (16, C)), out)
        out = jnp.where(cell == 16 - width + i, jnp.broadcast_to(left[at + i : at + i + 1, :], (16, C)), out)
    return out


def widened_grads(spec, width, g_ref, above, below, left, right, gw):
    rows, _ = row_offsets(spec)
    cols, _ = col_offsets(spec)
    for row in range(R + 2 * width):
        fits = inside(width, row)
        for part in range(4):
            if row < width:
                mid = above[rows["g", row, part]]
            elif row >= R + width:
                mid = below[rows["g", row - R - width, part]]
            else:
                mid = g_ref[row - width, :, quarter(part)]
            full = jnp.concatenate([mid.astype(F32), border(cols["g", row, part], width, left, right)], axis=0)
            gw[row * W : (row + 1) * W, quarter(part)] = jnp.where(fits, full, 0.0).astype(BF)


def back(n, gw, w_ref, z):
    cells = n * W
    for side in range(3):
        total = None
        for up in range(3):
            k = up * 3 + side
            slab = gw[(2 - up) * W : (2 - up) * W + cells, :]
            term = lax.dot_general(
                slab, w_ref[k * C : (k + 1) * C, :], (((1,), (1,)), ((), ())), preferred_element_type=F32
            )
            total = term if total is None else total + term
        z[side, 0:n, 8:56, :] = total.reshape(n, W, C)

    def wrap(row, carry):
        z[0, row, 56:57, :] = z[0, row, 8:9, :]
        z[2, row, 7:8, :] = z[2, row, 55:56, :]
        return carry

    lax.fori_loop(0, n, wrap, 0)


def summed(z, row, cells):
    return z[0, row, 9 : 9 + cells, :] + z[1, row, 8 : 8 + cells, :] + z[2, row, 7 : 7 + cells, :]


def last_kernel(g_ref, w_ref, near_r, far_r, near_c, far_c, dh_ref, above, below, left, right, gw, z):
    row_odd, col_odd = parities()
    arranged(row_odd, near_r, far_r, above, below)
    unpack_columns(col_odd, near_c, far_c, left, right)
    widened_grads(ROWS_C, 1, g_ref, above, below, left, right, gw)
    back(R, gw, w_ref, z)

    def one(row, carry):
        dh_ref[0, row] = summed(z, row, L).astype(BF)
        return carry

    lax.fori_loop(0, R, one, 0)


def theirs_kernel(g0_ref, g1_ref, g2_ref, p_ref, mine_ref, out_ref, turned, theirs):
    other = 1 - lax.axis_index("core")
    for frame, g_ref in enumerate((g0_ref, g1_ref, g2_ref)):
        flat = g_ref[...].reshape(R * L, 4 * C).astype(F32)
        turned[:, quarter(frame)] = jnp.transpose(flat).astype(BF)

    def pick(block, carry):
        at = pl.ds(pl.multiple_of(block * 32, 32), 32)
        theirs[at, :] = turned[pl.ds(pl.multiple_of(block * 64 + other * 32, 32), 32), :]
        mine_ref[at, :] = turned[pl.ds(pl.multiple_of(block * 64 + 32 - other * 32, 32), 32), :]
        return carry

    lax.fori_loop(0, 16, pick, 0)

    def one(n, carry):
        at = pl.ds(pl.multiple_of(n * 3 * C, C), 3 * C)
        out_ref[:, at] = jnp.dot(theirs[...], p_ref[:, at], preferred_element_type=F32).astype(BF)
        return carry

    lax.fori_loop(0, 3, one, 0)


def mine_kernel(mine_ref, p_ref, got_ref, out_ref):
    def one(n, carry):
        at = pl.ds(pl.multiple_of(n * 3 * C, C), 3 * C)
        total = jnp.dot(mine_ref[...], p_ref[:, at], preferred_element_type=F32)
        out_ref[:, at] = (total + got_ref[:, at].astype(F32)).astype(BF)
        return carry

    lax.fori_loop(0, 3, one, 0)


def inside(by, row):
    at_row = (lax.axis_index("x") * 2 + lax.axis_index("core")) * R + row - by
    cell = lax.broadcasted_iota(jnp.int32, (W, C), 0)
    column = jnp.where(cell < 40, cell, cell - W) + lax.axis_index("sx") * L
    fits = (column >= 0) & (column < 4 * L)
    return fits & jnp.broadcast_to((at_row >= 0) & (at_row < 8 * R), (W, C))


def sigmoid(value):
    return 0.5 * jnp.tanh(0.5 * value) + 0.5


def forward_kernel(count_ref, h_ref, c_ref, x_ref, t_ref, w_ref, near_r, far_r, near_c, far_c,
                   seq_ref, patch_ref, m1_ref, m0_ref, t1_ref, g2_ref, q_ref, near_out, far_out,
                   above, below, left, right, hs, cs, gates, shifted, wide):
    row_odd, col_odd = parities()
    count = count_ref[0]
    arranged(row_odd, near_r, far_r, above, below)

    unpack_columns(col_odd, near_c, far_c, left, right)

    rows, _ = row_offsets(ROWS_A)
    cols, _ = col_offsets(ROWS_A)
    widths = {name: width for name, width, _ in ROWS_A}

    def main(name, row, part):
        width = widths[name]
        if row < width:
            return above[rows[name, row, part]].astype(F32)
        if row >= R + width:
            return below[rows[name, row - R - width, part]].astype(F32)
        row -= width
        if name == "h":
            return h_ref[0, row].astype(F32)
        if name == "c":
            return c_ref[0, row]
        if name == "t1":
            return t_ref[0, 1, row].astype(F32)
        return x_ref[0, int(name[1]), row, :, quarter(part)].astype(F32)

    def sides(name, row, part):
        width = widths[name]
        at = cols[name, row, part]
        return right[at : at + width, :], left[at : at + width, :]

    zero16 = jnp.zeros((16, C), F32)
    hs[...] = jnp.zeros_like(hs)
    for row in range(R + 6):
        hs[row, 8:40, :] = main("h", row, 0)
        after, before = sides("h", row, 0)
        hs[row, 40:43, :] = after
        hs[row, 53:56, :] = before
        hs[row, 8:56, :] = jnp.where(inside(3, row), hs[row, 8:56, :], 0.0)
    for row in range(R + 4):
        cs[row, 0:32, :] = main("c", row, 0)
        cs[row, 32:48, :] = zero16
        after, before = sides("c", row, 0)
        cs[row, 32:34, :] = after
        cs[row, 46:48, :] = before

    def load_gates(name, by):
        for row in range(R + 2 * by):
            for part in range(4):
                at = row * W
                gates[at : at + 32, quarter(part)] = main(name, row, part)
                gates[at + 32 : at + W, quarter(part)] = zero16
                after, before = sides(name, row, part)
                gates[at + 32 : at + 32 + by, quarter(part)] = after
                gates[at + W - by : at + W, quarter(part)] = before

    def shift(n_rows):
        def one(row, carry):
            hs[row, 7:8, :] = hs[row, 55:56, :]
            hs[row, 56:57, :] = hs[row, 8:9, :]
            for side in range(3):
                shifted[side, row] = hs[row, 7 + side : 55 + side, :].astype(BF)
            return carry

        lax.fori_loop(0, n_rows, one, 0)

    def own_patches(frame, by):
        for k in range(9):
            up, side = k // 3, k % 3
            patch_ref[frame, :, quarter(k)] = shifted[side, by + up : by + up + R, 0:32, :].reshape(R * L, C)

    for frame in range(3):
        by = 2 - frame
        n = R + 2 * by
        cells = n * W if by else R * L
        valid = frame < count
        wcols = W if by else L
        shift(n + 2)
        own_patches(frame, by)
        if by:
            load_gates("x" + str(frame), by)
            for k in range(9):
                up, side = k // 3, k % 3
                wide[0:cells, quarter(k)] = shifted[side, up : up + n].reshape(cells, C)

            def one(at_n, carry, cells=cells):
                at = pl.ds(pl.multiple_of(at_n * 2 * C, C), 2 * C)
                gates[0:cells, at] = gates[0:cells, at] + jnp.dot(
                    wide[0:cells, :], w_ref[:, at], preferred_element_type=F32
                )
                return carry
        else:

            def one(at_n, carry):
                at = pl.ds(pl.multiple_of(at_n * 2 * C, C), 2 * C)
                gates[0 : R * L, at] = x_ref[0, 2, :, :, at].reshape(R * L, 2 * C).astype(F32) + jnp.dot(
                    patch_ref[2], w_ref[:, at], preferred_element_type=F32
                )
                return carry

        lax.fori_loop(0, 2, one, 0)

        def gating(row, carry, frame=frame, by=by, wcols=wcols, valid=valid):
            start = pl.multiple_of(row * wcols, 16)
            g = gates[pl.ds(start, wcols), :]
            si = sigmoid(g[:, 0:C])
            sf = sigmoid(g[:, C : 2 * C])
            tg = jnp.tanh(g[:, 2 * C : 3 * C])
            so = sigmoid(g[:, 3 * C :])
            cell = cs[row + (0 if frame == 0 else frame), 0:wcols, :]
            cell_new = sf * cell + si * tg
            tc = jnp.tanh(cell_new)
            h_new = (so * tc).astype(BF).astype(F32)
            factors = (
                so * (1.0 - tc * tc),
                tg * si * (1.0 - si),
                cell * sf * (1.0 - sf),
                si * (1.0 - tg * tg),
                tc * so * (1.0 - so),
                sf,
            )
            h_old = hs[row + 1, 8 : 8 + wcols, :]
            keep = jnp.broadcast_to(valid, h_new.shape)
            h_next = jnp.where(keep, h_new, h_old)
            cs[row + frame, 0:wcols, :] = jnp.where(keep, cell_new, cell)
            if by:
                hs[row, 8:56, :] = jnp.where(inside(by, row), h_next, 0.0)
            if frame == 0:

                @pl.when((row >= 2) & (row < 2 + R))
                def _():
                    seq_ref[0, 0, row - 2] = h_next[0:L].astype(BF)
                    for i, factor in enumerate(factors):
                        m0_ref[i, row - 2] = factor[0:L].astype(BF)
            elif frame == 1:
                for i, factor in enumerate(factors):
                    m1_ref[i, row] = factor.astype(BF)

                @pl.when((row >= 1) & (row < 1 + R))
                def _():
                    seq_ref[0, 1, row - 1] = h_next[0:L].astype(BF)
            else:
                seq_ref[0, 2, row] = h_next.astype(BF)
                a, bi, bfg, bg, bo, _ = factors
                grad_h = t_ref[0, 2, row].astype(F32)
                dc_new = grad_h * a
                for part, value in enumerate((dc_new * bi, dc_new * bfg, dc_new * bg, grad_h * bo)):
                    g2_ref[row, :, quarter(part)] = jnp.where(keep, value, 0.0).astype(BF)
                q_ref[row] = jnp.where(keep, dc_new * sf, grad_h)
            return carry

        lax.fori_loop(0, n, gating, 0)
    for row in range(R + 2):
        t1_ref[row, 0:32, :] = main("t1", row, 0).astype(BF)
        after, before = sides("t1", row, 0)
        cell = lax.broadcasted_iota(jnp.int32, (16, C), 0)
        pad = jnp.where(cell == 0, jnp.broadcast_to(after, (16, C)), jnp.where(cell == 15, jnp.broadcast_to(before, (16, C)), 0.0))
        t1_ref[row, 32:48, :] = pad.astype(BF)
    rows_b, _ = row_offsets(ROWS_B)
    for name, width, parts in ROWS_B:
        first = jnp.where(row_odd == 1, 0, R - width)
        last = jnp.where(row_odd == 1, R - width, 0)
        for row in range(width):
            for part in range(parts):
                unit = rows_b[name, row, part]
                for start, out in ((first, near_out), (last, far_out)):
                    if name == "q":
                        out[unit] = q_ref[start + row].astype(BF)
                    else:
                        out[unit] = g2_ref[start + row, :, quarter(part)]


def backward_kernel(count_ref, t0_ref, w_ref, m1_ref, m0_ref, t1_ref, g2_ref, q_ref, near_r, far_r, near_c, far_c,
                    g1_ref, g0_ref, dh_ref, dc_ref, near_out, far_out, above, below, left, right, gw, qs, z):
    row_odd, col_odd = parities()
    count = count_ref[0]
    arranged(row_odd, near_r, far_r, above, below)

    unpack_columns(col_odd, near_c, far_c, left, right)

    rows, _ = row_offsets(ROWS_B)
    cols, _ = col_offsets(ROWS_B)
    valid2, valid1 = 2 < count, 1 < count
    widened_grads(ROWS_B, 2, g2_ref, above, below, left, right, gw)
    for row in range(R + 2):
        if row < 1:
            mid = above[rows["q", 0, 0]].astype(F32)
        elif row >= R + 1:
            mid = below[rows["q", 0, 0]].astype(F32)
        else:
            mid = q_ref[row - 1]
        qs[row, 0:32, :] = mid
        qs[row, 32:48, :] = border(cols["q", row, 0], 1, left, right)

    back(R + 2, gw, w_ref, z)

    def first(row, carry):
        keep2 = jnp.broadcast_to(valid2, (W, C))
        keep1 = jnp.broadcast_to(valid1, (W, C))
        q = qs[row]
        grad_h = jnp.where(keep2, summed(z, row, W), q) + t1_ref[row].astype(F32)
        grad_c = jnp.where(keep2, q, 0.0)
        a, bi, bfg, bg, bo, sf = (m1_ref[i, row].astype(F32) for i in range(6))
        dc_new = grad_c + grad_h * a
        keep = keep1 & inside(1, row)
        at = pl.ds(pl.multiple_of(row * W, W), W)
        for part, value in enumerate((dc_new * bi, dc_new * bfg, dc_new * bg, grad_h * bo)):
            gw[at, quarter(part)] = jnp.where(keep, value, 0.0).astype(BF)

        @pl.when((row >= 1) & (row < 1 + R))
        def _():
            dc_ref[0, row - 1] = jnp.where(keep1, dc_new * sf, grad_c)[0:L]
            dh_ref[0, row - 1] = grad_h[0:L]
            for part in range(4):
                g1_ref[row - 1, :, quarter(part)] = gw[pl.ds(pl.multiple_of(row * W, W), L), quarter(part)]

        return carry

    lax.fori_loop(0, R + 2, first, 0)
    back(R, gw, w_ref, z)

    def second(row, carry):
        keep1 = jnp.broadcast_to(valid1, (L, C))
        grad_h = jnp.where(keep1, summed(z, row, L), dh_ref[0, row]) + t0_ref[0, 0, row].astype(F32)
        a, bi, bfg, bg, bo, sf = (m0_ref[i, row].astype(F32) for i in range(6))
        dc_new = dc_ref[0, row] + grad_h * a
        for part, value in enumerate((dc_new * bi, dc_new * bfg, dc_new * bg, grad_h * bo)):
            g0_ref[row, :, quarter(part)] = value.astype(BF)
        dc_ref[0, row] = dc_new * sf
        return carry

    lax.fori_loop(0, R, second, 0)
    first_row = jnp.where(row_odd == 1, 0, R - 1)
    last_row = jnp.where(row_odd == 1, R - 1, 0)
    for part in range(4):
        near_out[part] = g0_ref[first_row, :, quarter(part)]
        far_out[part] = g0_ref[last_row, :, quarter(part)]


def whole(shape):
    return pl.BlockSpec(shape, lambda _: (0,) * len(shape))


def call(kernel, inputs, outs, scratch, blocks=None, scalar=False, name=None, flops=0, limit=16):
    blocks = blocks or {}
    specs = [whole(blocks.get(i, value.shape)) for i, value in enumerate(inputs)]
    if scalar:
        specs[0] = pl.BlockSpec(memory_space=pltpu.SMEM)
    size = sum(value.size * value.dtype.itemsize for value in inputs)
    return pl.pallas_call(
        kernel,
        grid=(1,),
        in_specs=specs,
        out_specs=[whole(out.shape) for out in outs],
        out_shape=outs,
        scratch_shapes=scratch,
        name=name,
        compiler_params=pltpu.CompilerParams(vmem_limit_bytes=limit << 20),
        cost_estimate=pl.CostEstimate(flops=flops, bytes_accessed=size, transcendentals=0),
    )(*inputs)


def swap_rows(near, far):
    axis = ("x", "core")
    return lax.ppermute(near, axis, ring_pairs(8, 0)), lax.ppermute(far, axis, ring_pairs(8, 1))


def swap_cols(near, far):
    return lax.ppermute(near, "sx", ring_pairs(4, 0)), lax.ppermute(far, "sx", ring_pairs(4, 1))


def body(input_gates, recur_weight, hidden_init, cell_init, hidden_cot, frame_count):
    width = C
    out = jax.ShapeDtypeStruct
    vmem = pltpu.VMEM
    _, row_units = row_offsets(ROWS_A)
    _, col_units = col_offsets(ROWS_A)
    first_two = {2: (1, 2, R, L, 4 * C)}
    middle = hidden_cot[:, 1:2]
    border = out((row_units, L, C), BF)
    near, far = call(
        rows_a_kernel, (hidden_init, cell_init, input_gates, middle), [border] * 2, [], first_two, name="rows_a"
    )
    near_r, far_r = swap_rows(near, far)
    strip = out((col_units, C), BF)
    near, far = call(
        cols_a_kernel,
        (hidden_init, cell_init, input_gates, middle, near_r, far_r),
        [strip] * 2,
        [vmem((row_units, L, C), BF)] * 2 + [vmem((col_units, C), F32)] * 2,
        first_two,
        name="cols_a",
    )
    near_c, far_c = swap_cols(near, far)
    _, row_units_b = row_offsets(ROWS_B)
    _, col_units_b = col_offsets(ROWS_B)
    hidden_seq, patches, m1, m0, t1, g2, q, near, far = call(
        forward_kernel,
        (frame_count, hidden_init, cell_init, input_gates, hidden_cot, recur_weight, near_r, far_r, near_c, far_c),
        [
            out((1, 3, R, L, C), BF),
            out((3, R * L, 9 * C), BF),
            out((6, R + 2, W, C), BF),
            out((6, R, L, C), BF),
            out((R + 2, W, C), BF),
            out((R, L, 4 * C), BF),
            out((R, L, C), F32),
            out((row_units_b, L, C), BF),
            out((row_units_b, L, C), BF),
        ],
        [vmem((row_units, L, C), BF)] * 2
        + [vmem((col_units, C), F32)] * 2
        + [
            vmem((R + 6, 64, C), F32),
            vmem((R + 4, W, C), F32),
            vmem(((R + 4) * W, 4 * C), F32),
            vmem((3, R + 6, W, C), BF),
            vmem(((R + 4) * W, 9 * C), BF),
        ],
        scalar=True,
        name="forward",
        limit=28,
        flops=6 * 10**9,
    )
    near_r, far_r = swap_rows(near, far)
    strip = out((col_units_b, C), BF)
    near, far = call(
        cols_b_kernel,
        (g2, q, near_r, far_r),
        [strip] * 2,
        [vmem((row_units_b, L, C), BF)] * 2 + [vmem((col_units_b, C), F32)] * 2,
        name="cols_b",
    )
    near_c, far_c = swap_cols(near, far)
    g1, g0, _, cell_grad, near_c_rows, far_c_rows = call(
        backward_kernel,
        (frame_count, hidden_cot, recur_weight, m1, m0, t1, g2, q, near_r, far_r, near_c, far_c),
        [out((R, L, 4 * C), BF), out((R, L, 4 * C), BF), out((1, R, L, C), F32), out((1, R, L, C), F32),
         out((4, L, C), BF), out((4, L, C), BF)],
        [vmem((row_units_b, L, C), BF)] * 2
        + [vmem((col_units_b, C), F32)] * 2
        + [vmem(((R + 4) * W, 4 * C), BF), vmem((R + 2, W, C), F32), vmem((3, R + 2, 64, C), F32)],
        {1: (1, 1, R, L, C)},
        scalar=True,
        name="backward",
        limit=24,
        flops=4 * 10**9,
    )
    _, col_units_c = col_offsets(ROWS_C)
    near_r, far_r = swap_rows(near_c_rows, far_c_rows)
    flat_patches = patches.reshape(3 * R * L, 9 * C)
    half = out((512, 9 * C), BF)
    mine, theirs = call(
        theirs_kernel,
        (g0, g1, g2, flat_patches),
        [out((512, 3 * C), BF), half],
        [vmem((4 * C, 3 * C), BF), vmem((512, 3 * C), BF)],
        name="theirs",
        flops=2 * 10**9,
    )
    got = lax.ppermute(theirs, "core", [(0, 1), (1, 0)])
    (chip_sum,) = call(mine_kernel, (mine, flat_patches, got), [half], [], name="mine", flops=2 * 10**9)
    strip = out((col_units_c, C), BF)
    near, far = call(
        cols_c_kernel,
        (g0, near_r, far_r),
        [strip] * 2,
        [vmem((4, L, C), BF)] * 2 + [vmem((col_units_c, C), F32)] * 2,
        name="cols_c",
    )
    near_c, far_c = swap_cols(near, far)
    chip_sum, near_c, far_c = lax.optimization_barrier((chip_sum, near_c, far_c))
    (hidden_grad,) = call(
        last_kernel,
        (g0, recur_weight, near_r, far_r, near_c, far_c),
        [out((1, R, L, C), BF)],
        [vmem((4, L, C), BF)] * 2
        + [vmem((col_units_c, C), F32)] * 2
        + [vmem(((R + 2) * W, 4 * C), BF), vmem((3, R, 64, C), F32)],
        name="last",
        flops=2 * 10**9,
    )
    parts = lax.all_to_all(chip_sum, ("dp", "x", "sx"), 0, 0, tiled=True)
    weight_grad = jnp.sum(parts.reshape(64, 8, 9 * width).astype(jnp.float32), axis=0).T
    gate_grad = jnp.stack([g0, g1, g2])[None]
    return (hidden_seq, weight_grad, gate_grad, hidden_grad, cell_grad)


def solution(mesh):
    split = Mesh(mesh.devices.reshape(4, 4, 2, 4), ("dp", "x", "core", "sx"))
    sy = ("x", "core")
    step = jax.shard_map(
        body,
        mesh=split,
        in_specs=(
            P("dp", None, sy, "sx", None),
            P(),
            P("dp", sy, "sx", None),
            P("dp", sy, "sx", None),
            P("dp", None, sy, "sx", None),
            P("dp"),
        ),
        out_specs=(
            P("dp", None, sy, "sx", None),
            P(None, ("dp", "x", "core", "sx")),
            P("dp", None, sy, "sx", None),
            P("dp", sy, "sx", None),
            P("dp", sy, "sx", None),
        ),
        check_vma=False,
    )
    return step
```

time: 142 us -> 113 us (0.80)
  matrix products: 30.1 us -> 0 us
  Pallas kernels: 0 us -> 30.1 us
  waiting for transfers between devices: 57.1 us -> 43.7 us
  other arithmetic: 14.4 us -> 3.96 us
  starting transfers between devices: 27.1 us -> 24.5 us
    pallas_call x0 -> x9, Pallas kernels: none -> 30.1 us  [call(): pl.pallas_call(kernel, grid=(1,), in_specs=specs, out_specs=[whole(out.sh...]
    dot_general x31 -> x0, matrix products: 30.1 us -> none  [the longest x27 19.5 us: back_conv(): lax.dot_general(slab, weight_block, (((1,), (1,)), ((), ())), preferred_e...]
    ppermute x24 -> x12, waiting for transfers between devices: 38.3 us -> 17.6 us  [the longest x3 8.53 us: swap_rows(): lax.ppermute(far, axis, ring_pairs(8, 1))]
    all_to_all x1, waiting for transfers between devices: 18.9 us -> 26.1 us  [body(): parts = lax.all_to_all(chip_sum, ('dp', 'x', 'sx'), 0, 0, tiled=True)]
    slice x13 -> x1, local copies, waits for them, and re-layouts: 5.66 us -> 0.92 us  [body(): middle = hidden_cot[:, 1:2]]
    unnamed x66 -> x20, local copies, waits for them, and re-layouts: 4.02 us -> 7.94 us
    select_n x32 -> x0, other arithmetic: 3.81 us -> none  [the longest x12 1.75 us: with_halo(): near = lax.ppermute(jnp.where(odd, first, last), axis, ring_pairs(size, 0))]
    convert_element_type x11 -> x0, other arithmetic: 3.7 us -> none  [the longest x1 2.38 us: body(): (mine + got.astype(jnp.float32)).astype(jnp.bfloat16)]
  transfers between devices with their start and end apart: 26 -> 14, of which waited for: 21 -> 9; matrix products, arithmetic and copies ran while one was open for 15% -> 1% of each run, Pallas kernels for 0% -> 6%
where the time goes in v2:
time: 113 us
  waiting for transfers between devices  43.7 us (39%)
  Pallas kernels  30.1 us (27%)
  starting transfers between devices  24.5 us (22%)
  local copies, waits for them, and re-layouts  8.86 us (8%)
  other arithmetic  3.96 us (4%)
  between operations  1.4 us (1%)
    pallas_call x9, Pallas kernels, call(): pl.pallas_call(kernel, grid=(1,), in_specs=specs, out_specs=[whole(out.sh...  30.1 us
    all_to_all x1, waiting for transfers between devices, body(): parts = lax.all_to_all(chip_sum, ('dp', 'x', 'sx'), 0, 0, tiled=True)  26.1 us
    ppermute x3, waiting for transfers between devices, swap_rows(): lax.ppermute(far, axis, ring_pairs(8, 1))  8.53 us
    unnamed x20, local copies, waits for them, and re-layouts  7.94 us
    all_to_all x1, starting transfers between devices, body(): parts = lax.all_to_all(chip_sum, ('dp', 'x', 'sx'), 0, 0, tiled=True)  7.66 us
    ppermute x3, starting transfers between devices, swap_rows(): lax.ppermute(far, axis, ring_pairs(8, 1))  6.89 us
    ppermute x3, starting transfers between devices, swap_cols(): lax.ppermute(far, 'sx', ring_pairs(4, 1))  6.62 us
    ppermute x3, waiting for transfers between devices, swap_cols(): lax.ppermute(far, 'sx', ring_pairs(4, 1))  4.2 us
  transfers between devices with their start and end apart: 14, of which 9 were waited for; matrix products, arithmetic and copies ran while one was open for 1% of the time, Pallas kernels for 6%

profile of v2, /device:TPU:0, one launch (start us, length us, event | category | flops | bytes accessed | tf_op | source)
XLA Modules:
  0.0 112.5 jit_solution(14456820128340990790)
XLA Ops:
  0.6 0.9 slice.3.t_ref
  1.6 1.4 %copy-done = bf16[1,3,8,32,1024]{4,3,2,1,0:T(8,128)(2,1)S(1)} copy-done((bf16[1,3,8,32,1024]{4,3,2,1,0:T(8,128)(2,1)S(1)}, bf16[1,3,8,32,1024]{4,3,2,1,0:T(8,128)(2,1)}, u32[]{:S(2)}) %copy-start) | copy-done | bytes 1572888
  3.0 0.9 copy-done.2
  3.9 0.9 copy-done.4
  5.0 3.0 %collective-permute-start.1 = (bf16[18,32,256]{2,1,0:T(8,128)(2,1)S(1)}, bf16[18,32,256]{2,1,0:T(8,128)(2,1)S(1)}, u32[]{:S(2)}, u32[]{:S(2)}) collective-permute-start(bf16[18,32,256]{2,1,0:T(8,128)(2,1)S(1)} %get-tuple-element.33), channel_id=1, source_target_pairs={{4,8},{8,4},{12,16},{16,12},{20,24},{24,20},{28,0},{0,28},{5,9},{9... | collective-permute-start | bytes 884744 | tf_op jit(solution)/shard_map/ppermute | solution.py:540
  8.0 4.5 %collective-permute-done.1.far_r = bf16[18,32,256]{2,1,0:T(8,128)(2,1)S(1)} collective-permute-done((bf16[18,32,256]{2,1,0:T(8,128)(2,1)S(1)}, bf16[18,32,256]{2,1,0:T(8,128)(2,1)S(1)}, u32[]{:S(2)}, u32[]{:S(2)}) %collective-permute-start.1) | collective-permute-done | bytes 294944 | tf_op jit(solution)/shard_map/ppermute | solution.py:540
  12.6 1.8 %collective-permute-start.2 = (bf16[224,256]{1,0:T(8,128)(2,1)S(1)}, bf16[224,256]{1,0:T(8,128)(2,1)S(1)}, u32[]{:S(2)}, u32[]{:S(2)}) collective-permute-start(bf16[224,256]{1,0:T(8,128)(2,1)S(1)} %get-tuple-element.34), channel_id=1, source_target_pairs={{0,1},{1,0},{2,3},{3,2},{4,5},{5,4},{6,7},{7,6},{8,9},{9,8},{10,11... | collective-permute-start | bytes 344072 | tf_op jit(solution)/shard_map/ppermute | solution.py:544
  14.4 2.2 %collective-permute-start.3 = (bf16[224,256]{1,0:T(8,128)(2,1)S(1)}, bf16[224,256]{1,0:T(8,128)(2,1)S(1)}, u32[]{:S(2)}, u32[]{:S(2)}) collective-permute-start(bf16[224,256]{1,0:T(8,128)(2,1)S(1)} %get-tuple-element.35), channel_id=1, source_target_pairs={{1,2},{2,1},{3,0},{0,3},{5,6},{6,5},{7,4},{4,7},{9,10},{10,9},{11,... | collective-permute-start | bytes 344072 | tf_op jit(solution)/shard_map/ppermute | solution.py:544
  17.2 0.3 collective-permute-done.2.near_c
  17.5 2.9 %collective-permute-done.3.far_c = bf16[224,256]{1,0:T(8,128)(2,1)S(1)} collective-permute-done((bf16[224,256]{1,0:T(8,128)(2,1)S(1)}, bf16[224,256]{1,0:T(8,128)(2,1)S(1)}, u32[]{:S(2)}, u32[]{:S(2)}) %collective-permute-start.3) | collective-permute-done | bytes 114720 | tf_op jit(solution)/shard_map/ppermute | solution.py:544
  20.4 2.3 %copy-done.7 = bf16[2304,1024]{1,0:T(8,128)(2,1)S(1)} copy-done((bf16[2304,1024]{1,0:T(8,128)(2,1)S(1)}, bf16[2304,1024]{1,0:T(8,128)(2,1)}, u32[]{:S(2)}) %copy-start.7) | copy-done | bytes 4718616
  22.8 12.0 %forward.1 = (bf16[1,3,8,32,256]{4,3,2,1,0:T(8,128)(2,1)}, bf16[3,256,2304]{2,1,0:T(8,128)(2,1)S(1)}, bf16[6,10,48,256]{3,2,1,0:T(8,128)(2,1)S(1)}, bf16[6,8,32,...) custom-call(s32[1]{0:T(128)S(6)} %copy.11.count_ref, ...), custom_call_target="tpu_custom_call" | custom-call | flops 6000000000 | bytes 7897092 | tf_op jit(solution)/shard_map/forward/pallas_call | solution.py:525
  34.8 2.5 %collective-permute-start.5 = (bf16[9,32,256]{2,1,0:T(8,128)(2,1)S(1)}, bf16[9,32,256]{2,1,0:T(8,128)(2,1)S(1)}, u32[]{:S(2)}, u32[]{:S(2)}) collective-permute-start(bf16[9,32,256]{2,1,0:T(8,128)(2,1)S(1)} %get-tuple-element.43), channel_id=1, source_target_pairs={{4,8},{8,4},{12,16},{16,12},{20,24},{24,20},{28,0},{0,28},{5,9},{9... | collective-permute-start | bytes 442376 | tf_op jit(solution)/shard_map/ppermute | solution.py:540
  37.3 3.3 %collective-permute-done.5.far_r = bf16[9,32,256]{2,1,0:T(8,128)(2,1)S(1)} collective-permute-done((bf16[9,32,256]{2,1,0:T(8,128)(2,1)S(1)}, bf16[9,32,256]{2,1,0:T(8,128)(2,1)S(1)}, u32[]{:S(2)}, u32[]{:S(2)}) %collective-permute-start.5) | collective-permute-done | bytes 147488 | tf_op jit(solution)/shard_map/ppermute | solution.py:540
  40.8 2.3 %collective-permute-start.7 = (bf16[112,256]{1,0:T(8,128)(2,1)S(1)}, bf16[112,256]{1,0:T(8,128)(2,1)S(1)}, u32[]{:S(2)}, u32[]{:S(2)}) collective-permute-start(bf16[112,256]{1,0:T(8,128)(2,1)S(1)} %get-tuple-element.45), channel_id=1, source_target_pairs={{1,2},{2,1},{3,0},{0,3},{5,6},{6,5},{7,4},{4,7},{9,10},{10,9},{11,... | collective-permute-start | bytes 172040 | tf_op jit(solution)/shard_map/ppermute | solution.py:544
  43.0 1.9 %collective-permute-done.6.near_c = bf16[112,256]{1,0:T(8,128)(2,1)S(1)} collective-permute-done((bf16[112,256]{1,0:T(8,128)(2,1)S(1)}, bf16[112,256]{1,0:T(8,128)(2,1)S(1)}, u32[]{:S(2)}, u32[]{:S(2)}) %collective-permute-start.6) | collective-permute-done | bytes 57376 | tf_op jit(solution)/shard_map/ppermute | solution.py:544
  44.9 1.3 %collective-permute-done.7.far_c = bf16[112,256]{1,0:T(8,128)(2,1)S(1)} collective-permute-done((bf16[112,256]{1,0:T(8,128)(2,1)S(1)}, bf16[112,256]{1,0:T(8,128)(2,1)S(1)}, u32[]{:S(2)}, u32[]{:S(2)}) %collective-permute-start.7) | collective-permute-done | bytes 57376 | tf_op jit(solution)/shard_map/ppermute | solution.py:544
  46.2 7.9 %backward.1 = (bf16[8,32,1024]{2,1,0:T(8,128)(2,1)S(1)}, bf16[8,32,1024]{2,1,0:T(8,128)(2,1)S(1)}, f32[1,8,32,256]{3,2,1,0:T(8,128)}, f32[1,8,32,256]{3,2,1,0:T(...) custom-call(s32[1]{0:T(128)S(6)} %copy.11.count_ref, bf16[1,3,8,32,256]{4,3,2,1,0:T(8,128)(2,1)S(1)} %copy-done.6, ...), custom_call_target="tpu_custom_call" | custom-call | flops 4000000000 | bytes 8814596 | tf_op jit(solution)/shard_map/backward/pallas_call | solution.py:525
  54.2 3.0 %theirs.1 = (bf16[512,768]{1,0:T(8,128)(2,1)S(1)}, bf16[512,2304]{1,0:T(8,128)(2,1)S(1)}) custom-call(bf16[8,32,1024]{2,1,0:T(8,128)(2,1)S(1)} %get-tuple-element.46.g0_ref.g_ref, bf16[8,32,1024]{2,1,0:T(8,128)(2,1)S(1)} %get-tuple-element.47.g1_ref, bf16[8,32,1024]{2,1,0:T(8,128)(2,1)S(1)} %get-tuple-element.40.g_ref.g2_ref, bf16[768,2304]{1,0:T(8,128)(2,1)S(1)} %bitcast.8), custom_call_target="tpu_custom_call" | custom-call | flops 2000000000 | bytes 5111808 | tf_op jit(solution)/shard_map/theirs/pallas_call | solution.py:525
  57.3 0.5 collective-permute-start.9
  57.8 1.4 %collective-permute-start.10 = (bf16[4,32,256]{2,1,0:T(8,128)(2,1)S(1)}, bf16[4,32,256]{2,1,0:T(8,128)(2,1)S(1)}, u32[]{:S(2)}, u32[]{:S(2)}) collective-permute-start(bf16[4,32,256]{2,1,0:T(8,128)(2,1)S(1)} %get-tuple-element.52), channel_id=1, source_target_pairs={{4,8},{8,4},{12,16},{16,12},{20,24},{24,20},{28,0},{0,28},{5,9},{9... | collective-permute-start | bytes 196616 | tf_op jit(solution)/shard_map/ppermute | solution.py:540
  59.2 2.7 %collective-permute-done.9.near_r = bf16[4,32,256]{2,1,0:T(8,128)(2,1)S(1)} collective-permute-done((bf16[4,32,256]{2,1,0:T(8,128)(2,1)S(1)}, bf16[4,32,256]{2,1,0:T(8,128)(2,1)S(1)}, u32[]{:S(2)}, u32[]{:S(2)}) %collective-permute-start.9) | collective-permute-done | bytes 65568 | tf_op jit(solution)/shard_map/ppermute | solution.py:540
  61.9 0.8 collective-permute-done.10.far_r
  62.8 0.8 collective-permute-start.11
  63.6 2.2 %collective-permute-start.12 = (bf16[48,256]{1,0:T(8,128)(2,1)S(1)}, bf16[48,256]{1,0:T(8,128)(2,1)S(1)}, u32[]{:S(2)}, u32[]{:S(2)}) collective-permute-start(bf16[48,256]{1,0:T(8,128)(2,1)S(1)} %get-tuple-element.54), channel_id=1, source_target_pairs={{1,2},{2,1},{3,0},{0,3},{5,6},{6,5},{7,4},{4,7},{9,10},{10,9},{11,... | collective-permute-start | bytes 73736 | tf_op jit(solution)/shard_map/ppermute | solution.py:544
  65.8 3.8 %mine.1 = bf16[512,2304]{1,0:T(8,128)(2,1)} custom-call(bf16[512,768]{1,0:T(8,128)(2,1)S(1)} %get-tuple-element.49.mine_ref, bf16[768,2304]{1,0:T(8,128)(2,1)S(1)} %bitcast.9, bf16[512,2304]{1,0:T(8,128)(2,1)S(1)} %collective-permute-done.8.got_ref), custom_call_target="tpu_custom_call" | custom-call | flops 2000000000 | bytes 6684672 | tf_op jit(solution)/shard_map/mine/pallas_call | solution.py:525
  69.6 7.7 %all-to-all-start = ((bf16[64,8,2304]{2,1,0:T(8,128)(2,1)}), bf16[64,8,2304]{2,1,0:T(8,128)(2,1)}, u32[]{:S(2)}, u32[]{:S(2)}) async-start(bf16[64,8,2304]{2,1,0:T(8,128)(2,1)} %bitcast.1), calls=%async_computation | async-start | bytes 4718592 | tf_op jit(solution)/shard_map/all_to_all | solution.py:658
  77.2 1.3 %maximum_bitcast_fusion = bf16[1,3,8,32,1024]{4,3,2,1,0:T(8,128)(2,1)} fusion(bf16[1,8,32,1024]{3,2,1,0:T(8,128)(2,1)S(1)} %bitcast.11, bf16[1,8,32,1024]{3,2,1,0:T(8,128)(2,1)S(1)} %bitcast.12, bf16[1,8,32,1024]{3,2,1,0:T(8,128)(2,1)S(1)} %bitcast.10), kind=kLoop, calls=%fused_computation.1 | loop fusion | flops 1572864 | bytes 3145728 | tf_op jit(solution)/shard_map/broadcast_in_dim | solution.py:660
  78.6 2.3 %copy-done.9 = bf16[2304,1024]{1,0:T(8,128)(2,1)S(1)} copy-done((bf16[2304,1024]{1,0:T(8,128)(2,1)S(1)}, bf16[2304,1024]{1,0:T(8,128)(2,1)}, u32[]{:S(2)}) %copy-start.9) | copy-done | bytes 4718616
  80.9 2.9 %last.1 = bf16[1,8,32,256]{3,2,1,0:T(8,128)(2,1)} custom-call(bf16[8,32,1024]{2,1,0:T(8,128)(2,1)S(1)} %get-tuple-element.46.g0_ref.g_ref, bf16[2304,1024]{1,0:T(8,128)(2,1)S(1)} %copy-done.9, bf16[4,32,256]{2,1,0:T(8,128)(2,1)S(1)} %collective-permute-done.9.near_r, bf16[4,32,256]{2,1,0:T(8,128)(2,1)S(1)} %collective-permute-done.10.far_r, ...), custom_call_target="tpu_custom_call" | custom-call | flops 2000000000 | bytes 5423104 | tf_op jit(solution)/shard_map/last/pallas_call | solution.py:525
  83.8 26.1 %all-to-all-done = bf16[64,8,2304]{2,1,0:T(8,128)(2,1)} async-done(((bf16[64,8,2304]{2,1,0:T(8,128)(2,1)}), bf16[64,8,2304]{2,1,0:T(8,128)(2,1)}, u32[]{:S(2)}, u32[]{:S(2)}) %all-to-all-start) | async-done | bytes 2359328 | tf_op jit(solution)/shard_map/all_to_all | solution.py:658
  109.9 2.6 %convert_reduce_fusion = f32[8,2304]{1,0:T(8,128)} fusion(bf16[64,8,2304]{2,1,0:T(8,128)(2,1)} %all-to-all-done), kind=kLoop, calls=%fused_computation | loop fusion | flops 2340864 | bytes 2433024 | tf_op jit(solution)/shard_map/reduce_sum | solution.py:659
  (28 shorter events, 0.8 us)
Async XLA Ops:
  1.6 1.4 %copy-start = (bf16[1,3,8,32,1024]{4,3,2,1,0:T(8,128)(2,1)S(1)}, bf16[1,3,8,32,1024]{4,3,2,1,0:T(8,128)(2,1)}, u32[]{:S(2)}) copy-start(bf16[1,3,8,32,1024]{4,3,2,1,0:T(8,128)(2,1)} %x_ref.5) | copy-start | bytes 4718596
  3.0 0.9 copy-start.2
  3.9 0.9 copy-start.4
  4.8 15.6 %copy-start.1 = (bf16[1,3,8,32,1024]{4,3,2,1,0:T(8,128)(2,1)S(1)}, bf16[1,3,8,32,1024]{4,3,2,1,0:T(8,128)(2,1)}, u32[]{:S(2)}) copy-start(bf16[1,3,8,32,1024]{4,3,2,1,0:T(8,128)(2,1)} %x_ref.5) | copy-start | bytes 4718596
  4.8 15.6 %copy-start.3 = (f32[1,8,32,256]{3,2,1,0:T(8,128)S(1)}, f32[1,8,32,256]{3,2,1,0:T(8,128)}, u32[]{:S(2)}) copy-start(f32[1,8,32,256]{3,2,1,0:T(8,128)} %c_ref.5) | copy-start | bytes 786436
  4.8 15.6 %copy-start.5 = (bf16[1,8,32,256]{3,2,1,0:T(8,128)(2,1)S(1)}, bf16[1,8,32,256]{3,2,1,0:T(8,128)(2,1)}, u32[]{:S(2)}) copy-start(bf16[1,8,32,256]{3,2,1,0:T(8,128)(2,1)} %h_ref.5) | copy-start | bytes 393220
  4.8 15.6 %copy-start.6 = (bf16[1,3,8,32,256]{4,3,2,1,0:T(8,128)(2,1)S(1)}, bf16[1,3,8,32,256]{4,3,2,1,0:T(8,128)(2,1)}, u32[]{:S(2)}) copy-start(bf16[1,3,8,32,256]{4,3,2,1,0:T(8,128)(2,1)} %t0_ref.1) | copy-start | bytes 1179652
  4.9 3.1 %collective-permute-start = (bf16[18,32,256]{2,1,0:T(8,128)(2,1)S(1)}, bf16[18,32,256]{2,1,0:T(8,128)(2,1)S(1)}, u32[]{:S(2)}, u32[]{:S(2)}) collective-permute-start(bf16[18,32,256]{2,1,0:T(8,128)(2,1)S(1)} %get-tuple-element.32), channel_id=1, source_target_pairs={{0,4},{4,0},{8,12},{12,8},{16,20},{20,16},{24,28},{28,24},{1,5},{5... | collective-permute-start | bytes 884744 | tf_op jit(solution)/shard_map/ppermute | solution.py:540
  5.0 7.4 %collective-permute-start.1 = (bf16[18,32,256]{2,1,0:T(8,128)(2,1)S(1)}, bf16[18,32,256]{2,1,0:T(8,128)(2,1)S(1)}, u32[]{:S(2)}, u32[]{:S(2)}) collective-permute-start(bf16[18,32,256]{2,1,0:T(8,128)(2,1)S(1)} %get-tuple-element.33), channel_id=1, source_target_pairs={{4,8},{8,4},{12,16},{16,12},{20,24},{24,20},{28,0},{0,28},{5,9},{9... | collective-permute-start | bytes 884744 | tf_op jit(solution)/shard_map/ppermute | solution.py:540
  12.6 4.9 %collective-permute-start.2 = (bf16[224,256]{1,0:T(8,128)(2,1)S(1)}, bf16[224,256]{1,0:T(8,128)(2,1)S(1)}, u32[]{:S(2)}, u32[]{:S(2)}) collective-permute-start(bf16[224,256]{1,0:T(8,128)(2,1)S(1)} %get-tuple-element.34), channel_id=1, source_target_pairs={{0,1},{1,0},{2,3},{3,2},{4,5},{5,4},{6,7},{7,6},{8,9},{9,8},{10,11... | collective-permute-start | bytes 344072 | tf_op jit(solution)/shard_map/ppermute | solution.py:544
  14.4 6.0 %collective-permute-start.3 = (bf16[224,256]{1,0:T(8,128)(2,1)S(1)}, bf16[224,256]{1,0:T(8,128)(2,1)S(1)}, u32[]{:S(2)}, u32[]{:S(2)}) collective-permute-start(bf16[224,256]{1,0:T(8,128)(2,1)S(1)} %get-tuple-element.35), channel_id=1, source_target_pairs={{1,2},{2,1},{3,0},{0,3},{5,6},{6,5},{7,4},{4,7},{9,10},{10,9},{11,... | collective-permute-start | bytes 344072 | tf_op jit(solution)/shard_map/ppermute | solution.py:544
  20.4 2.3 %copy-start.7 = (bf16[2304,1024]{1,0:T(8,128)(2,1)S(1)}, bf16[2304,1024]{1,0:T(8,128)(2,1)}, u32[]{:S(2)}) copy-start(bf16[2304,1024]{1,0:T(8,128)(2,1)} %w_ref.5) | copy-start | bytes 14155780
  22.8 23.5 %copy-start.8 = (bf16[2304,1024]{1,0:T(8,128)(2,1)S(1)}, bf16[2304,1024]{1,0:T(8,128)(2,1)}, u32[]{:S(2)}) copy-start(bf16[2304,1024]{1,0:T(8,128)(2,1)} %w_ref.5) | copy-start | bytes 14155780
  34.8 2.5 %collective-permute-start.4 = (bf16[9,32,256]{2,1,0:T(8,128)(2,1)S(1)}, bf16[9,32,256]{2,1,0:T(8,128)(2,1)S(1)}, u32[]{:S(2)}, u32[]{:S(2)}) collective-permute-start(bf16[9,32,256]{2,1,0:T(8,128)(2,1)S(1)} %get-tuple-element.42), channel_id=1, source_target_pairs={{0,4},{4,0},{8,12},{12,8},{16,20},{20,16},{24,28},{28,24},{1,5},{5... | collective-permute-start | bytes 442376 | tf_op jit(solution)/shard_map/ppermute | solution.py:540
  34.8 5.8 %collective-permute-start.5 = (bf16[9,32,256]{2,1,0:T(8,128)(2,1)S(1)}, bf16[9,32,256]{2,1,0:T(8,128)(2,1)S(1)}, u32[]{:S(2)}, u32[]{:S(2)}) collective-permute-start(bf16[9,32,256]{2,1,0:T(8,128)(2,1)S(1)} %get-tuple-element.43), channel_id=1, source_target_pairs={{4,8},{8,4},{12,16},{16,12},{20,24},{24,20},{28,0},{0,28},{5,9},{9... | collective-permute-start | bytes 442376 | tf_op jit(solution)/shard_map/ppermute | solution.py:540
  40.7 4.3 %collective-permute-start.6 = (bf16[112,256]{1,0:T(8,128)(2,1)S(1)}, bf16[112,256]{1,0:T(8,128)(2,1)S(1)}, u32[]{:S(2)}, u32[]{:S(2)}) collective-permute-start(bf16[112,256]{1,0:T(8,128)(2,1)S(1)} %get-tuple-element.44), channel_id=1, source_target_pairs={{0,1},{1,0},{2,3},{3,2},{4,5},{5,4},{6,7},{7,6},{8,9},{9,8},{10,11... | collective-permute-start | bytes 172040 | tf_op jit(solution)/shard_map/ppermute | solution.py:544
  40.8 5.5 %collective-permute-start.7 = (bf16[112,256]{1,0:T(8,128)(2,1)S(1)}, bf16[112,256]{1,0:T(8,128)(2,1)S(1)}, u32[]{:S(2)}, u32[]{:S(2)}) collective-permute-start(bf16[112,256]{1,0:T(8,128)(2,1)S(1)} %get-tuple-element.45), channel_id=1, source_target_pairs={{1,2},{2,1},{3,0},{0,3},{5,6},{6,5},{7,4},{4,7},{9,10},{10,9},{11,... | collective-permute-start | bytes 172040 | tf_op jit(solution)/shard_map/ppermute | solution.py:544
  57.2 8.6 %collective-permute-start.8 = (bf16[512,2304]{1,0:T(8,128)(2,1)S(1)}, bf16[512,2304]{1,0:T(8,128)(2,1)S(1)}, u32[]{:S(2)}, u32[]{:S(2)}) collective-permute-start(bf16[512,2304]{1,0:T(8,128)(2,1)S(1)} %get-tuple-element.50), channel_id=1, source_target_pairs={{0,4},{4,0},{1,5},{5,1},{2,6},{6,2},{3,7},{7,3},{8,12},{12,8},{9,1... | collective-permute-start | bytes 7077896 | tf_op jit(solution)/shard_map/ppermute | solution.py:636
  57.3 4.6 %collective-permute-start.9 = (bf16[4,32,256]{2,1,0:T(8,128)(2,1)S(1)}, bf16[4,32,256]{2,1,0:T(8,128)(2,1)S(1)}, u32[]{:S(2)}, u32[]{:S(2)}) collective-permute-start(bf16[4,32,256]{2,1,0:T(8,128)(2,1)S(1)} %get-tuple-element.51), channel_id=1, source_target_pairs={{0,4},{4,0},{8,12},{12,8},{16,20},{20,16},{24,28},{28,24},{1,5},{5... | collective-permute-start | bytes 196616 | tf_op jit(solution)/shard_map/ppermute | solution.py:540
  57.8 4.9 %collective-permute-start.10 = (bf16[4,32,256]{2,1,0:T(8,128)(2,1)S(1)}, bf16[4,32,256]{2,1,0:T(8,128)(2,1)S(1)}, u32[]{:S(2)}, u32[]{:S(2)}) collective-permute-start(bf16[4,32,256]{2,1,0:T(8,128)(2,1)S(1)} %get-tuple-element.52), channel_id=1, source_target_pairs={{4,8},{8,4},{12,16},{16,12},{20,24},{24,20},{28,0},{0,28},{5,9},{9... | collective-permute-start | bytes 196616 | tf_op jit(solution)/shard_map/ppermute | solution.py:540
  62.8 6.8 %collective-permute-start.11 = (bf16[48,256]{1,0:T(8,128)(2,1)S(1)}, bf16[48,256]{1,0:T(8,128)(2,1)S(1)}, u32[]{:S(2)}, u32[]{:S(2)}) collective-permute-start(bf16[48,256]{1,0:T(8,128)(2,1)S(1)} %get-tuple-element.53), channel_id=1, source_target_pairs={{0,1},{1,0},{2,3},{3,2},{4,5},{5,4},{6,7},{7,6},{8,9},{9,8},{10,11... | collective-permute-start | bytes 73736 | tf_op jit(solution)/shard_map/ppermute | solution.py:544
  63.6 6.0 %collective-permute-start.12 = (bf16[48,256]{1,0:T(8,128)(2,1)S(1)}, bf16[48,256]{1,0:T(8,128)(2,1)S(1)}, u32[]{:S(2)}, u32[]{:S(2)}) collective-permute-start(bf16[48,256]{1,0:T(8,128)(2,1)S(1)} %get-tuple-element.54), channel_id=1, source_target_pairs={{1,2},{2,1},{3,0},{0,3},{5,6},{6,5},{7,4},{4,7},{9,10},{10,9},{11,... | collective-permute-start | bytes 73736 | tf_op jit(solution)/shard_map/ppermute | solution.py:544
  69.6 40.3 %all-to-all-start = ((bf16[64,8,2304]{2,1,0:T(8,128)(2,1)}), bf16[64,8,2304]{2,1,0:T(8,128)(2,1)}, u32[]{:S(2)}, u32[]{:S(2)}) async-start(bf16[64,8,2304]{2,1,0:T(8,128)(2,1)} %bitcast.1), calls=%async_computation | async-start | bytes 4718592 | tf_op jit(solution)/shard_map/all_to_all | solution.py:658
  78.6 2.3 %copy-start.9 = (bf16[2304,1024]{1,0:T(8,128)(2,1)S(1)}, bf16[2304,1024]{1,0:T(8,128)(2,1)}, u32[]{:S(2)}) copy-start(bf16[2304,1024]{1,0:T(8,128)(2,1)} %w_ref.5) | copy-start | bytes 14155780

commit v3 on v2

--- a/solution.py
+++ b/solution.py
@@ -13,6 +13,9 @@
     return [edge for a, b in pairs for edge in ((a, b), (b, a))]
 
 
+CORES = [(0, 1), (1, 0)]
+AXES = ("dp", "x", "core", "sx")
+HALF = 1152
 BF = jnp.bfloat16
 F32 = jnp.float32
 R, L, C = 8, 32, 256
@@ -227,36 +230,73 @@
     lax.fori_loop(0, R, one, 0)
 
 
-def theirs_kernel(g0_ref, g1_ref, g2_ref, p_ref, mine_ref, out_ref, turned, theirs):
-    other = 1 - lax.axis_index("core")
-    for frame, g_ref in enumerate((g0_ref, g1_ref, g2_ref)):
+def set_member(core, place, half, j):
+    near = jnp.where((place == 1) | (place == 2), 1, 0)
+    kind = jnp.where(core == 0, near, place // 2)
+    kind = jnp.where(half == 1, 1 - kind, kind)
+    return jnp.where(core == 0, kind + j * (3 - 2 * kind), 2 * kind + j)
+
+
+def turn(grads, turned, mine_ref, theirs_ref):
+    core = lax.axis_index("core")
+    for frame, g_ref in enumerate(grads):
         flat = g_ref[...].reshape(R * L, 4 * C).astype(F32)
         turned[:, quarter(frame)] = jnp.transpose(flat).astype(BF)
 
+    place = {axis: lax.axis_index(axis) for axis in ("dp", "x")}
+
     def pick(block, carry):
         at = pl.ds(pl.multiple_of(block * 32, 32), 32)
-        theirs[at, :] = turned[pl.ds(pl.multiple_of(block * 64 + other * 32, 32), 32), :]
-        mine_ref[at, :] = turned[pl.ds(pl.multiple_of(block * 64 + 32 - other * 32, 32), 32), :]
+        outer, inner = block // 4, block % 4
+        for who, out in ((core, mine_ref), (1 - core, theirs_ref)):
+            d = set_member(who, place["dp"], outer // 2, outer % 2)
+            x = set_member(who, place["x"], inner // 2, inner % 2)
+            out[at, :] = turned[pl.ds(pl.multiple_of(((d * 4 + x) * 2 + who) * 32, 32), 32), :]
         return carry
 
     lax.fori_loop(0, 16, pick, 0)
 
+
+def own_sum_kernel(mine_ref, p_ref, out_ref):
     def one(n, carry):
         at = pl.ds(pl.multiple_of(n * 3 * C, C), 3 * C)
-        out_ref[:, at] = jnp.dot(theirs[...], p_ref[:, at], preferred_element_type=F32).astype(BF)
+        out_ref[:, at] = jnp.dot(mine_ref[...], p_ref[:, at], preferred_element_type=F32)
         return carry
 
     lax.fori_loop(0, 3, one, 0)
 
 
-def mine_kernel(mine_ref, p_ref, got_ref, out_ref):
-    def one(n, carry):
-        at = pl.ds(pl.multiple_of(n * 3 * C, C), 3 * C)
-        total = jnp.dot(mine_ref[...], p_ref[:, at], preferred_element_type=F32)
-        out_ref[:, at] = (total + got_ref[:, at].astype(F32)).astype(BF)
+def parted(rows, total, keep, send):
+    for block in range(keep.shape[0] // rows):
+        src = block * 2 * rows
+        keep[block * rows : (block + 1) * rows, :] = total[src : src + rows].astype(BF)
+        send[block * rows : (block + 1) * rows, :] = total[src + rows : src + 2 * rows].astype(BF)
+
+
+def chip_sum_kernel(got_ref, p_ref, own_ref, keep0, send0, keep1, send1):
+    for color, (rows, keep, send) in enumerate(((256, keep0, send0), (64, keep1, send1))):
+        at = slice(color * HALF, (color + 1) * HALF)
+        total = own_ref[:, at] + jnp.dot(got_ref[...], p_ref[:, at], preferred_element_type=F32)
+        parted(rows, total, keep, send)
+
+
+def halve_kernel(kept0, came0, kept1, came1, keep0, send0, keep1, send1):
+    parted(64, kept0[...].astype(F32) + came0[...].astype(F32), keep0, send0)
+    parted(128, kept1[...].astype(F32) + came1[...].astype(F32), keep1, send1)
+
+
+def quarter_kernel(kept0, came0, kept1, came1, out_ref):
+    out_ref[:, 0:HALF] = (kept0[...].astype(F32) + came0[...].astype(F32)).astype(BF)
+    out_ref[:, HALF:] = (kept1[...].astype(F32) + came1[...].astype(F32)).astype(BF)
+
+
+def total_kernel(parts_ref, out_ref):
+    def one(i, carry):
+        out_ref[...] = out_ref[...] + parts_ref[i].astype(F32)
         return carry
 
-    lax.fori_loop(0, 3, one, 0)
+    out_ref[...] = jnp.zeros_like(out_ref)
+    lax.fori_loop(0, 16, one, 0)
 
 
 def inside(by, row):
@@ -446,7 +486,7 @@
 
 
 def backward_kernel(count_ref, t0_ref, w_ref, m1_ref, m0_ref, t1_ref, g2_ref, q_ref, near_r, far_r, near_c, far_c,
-                    g1_ref, g0_ref, dh_ref, dc_ref, near_out, far_out, above, below, left, right, gw, qs, z):
+                    g1_ref, g0_ref, dh_ref, dc_ref, near_out, far_out, mine_ref, theirs_ref, above, below, left, right, gw, qs, z, turned):
     row_odd, col_odd = parities()
     count = count_ref[0]
     arranged(row_odd, near_r, far_r, above, below)
@@ -510,6 +550,7 @@
     for part in range(4):
         near_out[part] = g0_ref[first_row, :, quarter(part)]
         far_out[part] = g0_ref[last_row, :, quarter(part)]
+    turn((g0_ref, g1_ref, g2_ref), turned, mine_ref, theirs_ref)
 
 
 def whole(shape):
@@ -542,6 +583,22 @@
 
 def swap_cols(near, far):
     return lax.ppermute(near, "sx", ring_pairs(4, 0)), lax.ppermute(far, "sx", ring_pairs(4, 1))
+
+
+def first_partner(value, axis):
+    flips = (1, 3)
+    pairs = [(i * 2 + c, (i ^ flips[c]) * 2 + c) for i in range(4) for c in range(2)]
+    return lax.ppermute(value, (axis, "core"), pairs)
+
+
+def owner_groups():
+    sets = (((0, 3), (1, 2)), ((0, 1), (2, 3)))
+    return [
+        [((d * 4 + x) * 2 + core) * 4 + y for d in ds for x in xs for y in range(4)]
+        for core in range(2)
+        for ds in sets[core]
+        for xs in sets[core]
+    ]
 
 
 def body(input_gates, recur_weight, hidden_init, cell_init, hidden_cot, frame_count):
@@ -598,6 +655,8 @@
         flops=6 * 10**9,
     )
     near_r, far_r = swap_rows(near, far)
+    flat_patches = patches.reshape(3 * R * L, 9 * C)
+    other_patches = lax.ppermute(flat_patches, "core", CORES)
     strip = out((col_units_b, C), BF)
     near, far = call(
         cols_b_kernel,
@@ -607,14 +666,14 @@
         name="cols_b",
     )
     near_c, far_c = swap_cols(near, far)
-    g1, g0, _, cell_grad, near_c_rows, far_c_rows = call(
+    g1, g0, _, cell_grad, near_c_rows, far_c_rows, mine, theirs = call(
         backward_kernel,
         (frame_count, hidden_cot, recur_weight, m1, m0, t1, g2, q, near_r, far_r, near_c, far_c),
         [out((R, L, 4 * C), BF), out((R, L, 4 * C), BF), out((1, R, L, C), F32), out((1, R, L, C), F32),
-         out((4, L, C), BF), out((4, L, C), BF)],
+         out((4, L, C), BF), out((4, L, C), BF), out((512, 3 * C), BF), out((512, 3 * C), BF)],
         [vmem((row_units_b, L, C), BF)] * 2
         + [vmem((col_units_b, C), F32)] * 2
-        + [vmem(((R + 4) * W, 4 * C), BF), vmem((R + 2, W, C), F32), vmem((3, R + 2, 64, C), F32)],
+        + [vmem(((R + 4) * W, 4 * C), BF), vmem((R + 2, W, C), F32), vmem((3, R + 2, 64, C), F32), vmem((4 * C, 3 * C), BF)],
         {1: (1, 1, R, L, C)},
         scalar=True,
         name="backward",
@@ -623,18 +682,17 @@
     )
     _, col_units_c = col_offsets(ROWS_C)
     near_r, far_r = swap_rows(near_c_rows, far_c_rows)
-    flat_patches = patches.reshape(3 * R * L, 9 * C)
-    half = out((512, 9 * C), BF)
-    mine, theirs = call(
-        theirs_kernel,
-        (g0, g1, g2, flat_patches),
-        [out((512, 3 * C), BF), half],
-        [vmem((4 * C, 3 * C), BF), vmem((512, 3 * C), BF)],
-        name="theirs",
+    got = lax.ppermute(theirs, "core", CORES)
+    (own_sum,) = call(own_sum_kernel, (mine, flat_patches), [out((512, 9 * C), F32)], [], name="own_sum", flops=2 * 10**9)
+    got, near_r, far_r = lax.optimization_barrier((got, near_r, far_r))
+    sent = call(
+        chip_sum_kernel,
+        (got, other_patches, own_sum),
+        [out((256, HALF), BF)] * 4,
+        [],
+        name="chip_sum",
         flops=2 * 10**9,
     )
-    got = lax.ppermute(theirs, "core", [(0, 1), (1, 0)])
-    (chip_sum,) = call(mine_kernel, (mine, flat_patches, got), [half], [], name="mine", flops=2 * 10**9)
     strip = out((col_units_c, C), BF)
     near, far = call(
         cols_c_kernel,
@@ -644,7 +702,10 @@
         name="cols_c",
     )
     near_c, far_c = swap_cols(near, far)
-    chip_sum, near_c, far_c = lax.optimization_barrier((chip_sum, near_c, far_c))
+    came = first_partner(sent[1], "dp"), first_partner(sent[3], "x")
+    *came, near_c, far_c = lax.optimization_barrier((*came, near_c, far_c))
+    sent = call(halve_kernel, (sent[0], came[0], sent[2], came[1]), [out((128, HALF), BF)] * 4, [], name="halve")
+    came = first_partner(sent[1], "x"), first_partner(sent[3], "dp")
     (hidden_grad,) = call(
         last_kernel,
         (g0, recur_weight, near_r, far_r, near_c, far_c),
@@ -655,8 +716,13 @@
         name="last",
         flops=2 * 10**9,
     )
-    parts = lax.all_to_all(chip_sum, ("dp", "x", "sx"), 0, 0, tiled=True)
-    weight_grad = jnp.sum(parts.reshape(64, 8, 9 * width).astype(jnp.float32), axis=0).T
+    *came, hidden_grad = lax.optimization_barrier((*came, hidden_grad))
+    (blocks,) = call(
+        quarter_kernel, (sent[0], came[0], sent[2], came[1]), [out((128, 9 * C), BF)], [], name="quarter"
+    )
+    parts = lax.all_to_all(blocks, AXES, 0, 0, tiled=True, axis_index_groups=owner_groups())
+    (total,) = call(total_kernel, (parts.reshape(16, 8, 9 * C),), [out((8, 9 * C), F32)], [], name="total")
+    weight_grad = total.T
     gate_grad = jnp.stack([g0, g1, g2])[None]
     return (hidden_seq, weight_grad, gate_grad, hidden_grad, cell_grad)
 

time: 113 us -> 104 us (0.920)
  waiting for transfers between devices: 43.7 us -> 36.4 us
  other arithmetic: 3.96 us -> 1.31 us
  local copies, waits for them, and re-layouts: 8.86 us -> 6.53 us
  starting transfers between devices: 24.5 us -> 26.8 us
    all_to_all x1, waiting for transfers between devices: 26.1 us -> 11.2 us  [body(): lax.all_to_all(blocks, AXES, 0, 0, tiled=True, axis_index_groups=owner_gr...]
    ppermute x1 -> x6, waiting for transfers between devices: 0.01 us -> 7.68 us  [the longest x4 7.67 us: first_partner(): return lax.ppermute(value, (axis, 'core'), pairs)]
    ppermute x3, waiting for transfers between devices: 8.53 us -> 4.5 us  [swap_rows(): lax.ppermute(far, axis, ring_pairs(8, 1))]
    reduce_sum x1 -> x0, other arithmetic: 2.64 us -> none  [body(): jnp.sum(parts.reshape(64, 8, 9 * width).astype(jnp.float32), axis=0)]
    unnamed x20 -> x18, local copies, waits for them, and re-layouts: 7.94 us -> 5.62 us
    ppermute x1 -> x6, starting transfers between devices: 0.09 us -> 2.28 us  [the longest x4 2.27 us: first_partner(): return lax.ppermute(value, (axis, 'core'), pairs)]
    ppermute x3, waiting for transfers between devices: 4.2 us -> 6.12 us  [swap_cols(): lax.ppermute(far, 'sx', ring_pairs(4, 1))]
    pallas_call x9 -> x12, Pallas kernels: 30.1 us -> 31.2 us  [call(): pl.pallas_call(kernel, grid=(1,), in_specs=specs, out_specs=[whole(out.sh...]
  transfers between devices with their start and end apart: 14 -> 19, of which waited for: 9 -> 13; matrix products, arithmetic and copies ran while one was open for 1% -> 1% of each run, Pallas kernels for 6% -> 14%
where the time goes in v3:
time: 104 us
  waiting for transfers between devices  36.4 us (35%)
  Pallas kernels  31.2 us (30%)
  starting transfers between devices  26.8 us (26%)
  local copies, waits for them, and re-layouts  6.53 us (6%)
  between operations  1.44 us (1%)
  other arithmetic  1.31 us (1%)
    pallas_call x12, Pallas kernels, call(): pl.pallas_call(kernel, grid=(1,), in_specs=specs, out_specs=[whole(out.sh...  31.2 us
    all_to_all x1, waiting for transfers between devices, body(): lax.all_to_all(blocks, AXES, 0, 0, tiled=True, axis_index_groups=owner_gr...  11.2 us
    ppermute x4, waiting for transfers between devices, first_partner(): return lax.ppermute(value, (axis, 'core'), pairs)  7.67 us
    ppermute x3, starting transfers between devices, swap_rows(): lax.ppermute(far, axis, ring_pairs(8, 1))  7.66 us
    all_to_all x1, starting transfers between devices, body(): lax.all_to_all(blocks, AXES, 0, 0, tiled=True, axis_index_groups=owner_gr...  7.04 us
    ppermute x3, starting transfers between devices, swap_cols(): lax.ppermute(far, 'sx', ring_pairs(4, 1))  6.61 us
    ppermute x3, waiting for transfers between devices, swap_cols(): lax.ppermute(far, 'sx', ring_pairs(4, 1))  6.12 us
    unnamed x18, local copies, waits for them, and re-layouts  5.62 us
  transfers between devices with their start and end apart: 19, of which 13 were waited for; matrix products, arithmetic and copies ran while one was open for 1% of the time, Pallas kernels for 14%

profile of v3, /device:TPU:0, one launch (start us, length us, event | category | flops | bytes accessed | tf_op | source)
XLA Modules:
  0.0 103.7 jit_solution(14819420422241545665)
XLA Ops:
  0.6 0.9 slice.3.t_ref
  1.6 1.4 %copy-done = bf16[1,3,8,32,1024]{4,3,2,1,0:T(8,128)(2,1)S(1)} copy-done((bf16[1,3,8,32,1024]{4,3,2,1,0:T(8,128)(2,1)S(1)}, bf16[1,3,8,32,1024]{4,3,2,1,0:T(8,128)(2,1)}, u32[]{:S(2)}) %copy-start) | copy-done | bytes 1572888
  3.0 0.9 copy-done.2
  3.9 0.9 copy-done.4
  5.0 3.0 %collective-permute-start.1 = (bf16[18,32,256]{2,1,0:T(8,128)(2,1)S(1)}, bf16[18,32,256]{2,1,0:T(8,128)(2,1)S(1)}, u32[]{:S(2)}, u32[]{:S(2)}) collective-permute-start(bf16[18,32,256]{2,1,0:T(8,128)(2,1)S(1)} %get-tuple-element.48), channel_id=1, source_target_pairs={{4,8},{8,4},{12,16},{16,12},{20,24},{24,20},{28,0},{0,28},{5,9},{9... | collective-permute-start | bytes 884744 | tf_op jit(solution)/shard_map/ppermute | solution.py:581
  8.0 4.5 %collective-permute-done.1.far_r = bf16[18,32,256]{2,1,0:T(8,128)(2,1)S(1)} collective-permute-done((bf16[18,32,256]{2,1,0:T(8,128)(2,1)S(1)}, bf16[18,32,256]{2,1,0:T(8,128)(2,1)S(1)}, u32[]{:S(2)}, u32[]{:S(2)}) %collective-permute-start.1) | collective-permute-done | bytes 294944 | tf_op jit(solution)/shard_map/ppermute | solution.py:581
  12.7 1.8 %collective-permute-start.2 = (bf16[224,256]{1,0:T(8,128)(2,1)S(1)}, bf16[224,256]{1,0:T(8,128)(2,1)S(1)}, u32[]{:S(2)}, u32[]{:S(2)}) collective-permute-start(bf16[224,256]{1,0:T(8,128)(2,1)S(1)} %get-tuple-element.49), channel_id=1, source_target_pairs={{0,1},{1,0},{2,3},{3,2},{4,5},{5,4},{6,7},{7,6},{8,9},{9,8},{10,11... | collective-permute-start | bytes 344072 | tf_op jit(solution)/shard_map/ppermute | solution.py:585
  14.4 2.2 %collective-permute-start.3 = (bf16[224,256]{1,0:T(8,128)(2,1)S(1)}, bf16[224,256]{1,0:T(8,128)(2,1)S(1)}, u32[]{:S(2)}, u32[]{:S(2)}) collective-permute-start(bf16[224,256]{1,0:T(8,128)(2,1)S(1)} %get-tuple-element.50), channel_id=1, source_target_pairs={{1,2},{2,1},{3,0},{0,3},{5,6},{6,5},{7,4},{4,7},{9,10},{10,9},{11,... | collective-permute-start | bytes 344072 | tf_op jit(solution)/shard_map/ppermute | solution.py:585
  17.5 2.9 %collective-permute-done.3.far_c = bf16[224,256]{1,0:T(8,128)(2,1)S(1)} collective-permute-done((bf16[224,256]{1,0:T(8,128)(2,1)S(1)}, bf16[224,256]{1,0:T(8,128)(2,1)S(1)}, u32[]{:S(2)}, u32[]{:S(2)}) %collective-permute-start.3) | collective-permute-done | bytes 114720 | tf_op jit(solution)/shard_map/ppermute | solution.py:585
  20.5 2.3 %copy-done.7 = bf16[2304,1024]{1,0:T(8,128)(2,1)S(1)} copy-done((bf16[2304,1024]{1,0:T(8,128)(2,1)S(1)}, bf16[2304,1024]{1,0:T(8,128)(2,1)}, u32[]{:S(2)}) %copy-start.7) | copy-done | bytes 4718616
  22.8 12.0 %forward.1 = (bf16[1,3,8,32,256]{4,3,2,1,0:T(8,128)(2,1)}, bf16[3,256,2304]{2,1,0:T(8,128)(2,1)S(1)}, bf16[6,10,48,256]{3,2,1,0:T(8,128)(2,1)S(1)}, bf16[6,8,32,...) custom-call(s32[1]{0:T(128)S(6)} %copy.11.count_ref, ...), custom_call_target="tpu_custom_call" | custom-call | flops 6000000000 | bytes 7897092 | tf_op jit(solution)/shard_map/forward/pallas_call | solution.py:566
  35.3 2.2 %collective-permute-start.5 = (bf16[9,32,256]{2,1,0:T(8,128)(2,1)S(1)}, bf16[9,32,256]{2,1,0:T(8,128)(2,1)S(1)}, u32[]{:S(2)}, u32[]{:S(2)}) collective-permute-start(bf16[9,32,256]{2,1,0:T(8,128)(2,1)S(1)} %get-tuple-element.58), channel_id=1, source_target_pairs={{4,8},{8,4},{12,16},{16,12},{20,24},{24,20},{28,0},{0,28},{5,9},{9... | collective-permute-start | bytes 442376 | tf_op jit(solution)/shard_map/ppermute | solution.py:581
  37.5 3.7 %collective-permute-done.4.near_r = bf16[9,32,256]{2,1,0:T(8,128)(2,1)S(1)} collective-permute-done((bf16[9,32,256]{2,1,0:T(8,128)(2,1)S(1)}, bf16[9,32,256]{2,1,0:T(8,128)(2,1)S(1)}, u32[]{:S(2)}, u32[]{:S(2)}) %collective-permute-start.4) | collective-permute-done | bytes 147488 | tf_op jit(solution)/shard_map/ppermute | solution.py:581
  41.5 2.2 %collective-permute-start.7 = (bf16[112,256]{1,0:T(8,128)(2,1)S(1)}, bf16[112,256]{1,0:T(8,128)(2,1)S(1)}, u32[]{:S(2)}, u32[]{:S(2)}) collective-permute-start(bf16[112,256]{1,0:T(8,128)(2,1)S(1)} %get-tuple-element.60), channel_id=1, source_target_pairs={{1,2},{2,1},{3,0},{0,3},{5,6},{6,5},{7,4},{4,7},{9,10},{10,9},{11,... | collective-permute-start | bytes 172040 | tf_op jit(solution)/shard_map/ppermute | solution.py:585
  43.7 1.9 %collective-permute-done.6.near_c = bf16[112,256]{1,0:T(8,128)(2,1)S(1)} collective-permute-done((bf16[112,256]{1,0:T(8,128)(2,1)S(1)}, bf16[112,256]{1,0:T(8,128)(2,1)S(1)}, u32[]{:S(2)}, u32[]{:S(2)}) %collective-permute-start.6) | collective-permute-done | bytes 57376 | tf_op jit(solution)/shard_map/ppermute | solution.py:585
  45.6 1.3 %collective-permute-done.7.far_c = bf16[112,256]{1,0:T(8,128)(2,1)S(1)} collective-permute-done((bf16[112,256]{1,0:T(8,128)(2,1)S(1)}, bf16[112,256]{1,0:T(8,128)(2,1)S(1)}, u32[]{:S(2)}, u32[]{:S(2)}) %collective-permute-start.7) | collective-permute-done | bytes 57376 | tf_op jit(solution)/shard_map/ppermute | solution.py:585
  46.9 9.2 %backward.1 = (bf16[8,32,1024]{2,1,0:T(8,128)(2,1)S(1)}, bf16[8,32,1024]{2,1,0:T(8,128)(2,1)S(1)}, f32[1,8,32,256]{3,2,1,0:T(8,128)}, f32[1,8,32,256]{3,2,1,0:T(...) custom-call(s32[1]{0:T(128)S(6)} %copy.11.count_ref, ...), custom_call_target="tpu_custom_call" | custom-call | flops 4000000000 | bytes 8814596 | tf_op jit(solution)/shard_map/backward/pallas_call | solution.py:566
  56.1 2.5 %collective-permute-start.10 = (bf16[4,32,256]{2,1,0:T(8,128)(2,1)S(1)}, bf16[4,32,256]{2,1,0:T(8,128)(2,1)S(1)}, u32[]{:S(2)}, u32[]{:S(2)}) collective-permute-start(bf16[4,32,256]{2,1,0:T(8,128)(2,1)S(1)} %get-tuple-element.63), channel_id=1, source_target_pairs={{4,8},{8,4},{12,16},{16,12},{20,24},{24,20},{28,0},{0,28},{5,9},{9... | collective-permute-start | bytes 196616 | tf_op jit(solution)/shard_map/ppermute | solution.py:581
  58.6 2.4 %own_sum.1.own_ref = f32[512,2304]{1,0:T(8,128)S(1)} custom-call(bf16[512,768]{1,0:T(8,128)(2,1)S(1)} %get-tuple-element.66.mine_ref, bf16[768,2304]{1,0:T(8,128)(2,1)S(1)} %bitcast.9), custom_call_target="tpu_custom_call" | custom-call | flops 2000000000 | bytes 4325376 | tf_op jit(solution)/shard_map/own_sum/pallas_call | solution.py:566
  61.1 2.2 %chip_sum.1 = (bf16[256,1152]{1,0:T(8,128)(2,1)S(1)}, bf16[256,1152]{1,0:T(8,128)(2,1)S(1)}, bf16[256,1152]{1,0:T(8,128)(2,1)S(1)}, bf16[256,1152]{1,0:T(8,128)(2,1)S(1)}) custom-call(bf16[512,768]{1,0:T(8,128)(2,1)S(1)} %collective-permute-done.8.got_ref, bf16[768,2304]{1,0:T(8,128)(2,1)S(1)} %collective-permute-done.11.p_ref, f32[512,2304]{1,0:T(8,128)S(1)} %own_sum.1.own_ref), custom_call_target="tpu_custom_call" | custom-call | flops 2000000000 | bytes 9043968 | tf_op jit(solution)/shard_map/chip_sum/pallas_call | solution.py:566
  63.3 2.0 %collective-permute-start.12 = (bf16[256,1152]{1,0:T(8,128)(2,1)S(1)}, bf16[256,1152]{1,0:T(8,128)(2,1)S(1)}, u32[]{:S(2)}, u32[]{:S(2)}) collective-permute-start(bf16[256,1152]{1,0:T(8,128)(2,1)S(1)} %get-tuple-element.68), channel_id=1, source_target_pairs={{0,32},{4,100},{32,0},{36,68},{64,96},{68,36},{96,64},{100,4},{1,3... | collective-permute-start | bytes 1769480 | tf_op jit(solution)/shard_map/ppermute | solution.py:591
  66.1 2.2 %collective-permute-start.15 = (bf16[48,256]{1,0:T(8,128)(2,1)S(1)}, bf16[48,256]{1,0:T(8,128)(2,1)S(1)}, u32[]{:S(2)}, u32[]{:S(2)}) collective-permute-start(bf16[48,256]{1,0:T(8,128)(2,1)S(1)} %get-tuple-element.74), channel_id=1, source_target_pairs={{1,2},{2,1},{3,0},{0,3},{5,6},{6,5},{7,4},{4,7},{9,10},{10,9},{11,... | collective-permute-start | bytes 73736 | tf_op jit(solution)/shard_map/ppermute | solution.py:585
  68.3 0.9 collective-permute-done.14.near_c
  69.3 1.9 %collective-permute-done.15.far_c = bf16[48,256]{1,0:T(8,128)(2,1)S(1)} collective-permute-done((bf16[48,256]{1,0:T(8,128)(2,1)S(1)}, bf16[48,256]{1,0:T(8,128)(2,1)S(1)}, u32[]{:S(2)}, u32[]{:S(2)}) %collective-permute-start.15) | collective-permute-done | bytes 24608 | tf_op jit(solution)/shard_map/ppermute | solution.py:585
  71.2 2.0 %collective-permute-done.12.came0 = bf16[256,1152]{1,0:T(8,128)(2,1)S(1)} collective-permute-done((bf16[256,1152]{1,0:T(8,128)(2,1)S(1)}, bf16[256,1152]{1,0:T(8,128)(2,1)S(1)}, u32[]{:S(2)}, u32[]{:S(2)}) %collective-permute-start.12) | collective-permute-done | bytes 589856 | tf_op jit(solution)/shard_map/ppermute | solution.py:591
  73.2 1.9 %collective-permute-done.13.came1 = bf16[256,1152]{1,0:T(8,128)(2,1)S(1)} collective-permute-done((bf16[256,1152]{1,0:T(8,128)(2,1)S(1)}, bf16[256,1152]{1,0:T(8,128)(2,1)S(1)}, u32[]{:S(2)}, u32[]{:S(2)}) %collective-permute-start.13) | collective-permute-done | bytes 589856 | tf_op jit(solution)/shard_map/ppermute | solution.py:591
  75.7 2.9 %last.1 = bf16[1,8,32,256]{3,2,1,0:T(8,128)(2,1)} custom-call(bf16[8,32,1024]{2,1,0:T(8,128)(2,1)S(1)} %get-tuple-element.70.g_ref, bf16[2304,1024]{1,0:T(8,128)(2,1)S(1)} %copy-done.8, bf16[4,32,256]{2,1,0:T(8,128)(2,1)S(1)} %collective-permute-done.9.near_r, bf16[4,32,256]{2,1,0:T(8,128)(2,1)S(1)} %collective-permute-done.10.far_r, ...), custom_call_target="tpu_custom_call" | custom-call | flops 2000000000 | bytes 5423104 | tf_op jit(solution)/shard_map/last/pallas_call | solution.py:566
  78.6 3.6 %collective-permute-done.16.came0 = bf16[128,1152]{1,0:T(8,128)(2,1)S(1)} collective-permute-done((bf16[128,1152]{1,0:T(8,128)(2,1)S(1)}, bf16[128,1152]{1,0:T(8,128)(2,1)S(1)}, u32[]{:S(2)}, u32[]{:S(2)}) %collective-permute-start.16) | collective-permute-done | bytes 294944 | tf_op jit(solution)/shard_map/ppermute | solution.py:591
  82.3 1.0 quarter.1
  83.3 7.0 %all-to-all-start = ((bf16[16,8,2304]{2,1,0:T(8,128)(2,1)}), bf16[16,8,2304]{2,1,0:T(8,128)(2,1)S(1)}, u32[]{:S(2)}, u32[]{:S(2)}) async-start(bf16[16,8,2304]{2,1,0:T(8,128)(2,1)} %bitcast.1), calls=%async_computation | async-start | bytes 1179648 | tf_op jit(solution)/shard_map/all_to_all | solution.py:723
  90.3 1.3 %maximum_bitcast_fusion = bf16[1,3,8,32,1024]{4,3,2,1,0:T(8,128)(2,1)} fusion(bf16[1,8,32,1024]{3,2,1,0:T(8,128)(2,1)S(1)} %bitcast.11, bf16[1,8,32,1024]{3,2,1,0:T(8,128)(2,1)S(1)} %bitcast.12, bf16[1,8,32,1024]{3,2,1,0:T(8,128)(2,1)S(1)} %bitcast.10), kind=kLoop, calls=%fused_computation | loop fusion | flops 1572864 | bytes 3145728 | tf_op jit(solution)/shard_map/broadcast_in_dim | solution.py:726
  91.6 11.2 %all-to-all-done.parts_ref = bf16[16,8,2304]{2,1,0:T(8,128)(2,1)S(1)} async-done(((bf16[16,8,2304]{2,1,0:T(8,128)(2,1)}), bf16[16,8,2304]{2,1,0:T(8,128)(2,1)S(1)}, u32[]{:S(2)}, u32[]{:S(2)}) %all-to-all-start) | async-done | bytes 589856 | tf_op jit(solution)/shard_map/all_to_all | solution.py:723
  (38 shorter events, 3.7 us)
Async XLA Ops:
  1.6 1.4 %copy-start = (bf16[1,3,8,32,1024]{4,3,2,1,0:T(8,128)(2,1)S(1)}, bf16[1,3,8,32,1024]{4,3,2,1,0:T(8,128)(2,1)}, u32[]{:S(2)}) copy-start(bf16[1,3,8,32,1024]{4,3,2,1,0:T(8,128)(2,1)} %x_ref.5) | copy-start | bytes 4718596
  3.0 0.9 copy-start.2
  3.9 0.9 copy-start.4
  4.9 15.6 %copy-start.1 = (bf16[1,3,8,32,1024]{4,3,2,1,0:T(8,128)(2,1)S(1)}, bf16[1,3,8,32,1024]{4,3,2,1,0:T(8,128)(2,1)}, u32[]{:S(2)}) copy-start(bf16[1,3,8,32,1024]{4,3,2,1,0:T(8,128)(2,1)} %x_ref.5) | copy-start | bytes 4718596
  4.9 15.6 %copy-start.3 = (f32[1,8,32,256]{3,2,1,0:T(8,128)S(1)}, f32[1,8,32,256]{3,2,1,0:T(8,128)}, u32[]{:S(2)}) copy-start(f32[1,8,32,256]{3,2,1,0:T(8,128)} %c_ref.5) | copy-start | bytes 786436
  4.9 15.6 %copy-start.5 = (bf16[1,8,32,256]{3,2,1,0:T(8,128)(2,1)S(1)}, bf16[1,8,32,256]{3,2,1,0:T(8,128)(2,1)}, u32[]{:S(2)}) copy-start(bf16[1,8,32,256]{3,2,1,0:T(8,128)(2,1)} %h_ref.5) | copy-start | bytes 393220
  4.9 15.5 %copy-start.6 = (bf16[1,3,8,32,256]{4,3,2,1,0:T(8,128)(2,1)S(1)}, bf16[1,3,8,32,256]{4,3,2,1,0:T(8,128)(2,1)}, u32[]{:S(2)}) copy-start(bf16[1,3,8,32,256]{4,3,2,1,0:T(8,128)(2,1)} %t0_ref.1) | copy-start | bytes 1179652
  4.9 3.1 %collective-permute-start = (bf16[18,32,256]{2,1,0:T(8,128)(2,1)S(1)}, bf16[18,32,256]{2,1,0:T(8,128)(2,1)S(1)}, u32[]{:S(2)}, u32[]{:S(2)}) collective-permute-start(bf16[18,32,256]{2,1,0:T(8,128)(2,1)S(1)} %get-tuple-element.47), channel_id=1, source_target_pairs={{0,4},{4,0},{8,12},{12,8},{16,20},{20,16},{24,28},{28,24},{1,5},{5... | collective-permute-start | bytes 884744 | tf_op jit(solution)/shard_map/ppermute | solution.py:581
  5.0 7.4 %collective-permute-start.1 = (bf16[18,32,256]{2,1,0:T(8,128)(2,1)S(1)}, bf16[18,32,256]{2,1,0:T(8,128)(2,1)S(1)}, u32[]{:S(2)}, u32[]{:S(2)}) collective-permute-start(bf16[18,32,256]{2,1,0:T(8,128)(2,1)S(1)} %get-tuple-element.48), channel_id=1, source_target_pairs={{4,8},{8,4},{12,16},{16,12},{20,24},{24,20},{28,0},{0,28},{5,9},{9... | collective-permute-start | bytes 884744 | tf_op jit(solution)/shard_map/ppermute | solution.py:581
  12.7 4.9 %collective-permute-start.2 = (bf16[224,256]{1,0:T(8,128)(2,1)S(1)}, bf16[224,256]{1,0:T(8,128)(2,1)S(1)}, u32[]{:S(2)}, u32[]{:S(2)}) collective-permute-start(bf16[224,256]{1,0:T(8,128)(2,1)S(1)} %get-tuple-element.49), channel_id=1, source_target_pairs={{0,1},{1,0},{2,3},{3,2},{4,5},{5,4},{6,7},{7,6},{8,9},{9,8},{10,11... | collective-permute-start | bytes 344072 | tf_op jit(solution)/shard_map/ppermute | solution.py:585
  14.4 6.0 %collective-permute-start.3 = (bf16[224,256]{1,0:T(8,128)(2,1)S(1)}, bf16[224,256]{1,0:T(8,128)(2,1)S(1)}, u32[]{:S(2)}, u32[]{:S(2)}) collective-permute-start(bf16[224,256]{1,0:T(8,128)(2,1)S(1)} %get-tuple-element.50), channel_id=1, source_target_pairs={{1,2},{2,1},{3,0},{0,3},{5,6},{6,5},{7,4},{4,7},{9,10},{10,9},{11,... | collective-permute-start | bytes 344072 | tf_op jit(solution)/shard_map/ppermute | solution.py:585
  20.4 2.3 %copy-start.7 = (bf16[2304,1024]{1,0:T(8,128)(2,1)S(1)}, bf16[2304,1024]{1,0:T(8,128)(2,1)}, u32[]{:S(2)}) copy-start(bf16[2304,1024]{1,0:T(8,128)(2,1)} %w_ref.5) | copy-start | bytes 14155780
  22.8 24.1 %copy-start.8 = (bf16[2304,1024]{1,0:T(8,128)(2,1)S(1)}, bf16[2304,1024]{1,0:T(8,128)(2,1)}, u32[]{:S(2)}) copy-start(bf16[2304,1024]{1,0:T(8,128)(2,1)} %w_ref.5) | copy-start | bytes 14155780
  34.8 26.2 %collective-permute-start.11 = (bf16[768,2304]{1,0:T(8,128)(2,1)S(1)}, bf16[768,2304]{1,0:T(8,128)(2,1)S(1)}, u32[]{:S(2)}, u32[]{:S(2)}) collective-permute-start(bf16[768,2304]{1,0:T(8,128)(2,1)S(1)} %bitcast.8), channel_id=1, source_target_pairs={{0,4},{4,0},{1,5},{5,1},{2,6},{6,2},{3,7},{7,3},{8,12},{12,8},{9,1... | collective-permute-start | bytes 10616840 | tf_op jit(solution)/shard_map/ppermute | solution.py:659
  34.8 6.4 %collective-permute-start.4 = (bf16[9,32,256]{2,1,0:T(8,128)(2,1)S(1)}, bf16[9,32,256]{2,1,0:T(8,128)(2,1)S(1)}, u32[]{:S(2)}, u32[]{:S(2)}) collective-permute-start(bf16[9,32,256]{2,1,0:T(8,128)(2,1)S(1)} %get-tuple-element.57), channel_id=1, source_target_pairs={{0,4},{4,0},{8,12},{12,8},{16,20},{20,16},{24,28},{28,24},{1,5},{5... | collective-permute-start | bytes 442376 | tf_op jit(solution)/shard_map/ppermute | solution.py:581
  35.3 5.9 %collective-permute-start.5 = (bf16[9,32,256]{2,1,0:T(8,128)(2,1)S(1)}, bf16[9,32,256]{2,1,0:T(8,128)(2,1)S(1)}, u32[]{:S(2)}, u32[]{:S(2)}) collective-permute-start(bf16[9,32,256]{2,1,0:T(8,128)(2,1)S(1)} %get-tuple-element.58), channel_id=1, source_target_pairs={{4,8},{8,4},{12,16},{16,12},{20,24},{24,20},{28,0},{0,28},{5,9},{9... | collective-permute-start | bytes 442376 | tf_op jit(solution)/shard_map/ppermute | solution.py:581
  41.4 4.3 %collective-permute-start.6 = (bf16[112,256]{1,0:T(8,128)(2,1)S(1)}, bf16[112,256]{1,0:T(8,128)(2,1)S(1)}, u32[]{:S(2)}, u32[]{:S(2)}) collective-permute-start(bf16[112,256]{1,0:T(8,128)(2,1)S(1)} %get-tuple-element.59), channel_id=1, source_target_pairs={{0,1},{1,0},{2,3},{3,2},{4,5},{5,4},{6,7},{7,6},{8,9},{9,8},{10,11... | collective-permute-start | bytes 172040 | tf_op jit(solution)/shard_map/ppermute | solution.py:585
  41.5 5.5 %collective-permute-start.7 = (bf16[112,256]{1,0:T(8,128)(2,1)S(1)}, bf16[112,256]{1,0:T(8,128)(2,1)S(1)}, u32[]{:S(2)}, u32[]{:S(2)}) collective-permute-start(bf16[112,256]{1,0:T(8,128)(2,1)S(1)} %get-tuple-element.60), channel_id=1, source_target_pairs={{1,2},{2,1},{3,0},{0,3},{5,6},{6,5},{7,4},{4,7},{9,10},{10,9},{11,... | collective-permute-start | bytes 172040 | tf_op jit(solution)/shard_map/ppermute | solution.py:585
  56.1 4.9 %collective-permute-start.8 = (bf16[512,768]{1,0:T(8,128)(2,1)S(1)}, bf16[512,768]{1,0:T(8,128)(2,1)S(1)}, u32[]{:S(2)}, u32[]{:S(2)}) collective-permute-start(bf16[512,768]{1,0:T(8,128)(2,1)S(1)} %get-tuple-element.61), channel_id=1, source_target_pairs={{0,4},{4,0},{1,5},{5,1},{2,6},{6,2},{3,7},{7,3},{8,12},{12,8},{9,1... | collective-permute-start | bytes 2359304 | tf_op jit(solution)/shard_map/ppermute | solution.py:685
  56.1 4.9 %collective-permute-start.10 = (bf16[4,32,256]{2,1,0:T(8,128)(2,1)S(1)}, bf16[4,32,256]{2,1,0:T(8,128)(2,1)S(1)}, u32[]{:S(2)}, u32[]{:S(2)}) collective-permute-start(bf16[4,32,256]{2,1,0:T(8,128)(2,1)S(1)} %get-tuple-element.63), channel_id=1, source_target_pairs={{4,8},{8,4},{12,16},{16,12},{20,24},{24,20},{28,0},{0,28},{5,9},{9... | collective-permute-start | bytes 196616 | tf_op jit(solution)/shard_map/ppermute | solution.py:581
  58.6 2.4 %collective-permute-start.9 = (bf16[4,32,256]{2,1,0:T(8,128)(2,1)S(1)}, bf16[4,32,256]{2,1,0:T(8,128)(2,1)S(1)}, u32[]{:S(2)}, u32[]{:S(2)}) collective-permute-start(bf16[4,32,256]{2,1,0:T(8,128)(2,1)S(1)} %get-tuple-element.62), channel_id=1, source_target_pairs={{0,4},{4,0},{8,12},{12,8},{16,20},{20,16},{24,28},{28,24},{1,5},{5... | collective-permute-start | bytes 196616 | tf_op jit(solution)/shard_map/ppermute | solution.py:581
  63.3 10.0 %collective-permute-start.12 = (bf16[256,1152]{1,0:T(8,128)(2,1)S(1)}, bf16[256,1152]{1,0:T(8,128)(2,1)S(1)}, u32[]{:S(2)}, u32[]{:S(2)}) collective-permute-start(bf16[256,1152]{1,0:T(8,128)(2,1)S(1)} %get-tuple-element.68), channel_id=1, source_target_pairs={{0,32},{4,100},{32,0},{36,68},{64,96},{68,36},{96,64},{100,4},{1,3... | collective-permute-start | bytes 1769480 | tf_op jit(solution)/shard_map/ppermute | solution.py:591
  65.3 9.9 %collective-permute-start.13 = (bf16[256,1152]{1,0:T(8,128)(2,1)S(1)}, bf16[256,1152]{1,0:T(8,128)(2,1)S(1)}, u32[]{:S(2)}, u32[]{:S(2)}) collective-permute-start(bf16[256,1152]{1,0:T(8,128)(2,1)S(1)} %get-tuple-element.69), channel_id=1, source_target_pairs={{0,8},{4,28},{8,0},{12,20},{16,24},{20,12},{24,16},{28,4},{1,9},{5... | collective-permute-start | bytes 1769480 | tf_op jit(solution)/shard_map/ppermute | solution.py:591
  65.4 3.9 %collective-permute-start.14 = (bf16[48,256]{1,0:T(8,128)(2,1)S(1)}, bf16[48,256]{1,0:T(8,128)(2,1)S(1)}, u32[]{:S(2)}, u32[]{:S(2)}) collective-permute-start(bf16[48,256]{1,0:T(8,128)(2,1)S(1)} %get-tuple-element.73), channel_id=1, source_target_pairs={{0,1},{1,0},{2,3},{3,2},{4,5},{5,4},{6,7},{7,6},{8,9},{9,8},{10,11... | collective-permute-start | bytes 73736 | tf_op jit(solution)/shard_map/ppermute | solution.py:585
  66.1 5.0 %collective-permute-start.15 = (bf16[48,256]{1,0:T(8,128)(2,1)S(1)}, bf16[48,256]{1,0:T(8,128)(2,1)S(1)}, u32[]{:S(2)}, u32[]{:S(2)}) collective-permute-start(bf16[48,256]{1,0:T(8,128)(2,1)S(1)} %get-tuple-element.74), channel_id=1, source_target_pairs={{1,2},{2,1},{3,0},{0,3},{5,6},{6,5},{7,4},{4,7},{9,10},{10,9},{11,... | collective-permute-start | bytes 73736 | tf_op jit(solution)/shard_map/ppermute | solution.py:585
  75.4 6.8 %collective-permute-start.16 = (bf16[128,1152]{1,0:T(8,128)(2,1)S(1)}, bf16[128,1152]{1,0:T(8,128)(2,1)S(1)}, u32[]{:S(2)}, u32[]{:S(2)}) collective-permute-start(bf16[128,1152]{1,0:T(8,128)(2,1)S(1)} %get-tuple-element.79), channel_id=1, source_target_pairs={{0,8},{4,28},{8,0},{12,20},{16,24},{20,12},{24,16},{28,4},{1,9},{5... | collective-permute-start | bytes 884744 | tf_op jit(solution)/shard_map/ppermute | solution.py:591
  75.5 6.8 %collective-permute-start.17 = (bf16[128,1152]{1,0:T(8,128)(2,1)S(1)}, bf16[128,1152]{1,0:T(8,128)(2,1)S(1)}, u32[]{:S(2)}, u32[]{:S(2)}) collective-permute-start(bf16[128,1152]{1,0:T(8,128)(2,1)S(1)} %get-tuple-element.80), channel_id=1, source_target_pairs={{0,32},{4,100},{32,0},{36,68},{64,96},{68,36},{96,64},{100,4},{1,3... | collective-permute-start | bytes 884744 | tf_op jit(solution)/shard_map/ppermute | solution.py:591
  83.3 19.6 %all-to-all-start = ((bf16[16,8,2304]{2,1,0:T(8,128)(2,1)}), bf16[16,8,2304]{2,1,0:T(8,128)(2,1)S(1)}, u32[]{:S(2)}, u32[]{:S(2)}) async-start(bf16[16,8,2304]{2,1,0:T(8,128)(2,1)} %bitcast.1), calls=%async_computation | async-start | bytes 1179648 | tf_op jit(solution)/shard_map/all_to_all | solution.py:723

commit v4 on v3

--- a/solution.py
+++ b/solution.py
@@ -94,26 +94,37 @@
         far[...] = left[...].astype(BF)
 
 
-def rows_a_kernel(h_ref, c_ref, x_ref, t_ref, near, far):
+def rows_a_kernel(h_ref, c_ref, x_ref, t_ref, near, far, cells, sems):
     odd, _ = parities()
     rows, _ = row_offsets(ROWS_A)
-    for name, width, parts in ROWS_A:
-        first = jnp.where(odd == 1, 0, R - width)
-        last = jnp.where(odd == 1, R - width, 0)
-        for row in range(width):
-            for part in range(parts):
-                unit = rows[name, row, part]
-                for start, out in ((first, near), (last, far)):
-                    at = start + row
-                    if name == "h":
-                        value = h_ref[0, at]
-                    elif name == "c":
-                        value = c_ref[0, at].astype(BF)
-                    elif name == "t1":
-                        value = t_ref[0, 0, at]
-                    else:
-                        value = x_ref[0, int(name[1]), at, :, quarter(part)]
-                    out[unit] = value
+    copies = []
+
+    def start(source, target):
+        copy = pltpu.make_async_copy(source, target, sems.at[len(copies)])
+        copy.start()
+        copies.append(copy)
+
+    for side, out in enumerate((near, far)):
+        top = odd == 1 if side == 0 else odd == 0
+        for name, width, parts in ROWS_A:
+            first = jnp.where(top, 0, R - width)
+            at = pl.ds(first, width)
+            unit = rows[name, 0, 0]
+            if name == "h":
+                start(h_ref.at[0, at], out.at[unit : unit + width])
+            elif name == "c":
+                start(c_ref.at[0, at], cells.at[side])
+            elif name == "t1":
+                start(t_ref.at[0, 1, at], out.at[unit : unit + width])
+            else:
+                for row in range(width):
+                    for part in range(parts):
+                        start(x_ref.at[0, int(name[1]), first + row, :, quarter(part)], out.at[rows[name, row, part]])
+    for copy in copies:
+        copy.wait()
+    for side, out in enumerate((near, far)):
+        for row in range(2):
+            out[rows["c", row, 0]] = cells[side, row].astype(BF)
 
 
 def cols_a_kernel(h_ref, c_ref, x_ref, t_ref, near_r, far_r, near, far, above, below, left, right):
@@ -126,7 +137,7 @@
         if name == "c":
             return c_ref[0, row, cells]
         if name == "t1":
-            return t_ref[0, 0, row, cells]
+            return t_ref[0, 1, row, cells]
         return x_ref[0, int(name[1]), row, cells, quarter(part)]
 
     pack_columns(ROWS_A, own, above, below, col_odd, near, far, left, right)
@@ -309,6 +320,16 @@
 
 def sigmoid(value):
     return 0.5 * jnp.tanh(0.5 * value) + 0.5
+
+
+def load_kernel(w_hbm, w_ref, sems):
+    copies = [
+        pltpu.make_async_copy(w_hbm.at[quarter(i)], w_ref.at[quarter(i)], sems.at[i]) for i in range(9)
+    ]
+    for copy in copies:
+        copy.start()
+    for copy in copies:
+        copy.wait()
 
 
 def forward_kernel(count_ref, h_ref, c_ref, x_ref, t_ref, w_ref, near_r, far_r, near_c, far_c,
@@ -557,9 +578,13 @@
     return pl.BlockSpec(shape, lambda _: (0,) * len(shape))
 
 
-def call(kernel, inputs, outs, scratch, blocks=None, scalar=False, name=None, flops=0, limit=16):
+def call(kernel, inputs, outs, scratch, blocks=None, scalar=False, name=None, flops=0, limit=16, outside=()):
     blocks = blocks or {}
     specs = [whole(blocks.get(i, value.shape)) for i, value in enumerate(inputs)]
+    inputs = list(inputs)
+    for i in outside:
+        specs[i] = pl.BlockSpec(memory_space=pltpu.HBM)
+        inputs[i] = pltpu.with_memory_space_constraint(inputs[i], pltpu.HBM)
     if scalar:
         specs[0] = pl.BlockSpec(memory_space=pltpu.SMEM)
     size = sum(value.size * value.dtype.itemsize for value in inputs)
@@ -608,22 +633,35 @@
     _, row_units = row_offsets(ROWS_A)
     _, col_units = col_offsets(ROWS_A)
     first_two = {2: (1, 2, R, L, 4 * C)}
-    middle = hidden_cot[:, 1:2]
     border = out((row_units, L, C), BF)
     near, far = call(
-        rows_a_kernel, (hidden_init, cell_init, input_gates, middle), [border] * 2, [], first_two, name="rows_a"
+        rows_a_kernel,
+        (hidden_init, cell_init, input_gates, hidden_cot),
+        [border] * 2,
+        [vmem((2, 2, L, C), F32), pltpu.SemaphoreType.DMA((30,))],
+        name="rows_a",
+        outside=(0, 1, 2, 3),
     )
     near_r, far_r = swap_rows(near, far)
     strip = out((col_units, C), BF)
     near, far = call(
         cols_a_kernel,
-        (hidden_init, cell_init, input_gates, middle, near_r, far_r),
+        (hidden_init, cell_init, input_gates, hidden_cot, near_r, far_r),
         [strip] * 2,
         [vmem((row_units, L, C), BF)] * 2 + [vmem((col_units, C), F32)] * 2,
         first_two,
         name="cols_a",
     )
     near_c, far_c = swap_cols(near, far)
+    weight_in, _ = lax.optimization_barrier((recur_weight, near))
+    (recur_weight,) = call(
+        load_kernel,
+        (weight_in,),
+        [out((9 * C, 4 * C), BF)],
+        [pltpu.SemaphoreType.DMA((9,))],
+        name="load",
+        outside=(0,),
+    )
     _, row_units_b = row_offsets(ROWS_B)
     _, col_units_b = col_offsets(ROWS_B)
     hidden_seq, patches, m1, m0, t1, g2, q, near, far = call(

time: 104 us -> 98.9 us (0.951)
  local copies, waits for them, and re-layouts: 6.53 us -> 0.02 us
  Pallas kernels: 31.2 us -> 35 us
  waiting for transfers between devices: 36.4 us -> 34 us
    unnamed x18 -> x8, local copies, waits for them, and re-layouts: 5.62 us -> 0.02 us
    pallas_call x12 -> x13, Pallas kernels: 31.2 us -> 35 us  [call(): pl.pallas_call(kernel, grid=(1,), in_specs=specs, out_specs=[whole(out.sh...]
    ppermute x3, waiting for transfers between devices: 6.12 us -> 4 us  [swap_cols(): lax.ppermute(far, 'sx', ring_pairs(4, 1))]
  transfers between devices with their start and end apart: 19 -> 19, of which waited for: 13 -> 12; matrix products, arithmetic and copies ran while one was open for 1% -> 1% of each run, Pallas kernels for 14% -> 17%
where the time goes in v4:
time: 98.9 us; the launch traced here: 98.6 us
  Pallas kernels  35 us (35%)
  waiting for transfers between devices  34 us (34%)
  starting transfers between devices  26.9 us (27%)
  between operations  1.45 us (1%)
  other arithmetic  1.31 us (1%)
    pallas_call x13, Pallas kernels, call(): pl.pallas_call(kernel, grid=(1,), in_specs=specs, out_specs=[whole(out.sh...  35 us
    all_to_all x1, waiting for transfers between devices, body(): lax.all_to_all(blocks, AXES, 0, 0, tiled=True, axis_index_groups=owner_gr...  11.2 us
    ppermute x3, starting transfers between devices, swap_rows(): lax.ppermute(far, axis, ring_pairs(8, 1))  7.69 us
    ppermute x4, waiting for transfers between devices, first_partner(): return lax.ppermute(value, (axis, 'core'), pairs)  7.66 us
    all_to_all x1, starting transfers between devices, body(): lax.all_to_all(blocks, AXES, 0, 0, tiled=True, axis_index_groups=owner_gr...  7.04 us
    ppermute x3, starting transfers between devices, swap_cols(): lax.ppermute(far, 'sx', ring_pairs(4, 1))  6.61 us
    ppermute x3, waiting for transfers between devices, swap_rows(): lax.ppermute(far, axis, ring_pairs(8, 1))  4.49 us
    ppermute x3, waiting for transfers between devices, swap_cols(): lax.ppermute(far, 'sx', ring_pairs(4, 1))  4 us
  transfers between devices with their start and end apart: 19, of which 12 were waited for; matrix products, arithmetic and copies ran while one was open for 1% of the time, Pallas kernels for 17%

profile of v4, /device:TPU:0, one launch (start us, length us, event | category | flops | bytes accessed | tf_op | source)
XLA Modules:
  0.0 98.6 jit_solution(18262791199568461653)
XLA Ops:
  0.7 1.5 %rows_a.1 = (bf16[18,32,256]{2,1,0:T(8,128)(2,1)S(1)}, bf16[18,32,256]{2,1,0:T(8,128)(2,1)S(1)}) custom-call(bf16[1,8,32,256]{3,2,1,0:T(8,128)(2,1)} %h_ref.5, f32[1,8,32,256]{3,2,1,0:T(8,128)} %c_ref.5, bf16[1,3,8,32,1024]{4,3,2,1,0:T(8,128)(2,1)} %x_ref.5, bf16[1,3,8,32,256]{4,3,2,1,0:T(8,128)(2,1)} %t0_ref.1), custom_call_target="tpu_custom_call" | custom-call | bytes 2359296 | tf_op jit(solution)/shard_map/rows_a/pallas_call | solution.py:591
  2.2 3.0 %collective-permute-start.1 = (bf16[18,32,256]{2,1,0:T(8,128)(2,1)S(1)}, bf16[18,32,256]{2,1,0:T(8,128)(2,1)S(1)}, u32[]{:S(2)}, u32[]{:S(2)}) collective-permute-start(bf16[18,32,256]{2,1,0:T(8,128)(2,1)S(1)} %get-tuple-element.49), channel_id=1, source_target_pairs={{4,8},{8,4},{12,16},{16,12},{20,24},{24,20},{28,0},{0,28},{5,9},{9... | collective-permute-start | bytes 884744 | tf_op jit(solution)/shard_map/ppermute | solution.py:606
  5.2 4.5 %collective-permute-done.1.far_r = bf16[18,32,256]{2,1,0:T(8,128)(2,1)S(1)} collective-permute-done((bf16[18,32,256]{2,1,0:T(8,128)(2,1)S(1)}, bf16[18,32,256]{2,1,0:T(8,128)(2,1)S(1)}, u32[]{:S(2)}, u32[]{:S(2)}) %collective-permute-start.1) | collective-permute-done | bytes 294944 | tf_op jit(solution)/shard_map/ppermute | solution.py:606
  9.9 1.8 %collective-permute-start.2 = (bf16[224,256]{1,0:T(8,128)(2,1)S(1)}, bf16[224,256]{1,0:T(8,128)(2,1)S(1)}, u32[]{:S(2)}, u32[]{:S(2)}) collective-permute-start(bf16[224,256]{1,0:T(8,128)(2,1)S(1)} %get-tuple-element.50), channel_id=1, source_target_pairs={{0,1},{1,0},{2,3},{3,2},{4,5},{5,4},{6,7},{7,6},{8,9},{9,8},{10,11... | collective-permute-start | bytes 344072 | tf_op jit(solution)/shard_map/ppermute | solution.py:610
  11.7 2.2 %collective-permute-start.3 = (bf16[224,256]{1,0:T(8,128)(2,1)S(1)}, bf16[224,256]{1,0:T(8,128)(2,1)S(1)}, u32[]{:S(2)}, u32[]{:S(2)}) collective-permute-start(bf16[224,256]{1,0:T(8,128)(2,1)S(1)} %get-tuple-element.52), channel_id=1, source_target_pairs={{1,2},{2,1},{3,0},{0,3},{5,6},{6,5},{7,4},{4,7},{9,10},{10,9},{11,... | collective-permute-start | bytes 344072 | tf_op jit(solution)/shard_map/ppermute | solution.py:610
  14.5 2.4 %load.1.w_ref = bf16[2304,1024]{1,0:T(8,128)(2,1)S(1)} custom-call(bf16[2304,1024]{1,0:T(8,128)(2,1)} %w_hbm), custom_call_target="tpu_custom_call" | custom-call | bytes 4718592 | tf_op jit(solution)/shard_map/load/pallas_call | solution.py:591
  16.9 0.8 collective-permute-done.3.far_c
  17.7 12.0 %forward.1 = (bf16[1,3,8,32,256]{4,3,2,1,0:T(8,128)(2,1)}, bf16[3,256,2304]{2,1,0:T(8,128)(2,1)S(1)}, bf16[6,10,48,256]{3,2,1,0:T(8,128)(2,1)S(1)}, bf16[6,8,32,...) custom-call(s32[1]{0:T(128)S(6)} %copy.11.count_ref, ...), custom_call_target="tpu_custom_call" | custom-call | flops 6000000000 | bytes 7897092 | tf_op jit(solution)/shard_map/forward/pallas_call | solution.py:591
  29.7 0.5 collective-permute-start.4
  30.2 2.2 %collective-permute-start.5 = (bf16[9,32,256]{2,1,0:T(8,128)(2,1)S(1)}, bf16[9,32,256]{2,1,0:T(8,128)(2,1)S(1)}, u32[]{:S(2)}, u32[]{:S(2)}) collective-permute-start(bf16[9,32,256]{2,1,0:T(8,128)(2,1)S(1)} %get-tuple-element.60), channel_id=1, source_target_pairs={{4,8},{8,4},{12,16},{16,12},{20,24},{24,20},{28,0},{0,28},{5,9},{9... | collective-permute-start | bytes 442376 | tf_op jit(solution)/shard_map/ppermute | solution.py:606
  32.4 3.7 %collective-permute-done.4.near_r = bf16[9,32,256]{2,1,0:T(8,128)(2,1)S(1)} collective-permute-done((bf16[9,32,256]{2,1,0:T(8,128)(2,1)S(1)}, bf16[9,32,256]{2,1,0:T(8,128)(2,1)S(1)}, u32[]{:S(2)}, u32[]{:S(2)}) %collective-permute-start.4) | collective-permute-done | bytes 147488 | tf_op jit(solution)/shard_map/ppermute | solution.py:606
  36.4 2.3 %collective-permute-start.7 = (bf16[112,256]{1,0:T(8,128)(2,1)S(1)}, bf16[112,256]{1,0:T(8,128)(2,1)S(1)}, u32[]{:S(2)}, u32[]{:S(2)}) collective-permute-start(bf16[112,256]{1,0:T(8,128)(2,1)S(1)} %get-tuple-element.62), channel_id=1, source_target_pairs={{1,2},{2,1},{3,0},{0,3},{5,6},{6,5},{7,4},{4,7},{9,10},{10,9},{11,... | collective-permute-start | bytes 172040 | tf_op jit(solution)/shard_map/ppermute | solution.py:610
  38.6 1.9 %collective-permute-done.6.near_c = bf16[112,256]{1,0:T(8,128)(2,1)S(1)} collective-permute-done((bf16[112,256]{1,0:T(8,128)(2,1)S(1)}, bf16[112,256]{1,0:T(8,128)(2,1)S(1)}, u32[]{:S(2)}, u32[]{:S(2)}) %collective-permute-start.6) | collective-permute-done | bytes 57376 | tf_op jit(solution)/shard_map/ppermute | solution.py:610
  40.5 1.3 %collective-permute-done.7.far_c = bf16[112,256]{1,0:T(8,128)(2,1)S(1)} collective-permute-done((bf16[112,256]{1,0:T(8,128)(2,1)S(1)}, bf16[112,256]{1,0:T(8,128)(2,1)S(1)}, u32[]{:S(2)}, u32[]{:S(2)}) %collective-permute-start.7) | collective-permute-done | bytes 57376 | tf_op jit(solution)/shard_map/ppermute | solution.py:610
  41.8 9.2 %backward.1 = (bf16[8,32,1024]{2,1,0:T(8,128)(2,1)S(1)}, bf16[8,32,1024]{2,1,0:T(8,128)(2,1)S(1)}, f32[1,8,32,256]{3,2,1,0:T(8,128)}, f32[1,8,32,256]{3,2,1,0:T(...) custom-call(s32[1]{0:T(128)S(6)} %copy.11.count_ref, ...), custom_call_target="tpu_custom_call" | custom-call | flops 4000000000 | bytes 8814596 | tf_op jit(solution)/shard_map/backward/pallas_call | solution.py:591
  51.0 2.5 %collective-permute-start.10 = (bf16[4,32,256]{2,1,0:T(8,128)(2,1)S(1)}, bf16[4,32,256]{2,1,0:T(8,128)(2,1)S(1)}, u32[]{:S(2)}, u32[]{:S(2)}) collective-permute-start(bf16[4,32,256]{2,1,0:T(8,128)(2,1)S(1)} %get-tuple-element.65), channel_id=1, source_target_pairs={{4,8},{8,4},{12,16},{16,12},{20,24},{24,20},{28,0},{0,28},{5,9},{9... | collective-permute-start | bytes 196616 | tf_op jit(solution)/shard_map/ppermute | solution.py:606
  53.5 2.4 %own_sum.1.own_ref = f32[512,2304]{1,0:T(8,128)S(1)} custom-call(bf16[512,768]{1,0:T(8,128)(2,1)S(1)} %get-tuple-element.68.mine_ref, bf16[768,2304]{1,0:T(8,128)(2,1)S(1)} %bitcast.9), custom_call_target="tpu_custom_call" | custom-call | flops 2000000000 | bytes 4325376 | tf_op jit(solution)/shard_map/own_sum/pallas_call | solution.py:591
  56.0 2.2 %chip_sum.1 = (bf16[256,1152]{1,0:T(8,128)(2,1)S(1)}, bf16[256,1152]{1,0:T(8,128)(2,1)S(1)}, bf16[256,1152]{1,0:T(8,128)(2,1)S(1)}, bf16[256,1152]{1,0:T(8,128)(2,1)S(1)}) custom-call(bf16[512,768]{1,0:T(8,128)(2,1)S(1)} %collective-permute-done.8.got_ref, bf16[768,2304]{1,0:T(8,128)(2,1)S(1)} %collective-permute-done.11.p_ref, f32[512,2304]{1,0:T(8,128)S(1)} %own_sum.1.own_ref), custom_call_target="tpu_custom_call" | custom-call | flops 2000000000 | bytes 9043968 | tf_op jit(solution)/shard_map/chip_sum/pallas_call | solution.py:591
  58.2 2.0 %collective-permute-start.12 = (bf16[256,1152]{1,0:T(8,128)(2,1)S(1)}, bf16[256,1152]{1,0:T(8,128)(2,1)S(1)}, u32[]{:S(2)}, u32[]{:S(2)}) collective-permute-start(bf16[256,1152]{1,0:T(8,128)(2,1)S(1)} %get-tuple-element.70), channel_id=1, source_target_pairs={{0,32},{4,100},{32,0},{36,68},{64,96},{68,36},{96,64},{100,4},{1,3... | collective-permute-start | bytes 1769480 | tf_op jit(solution)/shard_map/ppermute | solution.py:616
  60.3 0.8 collective-permute-start.14
  61.1 2.2 %collective-permute-start.15 = (bf16[48,256]{1,0:T(8,128)(2,1)S(1)}, bf16[48,256]{1,0:T(8,128)(2,1)S(1)}, u32[]{:S(2)}, u32[]{:S(2)}) collective-permute-start(bf16[48,256]{1,0:T(8,128)(2,1)S(1)} %get-tuple-element.76), channel_id=1, source_target_pairs={{1,2},{2,1},{3,0},{0,3},{5,6},{6,5},{7,4},{4,7},{9,10},{10,9},{11,... | collective-permute-start | bytes 73736 | tf_op jit(solution)/shard_map/ppermute | solution.py:610
  63.2 0.9 collective-permute-done.14.near_c
  64.2 1.9 %collective-permute-done.15.far_c = bf16[48,256]{1,0:T(8,128)(2,1)S(1)} collective-permute-done((bf16[48,256]{1,0:T(8,128)(2,1)S(1)}, bf16[48,256]{1,0:T(8,128)(2,1)S(1)}, u32[]{:S(2)}, u32[]{:S(2)}) %collective-permute-start.15) | collective-permute-done | bytes 24608 | tf_op jit(solution)/shard_map/ppermute | solution.py:610
  66.1 2.0 %collective-permute-done.12.came0 = bf16[256,1152]{1,0:T(8,128)(2,1)S(1)} collective-permute-done((bf16[256,1152]{1,0:T(8,128)(2,1)S(1)}, bf16[256,1152]{1,0:T(8,128)(2,1)S(1)}, u32[]{:S(2)}, u32[]{:S(2)}) %collective-permute-start.12) | collective-permute-done | bytes 589856 | tf_op jit(solution)/shard_map/ppermute | solution.py:616
  68.1 1.9 %collective-permute-done.13.came1 = bf16[256,1152]{1,0:T(8,128)(2,1)S(1)} collective-permute-done((bf16[256,1152]{1,0:T(8,128)(2,1)S(1)}, bf16[256,1152]{1,0:T(8,128)(2,1)S(1)}, u32[]{:S(2)}, u32[]{:S(2)}) %collective-permute-start.13) | collective-permute-done | bytes 589856 | tf_op jit(solution)/shard_map/ppermute | solution.py:616
  70.6 2.9 %last.1 = bf16[1,8,32,256]{3,2,1,0:T(8,128)(2,1)} custom-call(bf16[8,32,1024]{2,1,0:T(8,128)(2,1)S(1)} %get-tuple-element.72.g_ref, bf16[2304,1024]{1,0:T(8,128)(2,1)S(1)} %load.1.w_ref, bf16[4,32,256]{2,1,0:T(8,128)(2,1)S(1)} %collective-permute-done.9.near_r, bf16[4,32,256]{2,1,0:T(8,128)(2,1)S(1)} %collective-permute-done.10.far_r, ...), custom_call_target="tpu_custom_call" | custom-call | flops 2000000000 | bytes 5423104 | tf_op jit(solution)/shard_map/last/pallas_call | solution.py:591
  73.5 3.6 %collective-permute-done.16.came0 = bf16[128,1152]{1,0:T(8,128)(2,1)S(1)} collective-permute-done((bf16[128,1152]{1,0:T(8,128)(2,1)S(1)}, bf16[128,1152]{1,0:T(8,128)(2,1)S(1)}, u32[]{:S(2)}, u32[]{:S(2)}) %collective-permute-start.16) | collective-permute-done | bytes 294944 | tf_op jit(solution)/shard_map/ppermute | solution.py:616
  77.2 0.9 quarter.1
  78.2 7.0 %all-to-all-start = ((bf16[16,8,2304]{2,1,0:T(8,128)(2,1)}), bf16[16,8,2304]{2,1,0:T(8,128)(2,1)S(1)}, u32[]{:S(2)}, u32[]{:S(2)}) async-start(bf16[16,8,2304]{2,1,0:T(8,128)(2,1)} %bitcast.1), calls=%async_computation | async-start | bytes 1179648 | tf_op jit(solution)/shard_map/all_to_all | solution.py:761
  85.2 1.3 %maximum_bitcast_fusion = bf16[1,3,8,32,1024]{4,3,2,1,0:T(8,128)(2,1)} fusion(bf16[1,8,32,1024]{3,2,1,0:T(8,128)(2,1)S(1)} %bitcast.11, bf16[1,8,32,1024]{3,2,1,0:T(8,128)(2,1)S(1)} %bitcast.12, bf16[1,8,32,1024]{3,2,1,0:T(8,128)(2,1)S(1)} %bitcast.10), kind=kLoop, calls=%fused_computation | loop fusion | flops 1572864 | bytes 3145728 | tf_op jit(solution)/shard_map/broadcast_in_dim | solution.py:764
  86.5 11.2 %all-to-all-done.parts_ref = bf16[16,8,2304]{2,1,0:T(8,128)(2,1)S(1)} async-done(((bf16[16,8,2304]{2,1,0:T(8,128)(2,1)}), bf16[16,8,2304]{2,1,0:T(8,128)(2,1)S(1)}, u32[]{:S(2)}, u32[]{:S(2)}) %all-to-all-start) | async-done | bytes 589856 | tf_op jit(solution)/shard_map/all_to_all | solution.py:761
  97.8 0.8 total.1
  (28 shorter events, 1.3 us)
Async XLA Ops:
  0.6 9.0 %copy-start.1 = (bf16[1,3,8,32,256]{4,3,2,1,0:T(8,128)(2,1)S(1)}, bf16[1,3,8,32,256]{4,3,2,1,0:T(8,128)(2,1)}, u32[]{:S(2)}) copy-start(bf16[1,3,8,32,256]{4,3,2,1,0:T(8,128)(2,1)} %t0_ref.1) | copy-start | bytes 1179652
  0.6 9.0 %copy-start = (bf16[1,3,8,32,1024]{4,3,2,1,0:T(8,128)(2,1)S(1)}, bf16[1,3,8,32,1024]{4,3,2,1,0:T(8,128)(2,1)}, u32[]{:S(2)}) copy-start(bf16[1,3,8,32,1024]{4,3,2,1,0:T(8,128)(2,1)} %x_ref.5) | copy-start | bytes 4718596
  0.7 9.0 %copy-start.3 = (bf16[1,8,32,256]{3,2,1,0:T(8,128)(2,1)S(1)}, bf16[1,8,32,256]{3,2,1,0:T(8,128)(2,1)}, u32[]{:S(2)}) copy-start(bf16[1,8,32,256]{3,2,1,0:T(8,128)(2,1)} %h_ref.5) | copy-start | bytes 393220
  0.7 9.0 %copy-start.2 = (f32[1,8,32,256]{3,2,1,0:T(8,128)S(1)}, f32[1,8,32,256]{3,2,1,0:T(8,128)}, u32[]{:S(2)}) copy-start(f32[1,8,32,256]{3,2,1,0:T(8,128)} %c_ref.5) | copy-start | bytes 786436
  2.1 3.1 %collective-permute-start = (bf16[18,32,256]{2,1,0:T(8,128)(2,1)S(1)}, bf16[18,32,256]{2,1,0:T(8,128)(2,1)S(1)}, u32[]{:S(2)}, u32[]{:S(2)}) collective-permute-start(bf16[18,32,256]{2,1,0:T(8,128)(2,1)S(1)} %get-tuple-element.48), channel_id=1, source_target_pairs={{0,4},{4,0},{8,12},{12,8},{16,20},{20,16},{24,28},{28,24},{1,5},{5... | collective-permute-start | bytes 884744 | tf_op jit(solution)/shard_map/ppermute | solution.py:606
  2.2 7.4 %collective-permute-start.1 = (bf16[18,32,256]{2,1,0:T(8,128)(2,1)S(1)}, bf16[18,32,256]{2,1,0:T(8,128)(2,1)S(1)}, u32[]{:S(2)}, u32[]{:S(2)}) collective-permute-start(bf16[18,32,256]{2,1,0:T(8,128)(2,1)S(1)} %get-tuple-element.49), channel_id=1, source_target_pairs={{4,8},{8,4},{12,16},{16,12},{20,24},{24,20},{28,0},{0,28},{5,9},{9... | collective-permute-start | bytes 884744 | tf_op jit(solution)/shard_map/ppermute | solution.py:606
  9.9 7.0 %collective-permute-start.2 = (bf16[224,256]{1,0:T(8,128)(2,1)S(1)}, bf16[224,256]{1,0:T(8,128)(2,1)S(1)}, u32[]{:S(2)}, u32[]{:S(2)}) collective-permute-start(bf16[224,256]{1,0:T(8,128)(2,1)S(1)} %get-tuple-element.50), channel_id=1, source_target_pairs={{0,1},{1,0},{2,3},{3,2},{4,5},{5,4},{6,7},{7,6},{8,9},{9,8},{10,11... | collective-permute-start | bytes 344072 | tf_op jit(solution)/shard_map/ppermute | solution.py:610
  11.7 6.0 %collective-permute-start.3 = (bf16[224,256]{1,0:T(8,128)(2,1)S(1)}, bf16[224,256]{1,0:T(8,128)(2,1)S(1)}, u32[]{:S(2)}, u32[]{:S(2)}) collective-permute-start(bf16[224,256]{1,0:T(8,128)(2,1)S(1)} %get-tuple-element.52), channel_id=1, source_target_pairs={{1,2},{2,1},{3,0},{0,3},{5,6},{6,5},{7,4},{4,7},{9,10},{10,9},{11,... | collective-permute-start | bytes 344072 | tf_op jit(solution)/shard_map/ppermute | solution.py:610
  29.7 26.2 %collective-permute-start.11 = (bf16[768,2304]{1,0:T(8,128)(2,1)S(1)}, bf16[768,2304]{1,0:T(8,128)(2,1)S(1)}, u32[]{:S(2)}, u32[]{:S(2)}) collective-permute-start(bf16[768,2304]{1,0:T(8,128)(2,1)S(1)} %bitcast.8), channel_id=1, source_target_pairs={{0,4},{4,0},{1,5},{5,1},{2,6},{6,2},{3,7},{7,3},{8,12},{12,8},{9,1... | collective-permute-start | bytes 10616840 | tf_op jit(solution)/shard_map/ppermute | solution.py:697
  29.7 6.4 %collective-permute-start.4 = (bf16[9,32,256]{2,1,0:T(8,128)(2,1)S(1)}, bf16[9,32,256]{2,1,0:T(8,128)(2,1)S(1)}, u32[]{:S(2)}, u32[]{:S(2)}) collective-permute-start(bf16[9,32,256]{2,1,0:T(8,128)(2,1)S(1)} %get-tuple-element.59), channel_id=1, source_target_pairs={{0,4},{4,0},{8,12},{12,8},{16,20},{20,16},{24,28},{28,24},{1,5},{5... | collective-permute-start | bytes 442376 | tf_op jit(solution)/shard_map/ppermute | solution.py:606
  30.2 5.9 %collective-permute-start.5 = (bf16[9,32,256]{2,1,0:T(8,128)(2,1)S(1)}, bf16[9,32,256]{2,1,0:T(8,128)(2,1)S(1)}, u32[]{:S(2)}, u32[]{:S(2)}) collective-permute-start(bf16[9,32,256]{2,1,0:T(8,128)(2,1)S(1)} %get-tuple-element.60), channel_id=1, source_target_pairs={{4,8},{8,4},{12,16},{16,12},{20,24},{24,20},{28,0},{0,28},{5,9},{9... | collective-permute-start | bytes 442376 | tf_op jit(solution)/shard_map/ppermute | solution.py:606
  36.3 4.3 %collective-permute-start.6 = (bf16[112,256]{1,0:T(8,128)(2,1)S(1)}, bf16[112,256]{1,0:T(8,128)(2,1)S(1)}, u32[]{:S(2)}, u32[]{:S(2)}) collective-permute-start(bf16[112,256]{1,0:T(8,128)(2,1)S(1)} %get-tuple-element.61), channel_id=1, source_target_pairs={{0,1},{1,0},{2,3},{3,2},{4,5},{5,4},{6,7},{7,6},{8,9},{9,8},{10,11... | collective-permute-start | bytes 172040 | tf_op jit(solution)/shard_map/ppermute | solution.py:610
  36.4 5.5 %collective-permute-start.7 = (bf16[112,256]{1,0:T(8,128)(2,1)S(1)}, bf16[112,256]{1,0:T(8,128)(2,1)S(1)}, u32[]{:S(2)}, u32[]{:S(2)}) collective-permute-start(bf16[112,256]{1,0:T(8,128)(2,1)S(1)} %get-tuple-element.62), channel_id=1, source_target_pairs={{1,2},{2,1},{3,0},{0,3},{5,6},{6,5},{7,4},{4,7},{9,10},{10,9},{11,... | collective-permute-start | bytes 172040 | tf_op jit(solution)/shard_map/ppermute | solution.py:610
  51.0 4.9 %collective-permute-start.8 = (bf16[512,768]{1,0:T(8,128)(2,1)S(1)}, bf16[512,768]{1,0:T(8,128)(2,1)S(1)}, u32[]{:S(2)}, u32[]{:S(2)}) collective-permute-start(bf16[512,768]{1,0:T(8,128)(2,1)S(1)} %get-tuple-element.63), channel_id=1, source_target_pairs={{0,4},{4,0},{1,5},{5,1},{2,6},{6,2},{3,7},{7,3},{8,12},{12,8},{9,1... | collective-permute-start | bytes 2359304 | tf_op jit(solution)/shard_map/ppermute | solution.py:723
  51.0 4.9 %collective-permute-start.10 = (bf16[4,32,256]{2,1,0:T(8,128)(2,1)S(1)}, bf16[4,32,256]{2,1,0:T(8,128)(2,1)S(1)}, u32[]{:S(2)}, u32[]{:S(2)}) collective-permute-start(bf16[4,32,256]{2,1,0:T(8,128)(2,1)S(1)} %get-tuple-element.65), channel_id=1, source_target_pairs={{4,8},{8,4},{12,16},{16,12},{20,24},{24,20},{28,0},{0,28},{5,9},{9... | collective-permute-start | bytes 196616 | tf_op jit(solution)/shard_map/ppermute | solution.py:606
  53.5 2.4 %collective-permute-start.9 = (bf16[4,32,256]{2,1,0:T(8,128)(2,1)S(1)}, bf16[4,32,256]{2,1,0:T(8,128)(2,1)S(1)}, u32[]{:S(2)}, u32[]{:S(2)}) collective-permute-start(bf16[4,32,256]{2,1,0:T(8,128)(2,1)S(1)} %get-tuple-element.64), channel_id=1, source_target_pairs={{0,4},{4,0},{8,12},{12,8},{16,20},{20,16},{24,28},{28,24},{1,5},{5... | collective-permute-start | bytes 196616 | tf_op jit(solution)/shard_map/ppermute | solution.py:606
  58.2 10.0 %collective-permute-start.12 = (bf16[256,1152]{1,0:T(8,128)(2,1)S(1)}, bf16[256,1152]{1,0:T(8,128)(2,1)S(1)}, u32[]{:S(2)}, u32[]{:S(2)}) collective-permute-start(bf16[256,1152]{1,0:T(8,128)(2,1)S(1)} %get-tuple-element.70), channel_id=1, source_target_pairs={{0,32},{4,100},{32,0},{36,68},{64,96},{68,36},{96,64},{100,4},{1,3... | collective-permute-start | bytes 1769480 | tf_op jit(solution)/shard_map/ppermute | solution.py:616
  60.2 9.9 %collective-permute-start.13 = (bf16[256,1152]{1,0:T(8,128)(2,1)S(1)}, bf16[256,1152]{1,0:T(8,128)(2,1)S(1)}, u32[]{:S(2)}, u32[]{:S(2)}) collective-permute-start(bf16[256,1152]{1,0:T(8,128)(2,1)S(1)} %get-tuple-element.71), channel_id=1, source_target_pairs={{0,8},{4,28},{8,0},{12,20},{16,24},{20,12},{24,16},{28,4},{1,9},{5... | collective-permute-start | bytes 1769480 | tf_op jit(solution)/shard_map/ppermute | solution.py:616
  60.3 3.9 %collective-permute-start.14 = (bf16[48,256]{1,0:T(8,128)(2,1)S(1)}, bf16[48,256]{1,0:T(8,128)(2,1)S(1)}, u32[]{:S(2)}, u32[]{:S(2)}) collective-permute-start(bf16[48,256]{1,0:T(8,128)(2,1)S(1)} %get-tuple-element.75), channel_id=1, source_target_pairs={{0,1},{1,0},{2,3},{3,2},{4,5},{5,4},{6,7},{7,6},{8,9},{9,8},{10,11... | collective-permute-start | bytes 73736 | tf_op jit(solution)/shard_map/ppermute | solution.py:610
  61.1 5.0 %collective-permute-start.15 = (bf16[48,256]{1,0:T(8,128)(2,1)S(1)}, bf16[48,256]{1,0:T(8,128)(2,1)S(1)}, u32[]{:S(2)}, u32[]{:S(2)}) collective-permute-start(bf16[48,256]{1,0:T(8,128)(2,1)S(1)} %get-tuple-element.76), channel_id=1, source_target_pairs={{1,2},{2,1},{3,0},{0,3},{5,6},{6,5},{7,4},{4,7},{9,10},{10,9},{11,... | collective-permute-start | bytes 73736 | tf_op jit(solution)/shard_map/ppermute | solution.py:610
  70.3 6.8 %collective-permute-start.16 = (bf16[128,1152]{1,0:T(8,128)(2,1)S(1)}, bf16[128,1152]{1,0:T(8,128)(2,1)S(1)}, u32[]{:S(2)}, u32[]{:S(2)}) collective-permute-start(bf16[128,1152]{1,0:T(8,128)(2,1)S(1)} %get-tuple-element.81), channel_id=1, source_target_pairs={{0,8},{4,28},{8,0},{12,20},{16,24},{20,12},{24,16},{28,4},{1,9},{5... | collective-permute-start | bytes 884744 | tf_op jit(solution)/shard_map/ppermute | solution.py:616
  70.4 6.8 %collective-permute-start.17 = (bf16[128,1152]{1,0:T(8,128)(2,1)S(1)}, bf16[128,1152]{1,0:T(8,128)(2,1)S(1)}, u32[]{:S(2)}, u32[]{:S(2)}) collective-permute-start(bf16[128,1152]{1,0:T(8,128)(2,1)S(1)} %get-tuple-element.82), channel_id=1, source_target_pairs={{0,32},{4,100},{32,0},{36,68},{64,96},{68,36},{96,64},{100,4},{1,3... | collective-permute-start | bytes 884744 | tf_op jit(solution)/shard_map/ppermute | solution.py:616
  78.2 19.6 %all-to-all-start = ((bf16[16,8,2304]{2,1,0:T(8,128)(2,1)}), bf16[16,8,2304]{2,1,0:T(8,128)(2,1)S(1)}, u32[]{:S(2)}, u32[]{:S(2)}) async-start(bf16[16,8,2304]{2,1,0:T(8,128)(2,1)} %bitcast.1), calls=%async_computation | async-start | bytes 1179648 | tf_op jit(solution)/shard_map/all_to_all | solution.py:761

commit v5 on v4

--- a/solution.py
+++ b/solution.py
@@ -332,9 +332,37 @@
         copy.wait()
 
 
-def forward_kernel(count_ref, h_ref, c_ref, x_ref, t_ref, w_ref, near_r, far_r, near_c, far_c,
+def ahead_kernel(h_ref, w_ref, near_r, far_r, out_ref, above, below, hs, shifted, wide):
+    row_odd, _ = parities()
+    arranged(row_odd, near_r, far_r, above, below)
+    rows, _ = row_offsets(ROWS_A)
+    n = R + 4
+    hs[...] = jnp.zeros_like(hs)
+    for row in range(R + 6):
+        if row < 3:
+            mid = above[rows["h", row, 0]]
+        elif row >= R + 3:
+            mid = below[rows["h", row - R - 3, 0]]
+        else:
+            mid = h_ref[0, row - 3]
+        hs[row, 8:40, :] = jnp.where(inside(3, row)[0:L], mid.astype(F32), 0.0)
+        for side in range(3):
+            shifted[side, row] = hs[row, 7 + side : 39 + side, :].astype(BF)
+    for k in range(9):
+        up, side = k // 3, k % 3
+        wide[:, quarter(k)] = shifted[side, up : up + n].reshape(n * L, C)
+
+    def one(at_n, carry):
+        at = pl.ds(pl.multiple_of(at_n * 2 * C, C), 2 * C)
+        out_ref[:, at] = jnp.dot(wide[...], w_ref[:, at], preferred_element_type=F32)
+        return carry
+
+    lax.fori_loop(0, 2, one, 0)
+
+
+def forward_kernel(count_ref, h_ref, c_ref, x_ref, t_ref, w_ref, main_ref, near_r, far_r, near_c, far_c,
                    seq_ref, patch_ref, m1_ref, m0_ref, t1_ref, g2_ref, q_ref, near_out, far_out,
-                   above, below, left, right, hs, cs, gates, shifted, wide):
+                   above, below, left, right, hs, cs, gates, shifted, wide, edge, edge_gates):
     row_odd, col_odd = parities()
     count = count_ref[0]
     arranged(row_odd, near_r, far_r, above, below)
@@ -393,7 +421,7 @@
     def shift(n_rows):
         def one(row, carry):
             hs[row, 7:8, :] = hs[row, 55:56, :]
-            hs[row, 56:57, :] = hs[row, 8:9, :]
+            hs[row, 56:58, :] = hs[row, 8:10, :]
             for side in range(3):
                 shifted[side, row] = hs[row, 7 + side : 55 + side, :].astype(BF)
             return carry
@@ -404,6 +432,26 @@
         for k in range(9):
             up, side = k // 3, k % 3
             patch_ref[frame, :, quarter(k)] = shifted[side, by + up : by + up + R, 0:32, :].reshape(R * L, C)
+
+    def merge(row, carry):
+        cell = lax.broadcasted_iota(jnp.int32, (16, C), 0)
+        at = pl.multiple_of(row * W, 16)
+        for part in range(4):
+            main = main_ref[pl.ds(pl.multiple_of(row * L, 16), L), quarter(part)]
+            side = edge_gates[pl.ds(pl.multiple_of(row * 16, 16), 16), quarter(part)]
+
+            def put(value, slot, source):
+                return jnp.where(cell == slot, jnp.broadcast_to(side[source : source + 1], (16, C)), value)
+
+            low = put(main[0:16], 0, 15)
+            high = put(main[16:32], 15, 0)
+            out = jnp.zeros((16, C), F32)
+            for slot, source in ((0, 1), (1, 2), (14, 13), (15, 14)):
+                out = put(out, slot, source)
+            for i, value in enumerate((low, high, out)):
+                cells = pl.ds(at + 16 * i, 16)
+                gates[cells, quarter(part)] = gates[cells, quarter(part)] + value
+        return carry
 
     for frame in range(3):
         by = 2 - frame
@@ -413,8 +461,24 @@
         wcols = W if by else L
         shift(n + 2)
         own_patches(frame, by)
-        if by:
-            load_gates("x" + str(frame), by)
+        if frame == 0:
+            load_gates("x0", by)
+            for row in range(n + 2):
+                for side in range(3):
+                    near = hs[row, 38 + side : 46 + side, :]
+                    far = hs[row, 48 + side : 56 + side, :]
+                    edge[side, row] = jnp.concatenate([near, far], axis=0).astype(BF)
+            for k in range(9):
+                up, side = k // 3, k % 3
+                wide[0 : n * 16, quarter(k)] = edge[side, up : up + n].reshape(n * 16, C)
+
+            def one(at_n, carry):
+                at = pl.ds(pl.multiple_of(at_n * 2 * C, C), 2 * C)
+                edge_gates[:, at] = jnp.dot(wide[0 : 12 * 16, :], w_ref[:, at], preferred_element_type=F32)
+                return carry
+
+        elif by:
+            load_gates("x1", by)
             for k in range(9):
                 up, side = k // 3, k % 3
                 wide[0:cells, quarter(k)] = shifted[side, up : up + n].reshape(cells, C)
@@ -435,6 +499,8 @@
                 return carry
 
         lax.fori_loop(0, 2, one, 0)
+        if frame == 0:
+            lax.fori_loop(0, n, merge, 0)
 
         def gating(row, carry, frame=frame, by=by, wcols=wcols, valid=valid):
             start = pl.multiple_of(row * wcols, 16)
@@ -643,6 +709,24 @@
         outside=(0, 1, 2, 3),
     )
     near_r, far_r = swap_rows(near, far)
+    weight_in, _ = lax.optimization_barrier((recur_weight, near))
+    (recur_weight,) = call(
+        load_kernel,
+        (weight_in,),
+        [out((9 * C, 4 * C), BF)],
+        [pltpu.SemaphoreType.DMA((9,))],
+        name="load",
+        outside=(0,),
+    )
+    (own_gates,) = call(
+        ahead_kernel,
+        (hidden_init, recur_weight, near_r, far_r),
+        [out(((R + 4) * L, 4 * C), F32)],
+        [vmem((row_units, L, C), BF)] * 2
+        + [vmem((R + 6, 64, C), F32), vmem((3, R + 6, L, C), BF), vmem(((R + 4) * L, 9 * C), BF)],
+        name="ahead",
+        flops=2 * 10**9,
+    )
     strip = out((col_units, C), BF)
     near, far = call(
         cols_a_kernel,
@@ -653,20 +737,11 @@
         name="cols_a",
     )
     near_c, far_c = swap_cols(near, far)
-    weight_in, _ = lax.optimization_barrier((recur_weight, near))
-    (recur_weight,) = call(
-        load_kernel,
-        (weight_in,),
-        [out((9 * C, 4 * C), BF)],
-        [pltpu.SemaphoreType.DMA((9,))],
-        name="load",
-        outside=(0,),
-    )
     _, row_units_b = row_offsets(ROWS_B)
     _, col_units_b = col_offsets(ROWS_B)
     hidden_seq, patches, m1, m0, t1, g2, q, near, far = call(
         forward_kernel,
-        (frame_count, hidden_init, cell_init, input_gates, hidden_cot, recur_weight, near_r, far_r, near_c, far_c),
+        (frame_count, hidden_init, cell_init, input_gates, hidden_cot, recur_weight, own_gates, near_r, far_r, near_c, far_c),
         [
             out((1, 3, R, L, C), BF),
             out((3, R * L, 9 * C), BF),
@@ -686,10 +761,12 @@
             vmem(((R + 4) * W, 4 * C), F32),
             vmem((3, R + 6, W, C), BF),
             vmem(((R + 4) * W, 9 * C), BF),
+            vmem((3, R + 6, 16, C), BF),
+            vmem(((R + 4) * 16, 4 * C), F32),
         ],
         scalar=True,
         name="forward",
-        limit=28,
+        limit=30,
         flops=6 * 10**9,
     )
     near_r, far_r = swap_rows(near, far)

time: 98.9 us -> 97.4 us (0.985)
  waiting for transfers between devices: 34 us -> 31.6 us
    ppermute x3, waiting for transfers between devices: 4.49 us -> 1.44 us  [swap_rows(): lax.ppermute(far, axis, ring_pairs(8, 1))]
    pallas_call x13 -> x14, Pallas kernels: 35 us -> 35.9 us  [call(): pl.pallas_call(kernel, grid=(1,), in_specs=specs, out_specs=[whole(out.sh...]
  transfers between devices with their start and end apart: 19 -> 19, of which waited for: 12 -> 13; matrix products, arithmetic and copies ran while one was open for 1% -> 1% of each run, Pallas kernels for 17% -> 20%
where the time goes in v5:
time: 97.4 us; the launch traced here: 97.1 us
  Pallas kernels  35.9 us (37%)
  waiting for transfers between devices  31.6 us (32%)
  starting transfers between devices  26.9 us (28%)
  between operations  1.45 us (1%)
  other arithmetic  1.31 us (1%)
    pallas_call x14, Pallas kernels, call(): pl.pallas_call(kernel, grid=(1,), in_specs=specs, out_specs=[whole(out.sh...  35.9 us
    all_to_all x1, waiting for transfers between devices, body(): lax.all_to_all(blocks, AXES, 0, 0, tiled=True, axis_index_groups=owner_gr...  11.2 us
    ppermute x3, starting transfers between devices, swap_rows(): lax.ppermute(far, axis, ring_pairs(8, 1))  7.69 us
    ppermute x4, waiting for transfers between devices, first_partner(): return lax.ppermute(value, (axis, 'core'), pairs)  7.67 us
    all_to_all x1, starting transfers between devices, body(): lax.all_to_all(blocks, AXES, 0, 0, tiled=True, axis_index_groups=owner_gr...  7 us
    ppermute x3, starting transfers between devices, swap_cols(): lax.ppermute(far, 'sx', ring_pairs(4, 1))  6.64 us
    ppermute x3, waiting for transfers between devices, swap_cols(): lax.ppermute(far, 'sx', ring_pairs(4, 1))  4.66 us
    ppermute x3, waiting for transfers between devices, swap_rows(): lax.ppermute(near, axis, ring_pairs(8, 0))  3.72 us
  transfers between devices with their start and end apart: 19, of which 13 were waited for; matrix products, arithmetic and copies ran while one was open for 1% of the time, Pallas kernels for 20%

profile of v5, /device:TPU:0, one launch (start us, length us, event | category | flops | bytes accessed | tf_op | source)
XLA Modules:
  0.0 97.1 jit_solution(15742844919161363671)
XLA Ops:
  0.6 1.4 %rows_a.1 = (bf16[18,32,256]{2,1,0:T(8,128)(2,1)S(1)}, bf16[18,32,256]{2,1,0:T(8,128)(2,1)S(1)}) custom-call(bf16[1,8,32,256]{3,2,1,0:T(8,128)(2,1)} %h_ref.7, f32[1,8,32,256]{3,2,1,0:T(8,128)} %c_ref.5, bf16[1,3,8,32,1024]{4,3,2,1,0:T(8,128)(2,1)} %x_ref.5, bf16[1,3,8,32,256]{4,3,2,1,0:T(8,128)(2,1)} %t0_ref.1), custom_call_target="tpu_custom_call" | custom-call | bytes 2359296 | tf_op jit(solution)/shard_map/rows_a/pallas_call | solution.py:657
  2.1 3.0 %collective-permute-start.1 = (bf16[18,32,256]{2,1,0:T(8,128)(2,1)S(1)}, bf16[18,32,256]{2,1,0:T(8,128)(2,1)S(1)}, u32[]{:S(2)}, u32[]{:S(2)}) collective-permute-start(bf16[18,32,256]{2,1,0:T(8,128)(2,1)S(1)} %get-tuple-element.50), channel_id=1, source_target_pairs={{4,8},{8,4},{12,16},{16,12},{20,24},{24,20},{28,0},{0,28},{5,9},{9... | collective-permute-start | bytes 884744 | tf_op jit(solution)/shard_map/ppermute | solution.py:672
  5.2 2.4 %load.1.w_ref = bf16[2304,1024]{1,0:T(8,128)(2,1)S(1)} custom-call(bf16[2304,1024]{1,0:T(8,128)(2,1)} %w_hbm), custom_call_target="tpu_custom_call" | custom-call | bytes 4718592 | tf_op jit(solution)/shard_map/load/pallas_call | solution.py:657
  8.2 1.4 %collective-permute-done.1.far_r = bf16[18,32,256]{2,1,0:T(8,128)(2,1)S(1)} collective-permute-done((bf16[18,32,256]{2,1,0:T(8,128)(2,1)S(1)}, bf16[18,32,256]{2,1,0:T(8,128)(2,1)S(1)}, u32[]{:S(2)}, u32[]{:S(2)}) %collective-permute-start.1) | collective-permute-done | bytes 294944 | tf_op jit(solution)/shard_map/ppermute | solution.py:672
  9.8 1.8 %collective-permute-start.2 = (bf16[224,256]{1,0:T(8,128)(2,1)S(1)}, bf16[224,256]{1,0:T(8,128)(2,1)S(1)}, u32[]{:S(2)}, u32[]{:S(2)}) collective-permute-start(bf16[224,256]{1,0:T(8,128)(2,1)S(1)} %get-tuple-element.51), channel_id=1, source_target_pairs={{0,1},{1,0},{2,3},{3,2},{4,5},{5,4},{6,7},{7,6},{8,9},{9,8},{10,11... | collective-permute-start | bytes 344072 | tf_op jit(solution)/shard_map/ppermute | solution.py:676
  11.6 2.2 %collective-permute-start.3 = (bf16[224,256]{1,0:T(8,128)(2,1)S(1)}, bf16[224,256]{1,0:T(8,128)(2,1)S(1)}, u32[]{:S(2)}, u32[]{:S(2)}) collective-permute-start(bf16[224,256]{1,0:T(8,128)(2,1)S(1)} %get-tuple-element.52), channel_id=1, source_target_pairs={{1,2},{2,1},{3,0},{0,3},{5,6},{6,5},{7,4},{4,7},{9,10},{10,9},{11,... | collective-permute-start | bytes 344072 | tf_op jit(solution)/shard_map/ppermute | solution.py:676
  13.8 2.4 %ahead.1.main_ref = f32[384,1024]{1,0:T(8,128)S(1)} custom-call(bf16[1,8,32,256]{3,2,1,0:T(8,128)(2,1)S(1)} %copy-done.3, bf16[2304,1024]{1,0:T(8,128)(2,1)S(1)} %load.1.w_ref, bf16[18,32,256]{2,1,0:T(8,128)(2,1)S(1)} %collective-permute-done.near_r, bf16[18,32,256]{2,1,0:T(8,128)(2,1)S(1)} %collective-permute-done.1.far_r), custom_call_target="tpu_custom_call" | custom-call | flops 2000000000 | bytes 5439488 | tf_op jit(solution)/shard_map/ahead/pallas_call | solution.py:657
  16.2 1.4 %collective-permute-done.3.far_c = bf16[224,256]{1,0:T(8,128)(2,1)S(1)} collective-permute-done((bf16[224,256]{1,0:T(8,128)(2,1)S(1)}, bf16[224,256]{1,0:T(8,128)(2,1)S(1)}, u32[]{:S(2)}, u32[]{:S(2)}) %collective-permute-start.3) | collective-permute-done | bytes 114720 | tf_op jit(solution)/shard_map/ppermute | solution.py:676
  17.6 10.6 %forward.1 = (bf16[1,3,8,32,256]{4,3,2,1,0:T(8,128)(2,1)}, bf16[3,256,2304]{2,1,0:T(8,128)(2,1)S(1)}, bf16[6,10,48,256]{3,2,1,0:T(8,128)(2,1)S(1)}, bf16[6,8,32,...) custom-call(s32[1]{0:T(128)S(6)} %copy.11.count_ref, ...), custom_call_target="tpu_custom_call" | custom-call | flops 6000000000 | bytes 9469956 | tf_op jit(solution)/shard_map/forward/pallas_call | solution.py:657
  28.8 2.2 %collective-permute-start.5 = (bf16[9,32,256]{2,1,0:T(8,128)(2,1)S(1)}, bf16[9,32,256]{2,1,0:T(8,128)(2,1)S(1)}, u32[]{:S(2)}, u32[]{:S(2)}) collective-permute-start(bf16[9,32,256]{2,1,0:T(8,128)(2,1)S(1)} %get-tuple-element.60), channel_id=1, source_target_pairs={{4,8},{8,4},{12,16},{16,12},{20,24},{24,20},{28,0},{0,28},{5,9},{9... | collective-permute-start | bytes 442376 | tf_op jit(solution)/shard_map/ppermute | solution.py:672
  31.0 3.7 %collective-permute-done.4.near_r = bf16[9,32,256]{2,1,0:T(8,128)(2,1)S(1)} collective-permute-done((bf16[9,32,256]{2,1,0:T(8,128)(2,1)S(1)}, bf16[9,32,256]{2,1,0:T(8,128)(2,1)S(1)}, u32[]{:S(2)}, u32[]{:S(2)}) %collective-permute-start.4) | collective-permute-done | bytes 147488 | tf_op jit(solution)/shard_map/ppermute | solution.py:672
  34.9 2.3 %collective-permute-start.7 = (bf16[112,256]{1,0:T(8,128)(2,1)S(1)}, bf16[112,256]{1,0:T(8,128)(2,1)S(1)}, u32[]{:S(2)}, u32[]{:S(2)}) collective-permute-start(bf16[112,256]{1,0:T(8,128)(2,1)S(1)} %get-tuple-element.62), channel_id=1, source_target_pairs={{1,2},{2,1},{3,0},{0,3},{5,6},{6,5},{7,4},{4,7},{9,10},{10,9},{11,... | collective-permute-start | bytes 172040 | tf_op jit(solution)/shard_map/ppermute | solution.py:676
  37.2 1.9 %collective-permute-done.6.near_c = bf16[112,256]{1,0:T(8,128)(2,1)S(1)} collective-permute-done((bf16[112,256]{1,0:T(8,128)(2,1)S(1)}, bf16[112,256]{1,0:T(8,128)(2,1)S(1)}, u32[]{:S(2)}, u32[]{:S(2)}) %collective-permute-start.6) | collective-permute-done | bytes 57376 | tf_op jit(solution)/shard_map/ppermute | solution.py:676
  39.1 1.3 %collective-permute-done.7.far_c = bf16[112,256]{1,0:T(8,128)(2,1)S(1)} collective-permute-done((bf16[112,256]{1,0:T(8,128)(2,1)S(1)}, bf16[112,256]{1,0:T(8,128)(2,1)S(1)}, u32[]{:S(2)}, u32[]{:S(2)}) %collective-permute-start.7) | collective-permute-done | bytes 57376 | tf_op jit(solution)/shard_map/ppermute | solution.py:676
  40.4 9.2 %backward.1 = (bf16[8,32,1024]{2,1,0:T(8,128)(2,1)S(1)}, bf16[8,32,1024]{2,1,0:T(8,128)(2,1)S(1)}, f32[1,8,32,256]{3,2,1,0:T(8,128)}, f32[1,8,32,256]{3,2,1,0:T(...) custom-call(s32[1]{0:T(128)S(6)} %copy.11.count_ref, ...), custom_call_target="tpu_custom_call" | custom-call | flops 4000000000 | bytes 8814596 | tf_op jit(solution)/shard_map/backward/pallas_call | solution.py:657
  49.6 2.5 %collective-permute-start.10 = (bf16[4,32,256]{2,1,0:T(8,128)(2,1)S(1)}, bf16[4,32,256]{2,1,0:T(8,128)(2,1)S(1)}, u32[]{:S(2)}, u32[]{:S(2)}) collective-permute-start(bf16[4,32,256]{2,1,0:T(8,128)(2,1)S(1)} %get-tuple-element.65), channel_id=1, source_target_pairs={{4,8},{8,4},{12,16},{16,12},{20,24},{24,20},{28,0},{0,28},{5,9},{9... | collective-permute-start | bytes 196616 | tf_op jit(solution)/shard_map/ppermute | solution.py:672
  52.0 2.4 %own_sum.1.own_ref = f32[512,2304]{1,0:T(8,128)S(1)} custom-call(bf16[512,768]{1,0:T(8,128)(2,1)S(1)} %get-tuple-element.68.mine_ref, bf16[768,2304]{1,0:T(8,128)(2,1)S(1)} %bitcast.9), custom_call_target="tpu_custom_call" | custom-call | flops 2000000000 | bytes 4325376 | tf_op jit(solution)/shard_map/own_sum/pallas_call | solution.py:657
  54.5 2.2 %chip_sum.1 = (bf16[256,1152]{1,0:T(8,128)(2,1)S(1)}, bf16[256,1152]{1,0:T(8,128)(2,1)S(1)}, bf16[256,1152]{1,0:T(8,128)(2,1)S(1)}, bf16[256,1152]{1,0:T(8,128)(2,1)S(1)}) custom-call(bf16[512,768]{1,0:T(8,128)(2,1)S(1)} %collective-permute-done.8.got_ref, bf16[768,2304]{1,0:T(8,128)(2,1)S(1)} %collective-permute-done.11.p_ref, f32[512,2304]{1,0:T(8,128)S(1)} %own_sum.1.own_ref), custom_call_target="tpu_custom_call" | custom-call | flops 2000000000 | bytes 9043968 | tf_op jit(solution)/shard_map/chip_sum/pallas_call | solution.py:657
  56.7 2.0 %collective-permute-start.12 = (bf16[256,1152]{1,0:T(8,128)(2,1)S(1)}, bf16[256,1152]{1,0:T(8,128)(2,1)S(1)}, u32[]{:S(2)}, u32[]{:S(2)}) collective-permute-start(bf16[256,1152]{1,0:T(8,128)(2,1)S(1)} %get-tuple-element.70), channel_id=1, source_target_pairs={{0,32},{4,100},{32,0},{36,68},{64,96},{68,36},{96,64},{100,4},{1,3... | collective-permute-start | bytes 1769480 | tf_op jit(solution)/shard_map/ppermute | solution.py:682
  58.8 0.8 collective-permute-start.14
  59.6 2.2 %collective-permute-start.15 = (bf16[48,256]{1,0:T(8,128)(2,1)S(1)}, bf16[48,256]{1,0:T(8,128)(2,1)S(1)}, u32[]{:S(2)}, u32[]{:S(2)}) collective-permute-start(bf16[48,256]{1,0:T(8,128)(2,1)S(1)} %get-tuple-element.76), channel_id=1, source_target_pairs={{1,2},{2,1},{3,0},{0,3},{5,6},{6,5},{7,4},{4,7},{9,10},{10,9},{11,... | collective-permute-start | bytes 73736 | tf_op jit(solution)/shard_map/ppermute | solution.py:676
  61.8 0.9 collective-permute-done.14.near_c
  62.7 1.9 %collective-permute-done.15.far_c = bf16[48,256]{1,0:T(8,128)(2,1)S(1)} collective-permute-done((bf16[48,256]{1,0:T(8,128)(2,1)S(1)}, bf16[48,256]{1,0:T(8,128)(2,1)S(1)}, u32[]{:S(2)}, u32[]{:S(2)}) %collective-permute-start.15) | collective-permute-done | bytes 24608 | tf_op jit(solution)/shard_map/ppermute | solution.py:676
  64.6 2.0 %collective-permute-done.12.came0 = bf16[256,1152]{1,0:T(8,128)(2,1)S(1)} collective-permute-done((bf16[256,1152]{1,0:T(8,128)(2,1)S(1)}, bf16[256,1152]{1,0:T(8,128)(2,1)S(1)}, u32[]{:S(2)}, u32[]{:S(2)}) %collective-permute-start.12) | collective-permute-done | bytes 589856 | tf_op jit(solution)/shard_map/ppermute | solution.py:682
  66.7 1.9 %collective-permute-done.13.came1 = bf16[256,1152]{1,0:T(8,128)(2,1)S(1)} collective-permute-done((bf16[256,1152]{1,0:T(8,128)(2,1)S(1)}, bf16[256,1152]{1,0:T(8,128)(2,1)S(1)}, u32[]{:S(2)}, u32[]{:S(2)}) %collective-permute-start.13) | collective-permute-done | bytes 589856 | tf_op jit(solution)/shard_map/ppermute | solution.py:682
  69.1 2.9 %last.1 = bf16[1,8,32,256]{3,2,1,0:T(8,128)(2,1)} custom-call(bf16[8,32,1024]{2,1,0:T(8,128)(2,1)S(1)} %get-tuple-element.72.g_ref, bf16[2304,1024]{1,0:T(8,128)(2,1)S(1)} %load.1.w_ref, bf16[4,32,256]{2,1,0:T(8,128)(2,1)S(1)} %collective-permute-done.9.near_r, bf16[4,32,256]{2,1,0:T(8,128)(2,1)S(1)} %collective-permute-done.10.far_r, ...), custom_call_target="tpu_custom_call" | custom-call | flops 2000000000 | bytes 5423104 | tf_op jit(solution)/shard_map/last/pallas_call | solution.py:657
  72.0 3.6 %collective-permute-done.16.came0 = bf16[128,1152]{1,0:T(8,128)(2,1)S(1)} collective-permute-done((bf16[128,1152]{1,0:T(8,128)(2,1)S(1)}, bf16[128,1152]{1,0:T(8,128)(2,1)S(1)}, u32[]{:S(2)}, u32[]{:S(2)}) %collective-permute-start.16) | collective-permute-done | bytes 294944 | tf_op jit(solution)/shard_map/ppermute | solution.py:682
  75.8 0.9 quarter.1
  76.7 7.0 %all-to-all-start = ((bf16[16,8,2304]{2,1,0:T(8,128)(2,1)}), bf16[16,8,2304]{2,1,0:T(8,128)(2,1)S(1)}, u32[]{:S(2)}, u32[]{:S(2)}) async-start(bf16[16,8,2304]{2,1,0:T(8,128)(2,1)} %bitcast.1), calls=%async_computation | async-start | bytes 1179648 | tf_op jit(solution)/shard_map/all_to_all | solution.py:838
  83.7 1.3 %maximum_bitcast_fusion = bf16[1,3,8,32,1024]{4,3,2,1,0:T(8,128)(2,1)} fusion(bf16[1,8,32,1024]{3,2,1,0:T(8,128)(2,1)S(1)} %bitcast.11, bf16[1,8,32,1024]{3,2,1,0:T(8,128)(2,1)S(1)} %bitcast.12, bf16[1,8,32,1024]{3,2,1,0:T(8,128)(2,1)S(1)} %bitcast.10), kind=kLoop, calls=%fused_computation | loop fusion | flops 1572864 | bytes 3145728 | tf_op jit(solution)/shard_map/broadcast_in_dim | solution.py:841
  85.0 11.2 %all-to-all-done.parts_ref = bf16[16,8,2304]{2,1,0:T(8,128)(2,1)S(1)} async-done(((bf16[16,8,2304]{2,1,0:T(8,128)(2,1)}), bf16[16,8,2304]{2,1,0:T(8,128)(2,1)S(1)}, u32[]{:S(2)}, u32[]{:S(2)}) %all-to-all-start) | async-done | bytes 589856 | tf_op jit(solution)/shard_map/all_to_all | solution.py:838
  96.3 0.8 total.1
  (29 shorter events, 1.8 us)
Async XLA Ops:
  2.0 6.2 %collective-permute-start = (bf16[18,32,256]{2,1,0:T(8,128)(2,1)S(1)}, bf16[18,32,256]{2,1,0:T(8,128)(2,1)S(1)}, u32[]{:S(2)}, u32[]{:S(2)}) collective-permute-start(bf16[18,32,256]{2,1,0:T(8,128)(2,1)S(1)} %get-tuple-element.48), channel_id=1, source_target_pairs={{0,4},{4,0},{8,12},{12,8},{16,20},{20,16},{24,28},{28,24},{1,5},{5... | collective-permute-start | bytes 884744 | tf_op jit(solution)/shard_map/ppermute | solution.py:672
  2.1 7.5 %copy-start = (bf16[1,3,8,32,1024]{4,3,2,1,0:T(8,128)(2,1)S(1)}, bf16[1,3,8,32,1024]{4,3,2,1,0:T(8,128)(2,1)}, u32[]{:S(2)}) copy-start(bf16[1,3,8,32,1024]{4,3,2,1,0:T(8,128)(2,1)} %x_ref.5) | copy-start | bytes 4718596
  2.1 7.5 %copy-start.1 = (bf16[1,3,8,32,256]{4,3,2,1,0:T(8,128)(2,1)S(1)}, bf16[1,3,8,32,256]{4,3,2,1,0:T(8,128)(2,1)}, u32[]{:S(2)}) copy-start(bf16[1,3,8,32,256]{4,3,2,1,0:T(8,128)(2,1)} %t0_ref.1) | copy-start | bytes 1179652
  2.1 7.5 %copy-start.2 = (f32[1,8,32,256]{3,2,1,0:T(8,128)S(1)}, f32[1,8,32,256]{3,2,1,0:T(8,128)}, u32[]{:S(2)}) copy-start(f32[1,8,32,256]{3,2,1,0:T(8,128)} %c_ref.5) | copy-start | bytes 786436
  2.1 7.5 %copy-start.3 = (bf16[1,8,32,256]{3,2,1,0:T(8,128)(2,1)S(1)}, bf16[1,8,32,256]{3,2,1,0:T(8,128)(2,1)}, u32[]{:S(2)}) copy-start(bf16[1,8,32,256]{3,2,1,0:T(8,128)(2,1)} %h_ref.7) | copy-start | bytes 393220
  2.1 7.4 %collective-permute-start.1 = (bf16[18,32,256]{2,1,0:T(8,128)(2,1)S(1)}, bf16[18,32,256]{2,1,0:T(8,128)(2,1)S(1)}, u32[]{:S(2)}, u32[]{:S(2)}) collective-permute-start(bf16[18,32,256]{2,1,0:T(8,128)(2,1)S(1)} %get-tuple-element.50), channel_id=1, source_target_pairs={{4,8},{8,4},{12,16},{16,12},{20,24},{24,20},{28,0},{0,28},{5,9},{9... | collective-permute-start | bytes 884744 | tf_op jit(solution)/shard_map/ppermute | solution.py:672
  9.8 6.3 %collective-permute-start.2 = (bf16[224,256]{1,0:T(8,128)(2,1)S(1)}, bf16[224,256]{1,0:T(8,128)(2,1)S(1)}, u32[]{:S(2)}, u32[]{:S(2)}) collective-permute-start(bf16[224,256]{1,0:T(8,128)(2,1)S(1)} %get-tuple-element.51), channel_id=1, source_target_pairs={{0,1},{1,0},{2,3},{3,2},{4,5},{5,4},{6,7},{7,6},{8,9},{9,8},{10,11... | collective-permute-start | bytes 344072 | tf_op jit(solution)/shard_map/ppermute | solution.py:676
  11.6 6.0 %collective-permute-start.3 = (bf16[224,256]{1,0:T(8,128)(2,1)S(1)}, bf16[224,256]{1,0:T(8,128)(2,1)S(1)}, u32[]{:S(2)}, u32[]{:S(2)}) collective-permute-start(bf16[224,256]{1,0:T(8,128)(2,1)S(1)} %get-tuple-element.52), channel_id=1, source_target_pairs={{1,2},{2,1},{3,0},{0,3},{5,6},{6,5},{7,4},{4,7},{9,10},{10,9},{11,... | collective-permute-start | bytes 344072 | tf_op jit(solution)/shard_map/ppermute | solution.py:676
  28.3 26.2 %collective-permute-start.11 = (bf16[768,2304]{1,0:T(8,128)(2,1)S(1)}, bf16[768,2304]{1,0:T(8,128)(2,1)S(1)}, u32[]{:S(2)}, u32[]{:S(2)}) collective-permute-start(bf16[768,2304]{1,0:T(8,128)(2,1)S(1)} %bitcast.8), channel_id=1, source_target_pairs={{0,4},{4,0},{1,5},{5,1},{2,6},{6,2},{3,7},{7,3},{8,12},{12,8},{9,1... | collective-permute-start | bytes 10616840 | tf_op jit(solution)/shard_map/ppermute | solution.py:774
  28.3 6.4 %collective-permute-start.4 = (bf16[9,32,256]{2,1,0:T(8,128)(2,1)S(1)}, bf16[9,32,256]{2,1,0:T(8,128)(2,1)S(1)}, u32[]{:S(2)}, u32[]{:S(2)}) collective-permute-start(bf16[9,32,256]{2,1,0:T(8,128)(2,1)S(1)} %get-tuple-element.59), channel_id=1, source_target_pairs={{0,4},{4,0},{8,12},{12,8},{16,20},{20,16},{24,28},{28,24},{1,5},{5... | collective-permute-start | bytes 442376 | tf_op jit(solution)/shard_map/ppermute | solution.py:672
  28.8 5.9 %collective-permute-start.5 = (bf16[9,32,256]{2,1,0:T(8,128)(2,1)S(1)}, bf16[9,32,256]{2,1,0:T(8,128)(2,1)S(1)}, u32[]{:S(2)}, u32[]{:S(2)}) collective-permute-start(bf16[9,32,256]{2,1,0:T(8,128)(2,1)S(1)} %get-tuple-element.60), channel_id=1, source_target_pairs={{4,8},{8,4},{12,16},{16,12},{20,24},{24,20},{28,0},{0,28},{5,9},{9... | collective-permute-start | bytes 442376 | tf_op jit(solution)/shard_map/ppermute | solution.py:672
  34.8 4.3 %collective-permute-start.6 = (bf16[112,256]{1,0:T(8,128)(2,1)S(1)}, bf16[112,256]{1,0:T(8,128)(2,1)S(1)}, u32[]{:S(2)}, u32[]{:S(2)}) collective-permute-start(bf16[112,256]{1,0:T(8,128)(2,1)S(1)} %get-tuple-element.61), channel_id=1, source_target_pairs={{0,1},{1,0},{2,3},{3,2},{4,5},{5,4},{6,7},{7,6},{8,9},{9,8},{10,11... | collective-permute-start | bytes 172040 | tf_op jit(solution)/shard_map/ppermute | solution.py:676
  34.9 5.5 %collective-permute-start.7 = (bf16[112,256]{1,0:T(8,128)(2,1)S(1)}, bf16[112,256]{1,0:T(8,128)(2,1)S(1)}, u32[]{:S(2)}, u32[]{:S(2)}) collective-permute-start(bf16[112,256]{1,0:T(8,128)(2,1)S(1)} %get-tuple-element.62), channel_id=1, source_target_pairs={{1,2},{2,1},{3,0},{0,3},{5,6},{6,5},{7,4},{4,7},{9,10},{10,9},{11,... | collective-permute-start | bytes 172040 | tf_op jit(solution)/shard_map/ppermute | solution.py:676
  49.6 4.9 %collective-permute-start.8 = (bf16[512,768]{1,0:T(8,128)(2,1)S(1)}, bf16[512,768]{1,0:T(8,128)(2,1)S(1)}, u32[]{:S(2)}, u32[]{:S(2)}) collective-permute-start(bf16[512,768]{1,0:T(8,128)(2,1)S(1)} %get-tuple-element.63), channel_id=1, source_target_pairs={{0,4},{4,0},{1,5},{5,1},{2,6},{6,2},{3,7},{7,3},{8,12},{12,8},{9,1... | collective-permute-start | bytes 2359304 | tf_op jit(solution)/shard_map/ppermute | solution.py:800
  49.6 4.9 %collective-permute-start.10 = (bf16[4,32,256]{2,1,0:T(8,128)(2,1)S(1)}, bf16[4,32,256]{2,1,0:T(8,128)(2,1)S(1)}, u32[]{:S(2)}, u32[]{:S(2)}) collective-permute-start(bf16[4,32,256]{2,1,0:T(8,128)(2,1)S(1)} %get-tuple-element.65), channel_id=1, source_target_pairs={{4,8},{8,4},{12,16},{16,12},{20,24},{24,20},{28,0},{0,28},{5,9},{9... | collective-permute-start | bytes 196616 | tf_op jit(solution)/shard_map/ppermute | solution.py:672
  52.0 2.4 %collective-permute-start.9 = (bf16[4,32,256]{2,1,0:T(8,128)(2,1)S(1)}, bf16[4,32,256]{2,1,0:T(8,128)(2,1)S(1)}, u32[]{:S(2)}, u32[]{:S(2)}) collective-permute-start(bf16[4,32,256]{2,1,0:T(8,128)(2,1)S(1)} %get-tuple-element.64), channel_id=1, source_target_pairs={{0,4},{4,0},{8,12},{12,8},{16,20},{20,16},{24,28},{28,24},{1,5},{5... | collective-permute-start | bytes 196616 | tf_op jit(solution)/shard_map/ppermute | solution.py:672
  56.7 10.0 %collective-permute-start.12 = (bf16[256,1152]{1,0:T(8,128)(2,1)S(1)}, bf16[256,1152]{1,0:T(8,128)(2,1)S(1)}, u32[]{:S(2)}, u32[]{:S(2)}) collective-permute-start(bf16[256,1152]{1,0:T(8,128)(2,1)S(1)} %get-tuple-element.70), channel_id=1, source_target_pairs={{0,32},{4,100},{32,0},{36,68},{64,96},{68,36},{96,64},{100,4},{1,3... | collective-permute-start | bytes 1769480 | tf_op jit(solution)/shard_map/ppermute | solution.py:682
  58.7 9.9 %collective-permute-start.13 = (bf16[256,1152]{1,0:T(8,128)(2,1)S(1)}, bf16[256,1152]{1,0:T(8,128)(2,1)S(1)}, u32[]{:S(2)}, u32[]{:S(2)}) collective-permute-start(bf16[256,1152]{1,0:T(8,128)(2,1)S(1)} %get-tuple-element.71), channel_id=1, source_target_pairs={{0,8},{4,28},{8,0},{12,20},{16,24},{20,12},{24,16},{28,4},{1,9},{5... | collective-permute-start | bytes 1769480 | tf_op jit(solution)/shard_map/ppermute | solution.py:682
  58.8 3.9 %collective-permute-start.14 = (bf16[48,256]{1,0:T(8,128)(2,1)S(1)}, bf16[48,256]{1,0:T(8,128)(2,1)S(1)}, u32[]{:S(2)}, u32[]{:S(2)}) collective-permute-start(bf16[48,256]{1,0:T(8,128)(2,1)S(1)} %get-tuple-element.75), channel_id=1, source_target_pairs={{0,1},{1,0},{2,3},{3,2},{4,5},{5,4},{6,7},{7,6},{8,9},{9,8},{10,11... | collective-permute-start | bytes 73736 | tf_op jit(solution)/shard_map/ppermute | solution.py:676
  59.6 5.0 %collective-permute-start.15 = (bf16[48,256]{1,0:T(8,128)(2,1)S(1)}, bf16[48,256]{1,0:T(8,128)(2,1)S(1)}, u32[]{:S(2)}, u32[]{:S(2)}) collective-permute-start(bf16[48,256]{1,0:T(8,128)(2,1)S(1)} %get-tuple-element.76), channel_id=1, source_target_pairs={{1,2},{2,1},{3,0},{0,3},{5,6},{6,5},{7,4},{4,7},{9,10},{10,9},{11,... | collective-permute-start | bytes 73736 | tf_op jit(solution)/shard_map/ppermute | solution.py:676
  68.9 6.8 %collective-permute-start.16 = (bf16[128,1152]{1,0:T(8,128)(2,1)S(1)}, bf16[128,1152]{1,0:T(8,128)(2,1)S(1)}, u32[]{:S(2)}, u32[]{:S(2)}) collective-permute-start(bf16[128,1152]{1,0:T(8,128)(2,1)S(1)} %get-tuple-element.81), channel_id=1, source_target_pairs={{0,8},{4,28},{8,0},{12,20},{16,24},{20,12},{24,16},{28,4},{1,9},{5... | collective-permute-start | bytes 884744 | tf_op jit(solution)/shard_map/ppermute | solution.py:682
  69.0 6.8 %collective-permute-start.17 = (bf16[128,1152]{1,0:T(8,128)(2,1)S(1)}, bf16[128,1152]{1,0:T(8,128)(2,1)S(1)}, u32[]{:S(2)}, u32[]{:S(2)}) collective-permute-start(bf16[128,1152]{1,0:T(8,128)(2,1)S(1)} %get-tuple-element.82), channel_id=1, source_target_pairs={{0,32},{4,100},{32,0},{36,68},{64,96},{68,36},{96,64},{100,4},{1,3... | collective-permute-start | bytes 884744 | tf_op jit(solution)/shard_map/ppermute | solution.py:682
  76.7 19.6 %all-to-all-start = ((bf16[16,8,2304]{2,1,0:T(8,128)(2,1)}), bf16[16,8,2304]{2,1,0:T(8,128)(2,1)S(1)}, u32[]{:S(2)}, u32[]{:S(2)}) async-start(bf16[16,8,2304]{2,1,0:T(8,128)(2,1)} %bitcast.1), calls=%async_computation | async-start | bytes 1179648 | tf_op jit(solution)/shard_map/all_to_all | solution.py:838

commit v6 on v5

--- a/solution.py
+++ b/solution.py
@@ -202,25 +202,19 @@
             gw[row * W : (row + 1) * W, quarter(part)] = jnp.where(fits, full, 0.0).astype(BF)
 
 
-def back(n, gw, w_ref, z):
-    cells = n * W
-    for side in range(3):
-        total = None
-        for up in range(3):
-            k = up * 3 + side
-            slab = gw[(2 - up) * W : (2 - up) * W + cells, :]
-            term = lax.dot_general(
-                slab, w_ref[k * C : (k + 1) * C, :], (((1,), (1,)), ((), ())), preferred_element_type=F32
-            )
-            total = term if total is None else total + term
-        z[side, 0:n, 8:56, :] = total.reshape(n, W, C)
-
+def wrapped(n, z):
     def wrap(row, carry):
         z[0, row, 56:57, :] = z[0, row, 8:9, :]
         z[2, row, 7:8, :] = z[2, row, 55:56, :]
         return carry
 
     lax.fori_loop(0, n, wrap, 0)
+
+
+def back(n, gw, w_ref, z):
+    for side in range(3):
+        z[side, 0:n, 8:56, :] = products(gw, w_ref, side, n, W).reshape(n, W, C)
+    wrapped(n, z)
 
 
 def summed(z, row, cells):
@@ -572,8 +566,41 @@
                         out[unit] = g2_ref[start + row, :, quarter(part)]
 
 
-def backward_kernel(count_ref, t0_ref, w_ref, m1_ref, m0_ref, t1_ref, g2_ref, q_ref, near_r, far_r, near_c, far_c,
-                    g1_ref, g0_ref, dh_ref, dc_ref, near_out, far_out, mine_ref, theirs_ref, above, below, left, right, gw, qs, z, turned):
+def ahead_back_kernel(g_ref, w_ref, near_r, far_r, z_ref, above, below, gm):
+    row_odd, _ = parities()
+    arranged(row_odd, near_r, far_r, above, below)
+    rows, _ = row_offsets(ROWS_B)
+    for row in range(R + 4):
+        fits = inside(2, row)[0:L]
+        for part in range(4):
+            if row < 2:
+                mid = above[rows["g", row, part]]
+            elif row >= R + 2:
+                mid = below[rows["g", row - R - 2, part]]
+            else:
+                mid = g_ref[row - 2, :, quarter(part)]
+            gm[row * L : (row + 1) * L, quarter(part)] = jnp.where(fits, mid.astype(F32), 0.0).astype(BF)
+    n = R + 2
+    for side in range(3):
+        z_ref[side] = products(gm, w_ref, side, n, L).reshape(n, L, C)
+
+
+def products(grads, w_ref, side, n, cells):
+    total = None
+    for up in range(3):
+        k = up * 3 + side
+        term = lax.dot_general(
+            grads[(2 - up) * cells : (2 - up + n) * cells, :],
+            w_ref[k * C : (k + 1) * C, :],
+            (((1,), (1,)), ((), ())),
+            preferred_element_type=F32,
+        )
+        total = term if total is None else total + term
+    return total
+
+
+def backward_kernel(count_ref, t0_ref, w_ref, zmain_ref, m1_ref, m0_ref, t1_ref, g2_ref, q_ref, near_r, far_r, near_c, far_c,
+                    g1_ref, g0_ref, dh_ref, dc_ref, near_out, far_out, mine_ref, theirs_ref, above, below, left, right, gw, qs, z, turned, gb):
     row_odd, col_odd = parities()
     count = count_ref[0]
     arranged(row_odd, near_r, far_r, above, below)
@@ -583,7 +610,11 @@
     rows, _ = row_offsets(ROWS_B)
     cols, _ = col_offsets(ROWS_B)
     valid2, valid1 = 2 < count, 1 < count
-    widened_grads(ROWS_B, 2, g2_ref, above, below, left, right, gw)
+    for row in range(R + 4):
+        fits = inside(2, row)[L:W]
+        for part in range(4):
+            value = border(cols["g", row, part], 2, left, right)
+            gb[row * 16 : (row + 1) * 16, quarter(part)] = jnp.where(fits, value, 0.0).astype(BF)
     for row in range(R + 2):
         if row < 1:
             mid = above[rows["q", 0, 0]].astype(F32)
@@ -594,7 +625,10 @@
         qs[row, 0:32, :] = mid
         qs[row, 32:48, :] = border(cols["q", row, 0], 1, left, right)
 
-    back(R + 2, gw, w_ref, z)
+    for side in range(3):
+        z[side, 0 : R + 2, 8:40, :] = zmain_ref[side]
+        z[side, 0 : R + 2, 40:56, :] = products(gb, w_ref, side, R + 2, 16).reshape(R + 2, 16, C)
+    wrapped(R + 2, z)
 
     def first(row, carry):
         keep2 = jnp.broadcast_to(valid2, (W, C))
@@ -772,6 +806,14 @@
     near_r, far_r = swap_rows(near, far)
     flat_patches = patches.reshape(3 * R * L, 9 * C)
     other_patches = lax.ppermute(flat_patches, "core", CORES)
+    (zmain,) = call(
+        ahead_back_kernel,
+        (g2, recur_weight, near_r, far_r),
+        [out((3, R + 2, L, C), F32)],
+        [vmem((row_units_b, L, C), BF)] * 2 + [vmem(((R + 4) * L, 4 * C), BF)],
+        name="ahead_back",
+        flops=2 * 10**9,
+    )
     strip = out((col_units_b, C), BF)
     near, far = call(
         cols_b_kernel,
@@ -783,12 +825,12 @@
     near_c, far_c = swap_cols(near, far)
     g1, g0, _, cell_grad, near_c_rows, far_c_rows, mine, theirs = call(
         backward_kernel,
-        (frame_count, hidden_cot, recur_weight, m1, m0, t1, g2, q, near_r, far_r, near_c, far_c),
+        (frame_count, hidden_cot, recur_weight, zmain, m1, m0, t1, g2, q, near_r, far_r, near_c, far_c),
         [out((R, L, 4 * C), BF), out((R, L, 4 * C), BF), out((1, R, L, C), F32), out((1, R, L, C), F32),
          out((4, L, C), BF), out((4, L, C), BF), out((512, 3 * C), BF), out((512, 3 * C), BF)],
         [vmem((row_units_b, L, C), BF)] * 2
         + [vmem((col_units_b, C), F32)] * 2
-        + [vmem(((R + 4) * W, 4 * C), BF), vmem((R + 2, W, C), F32), vmem((3, R + 2, 64, C), F32), vmem((4 * C, 3 * C), BF)],
+        + [vmem(((R + 4) * W, 4 * C), BF), vmem((R + 2, W, C), F32), vmem((3, R + 2, 64, C), F32), vmem((4 * C, 3 * C), BF), vmem(((R + 4) * 16, 4 * C), BF)],
         {1: (1, 1, R, L, C)},
         scalar=True,
         name="backward",

time: 97.4 us -> 95.9 us (0.985)
  waiting for transfers between devices: 31.6 us -> 29.8 us
    ppermute x3, waiting for transfers between devices: 2.82 us -> 1.06 us  [swap_cols(): lax.ppermute(near, 'sx', ring_pairs(4, 0))]
    pallas_call x14 -> x15, Pallas kernels: 35.9 us -> 36.1 us  [call(): pl.pallas_call(kernel, grid=(1,), in_specs=specs, out_specs=[whole(out.sh...]
  transfers between devices with their start and end apart: 19 -> 19, of which waited for: 13 -> 13; matrix products, arithmetic and copies ran while one was open for 1% -> 1% of each run, Pallas kernels for 20% -> 21%
where the time goes in v6:
time: 95.9 us; the launch traced here: 95.6 us
  Pallas kernels  36.1 us (38%)
  waiting for transfers between devices  29.8 us (31%)
  starting transfers between devices  26.9 us (28%)
  between operations  1.45 us (2%)
  other arithmetic  1.31 us (1%)
    pallas_call x15, Pallas kernels, call(): pl.pallas_call(kernel, grid=(1,), in_specs=specs, out_specs=[whole(out.sh...  36.1 us
    all_to_all x1, waiting for transfers between devices, body(): lax.all_to_all(blocks, AXES, 0, 0, tiled=True, axis_index_groups=owner_gr...  11.2 us
    ppermute x3, starting transfers between devices, swap_rows(): lax.ppermute(far, axis, ring_pairs(8, 1))  7.69 us
    ppermute x4, waiting for transfers between devices, first_partner(): return lax.ppermute(value, (axis, 'core'), pairs)  7.66 us
    all_to_all x1, starting transfers between devices, body(): lax.all_to_all(blocks, AXES, 0, 0, tiled=True, axis_index_groups=owner_gr...  7.01 us
    ppermute x3, starting transfers between devices, swap_cols(): lax.ppermute(far, 'sx', ring_pairs(4, 1))  6.63 us
    ppermute x3, waiting for transfers between devices, swap_cols(): lax.ppermute(far, 'sx', ring_pairs(4, 1))  4.67 us
    ppermute x3, waiting for transfers between devices, swap_rows(): lax.ppermute(near, axis, ring_pairs(8, 0))  3.72 us
  transfers between devices with their start and end apart: 19, of which 13 were waited for; matrix products, arithmetic and copies ran while one was open for 1% of the time, Pallas kernels for 21%

profile of v6, /device:TPU:0, one launch (start us, length us, event | category | flops | bytes accessed | tf_op | source)
XLA Modules:
  0.0 95.6 jit_solution(1629515188822226522)
XLA Ops:
  0.6 1.4 %rows_a.1 = (bf16[18,32,256]{2,1,0:T(8,128)(2,1)S(1)}, bf16[18,32,256]{2,1,0:T(8,128)(2,1)S(1)}) custom-call(bf16[1,8,32,256]{3,2,1,0:T(8,128)(2,1)} %h_ref.7, f32[1,8,32,256]{3,2,1,0:T(8,128)} %c_ref.5, bf16[1,3,8,32,1024]{4,3,2,1,0:T(8,128)(2,1)} %x_ref.5, bf16[1,3,8,32,256]{4,3,2,1,0:T(8,128)(2,1)} %t0_ref.1), custom_call_target="tpu_custom_call" | custom-call | bytes 2359296 | tf_op jit(solution)/shard_map/rows_a/pallas_call | solution.py:691
  2.1 3.0 %collective-permute-start.1 = (bf16[18,32,256]{2,1,0:T(8,128)(2,1)S(1)}, bf16[18,32,256]{2,1,0:T(8,128)(2,1)S(1)}, u32[]{:S(2)}, u32[]{:S(2)}) collective-permute-start(bf16[18,32,256]{2,1,0:T(8,128)(2,1)S(1)} %get-tuple-element.50), channel_id=1, source_target_pairs={{4,8},{8,4},{12,16},{16,12},{20,24},{24,20},{28,0},{0,28},{5,9},{9... | collective-permute-start | bytes 884744 | tf_op jit(solution)/shard_map/ppermute | solution.py:706
  5.2 2.4 %load.1.w_ref = bf16[2304,1024]{1,0:T(8,128)(2,1)S(1)} custom-call(bf16[2304,1024]{1,0:T(8,128)(2,1)} %w_hbm), custom_call_target="tpu_custom_call" | custom-call | bytes 4718592 | tf_op jit(solution)/shard_map/load/pallas_call | solution.py:691
  8.2 1.4 %collective-permute-done.1.far_r = bf16[18,32,256]{2,1,0:T(8,128)(2,1)S(1)} collective-permute-done((bf16[18,32,256]{2,1,0:T(8,128)(2,1)S(1)}, bf16[18,32,256]{2,1,0:T(8,128)(2,1)S(1)}, u32[]{:S(2)}, u32[]{:S(2)}) %collective-permute-start.1) | collective-permute-done | bytes 294944 | tf_op jit(solution)/shard_map/ppermute | solution.py:706
  9.8 1.8 %collective-permute-start.2 = (bf16[224,256]{1,0:T(8,128)(2,1)S(1)}, bf16[224,256]{1,0:T(8,128)(2,1)S(1)}, u32[]{:S(2)}, u32[]{:S(2)}) collective-permute-start(bf16[224,256]{1,0:T(8,128)(2,1)S(1)} %get-tuple-element.51), channel_id=1, source_target_pairs={{0,1},{1,0},{2,3},{3,2},{4,5},{5,4},{6,7},{7,6},{8,9},{9,8},{10,11... | collective-permute-start | bytes 344072 | tf_op jit(solution)/shard_map/ppermute | solution.py:710
  11.6 2.2 %collective-permute-start.3 = (bf16[224,256]{1,0:T(8,128)(2,1)S(1)}, bf16[224,256]{1,0:T(8,128)(2,1)S(1)}, u32[]{:S(2)}, u32[]{:S(2)}) collective-permute-start(bf16[224,256]{1,0:T(8,128)(2,1)S(1)} %get-tuple-element.52), channel_id=1, source_target_pairs={{1,2},{2,1},{3,0},{0,3},{5,6},{6,5},{7,4},{4,7},{9,10},{10,9},{11,... | collective-permute-start | bytes 344072 | tf_op jit(solution)/shard_map/ppermute | solution.py:710
  13.8 2.4 %ahead.1.main_ref = f32[384,1024]{1,0:T(8,128)S(1)} custom-call(bf16[1,8,32,256]{3,2,1,0:T(8,128)(2,1)S(1)} %copy-done.3, bf16[2304,1024]{1,0:T(8,128)(2,1)S(1)} %load.1.w_ref, bf16[18,32,256]{2,1,0:T(8,128)(2,1)S(1)} %collective-permute-done.near_r, bf16[18,32,256]{2,1,0:T(8,128)(2,1)S(1)} %collective-permute-done.1.far_r), custom_call_target="tpu_custom_call" | custom-call | flops 2000000000 | bytes 5439488 | tf_op jit(solution)/shard_map/ahead/pallas_call | solution.py:691
  16.2 1.4 %collective-permute-done.3.far_c = bf16[224,256]{1,0:T(8,128)(2,1)S(1)} collective-permute-done((bf16[224,256]{1,0:T(8,128)(2,1)S(1)}, bf16[224,256]{1,0:T(8,128)(2,1)S(1)}, u32[]{:S(2)}, u32[]{:S(2)}) %collective-permute-start.3) | collective-permute-done | bytes 114720 | tf_op jit(solution)/shard_map/ppermute | solution.py:710
  17.6 10.6 %forward.1 = (bf16[1,3,8,32,256]{4,3,2,1,0:T(8,128)(2,1)}, bf16[3,256,2304]{2,1,0:T(8,128)(2,1)S(1)}, bf16[6,10,48,256]{3,2,1,0:T(8,128)(2,1)S(1)}, bf16[6,8,32,...) custom-call(s32[1]{0:T(128)S(6)} %copy.11.count_ref, ...), custom_call_target="tpu_custom_call" | custom-call | flops 6000000000 | bytes 9469956 | tf_op jit(solution)/shard_map/forward/pallas_call | solution.py:691
  28.8 2.2 %collective-permute-start.5 = (bf16[9,32,256]{2,1,0:T(8,128)(2,1)S(1)}, bf16[9,32,256]{2,1,0:T(8,128)(2,1)S(1)}, u32[]{:S(2)}, u32[]{:S(2)}) collective-permute-start(bf16[9,32,256]{2,1,0:T(8,128)(2,1)S(1)} %get-tuple-element.56), channel_id=1, source_target_pairs={{4,8},{8,4},{12,16},{16,12},{20,24},{24,20},{28,0},{0,28},{5,9},{9... | collective-permute-start | bytes 442376 | tf_op jit(solution)/shard_map/ppermute | solution.py:706
  31.0 3.7 %collective-permute-done.4.near_r = bf16[9,32,256]{2,1,0:T(8,128)(2,1)S(1)} collective-permute-done((bf16[9,32,256]{2,1,0:T(8,128)(2,1)S(1)}, bf16[9,32,256]{2,1,0:T(8,128)(2,1)S(1)}, u32[]{:S(2)}, u32[]{:S(2)}) %collective-permute-start.4) | collective-permute-done | bytes 147488 | tf_op jit(solution)/shard_map/ppermute | solution.py:706
  34.9 2.3 %collective-permute-start.7 = (bf16[112,256]{1,0:T(8,128)(2,1)S(1)}, bf16[112,256]{1,0:T(8,128)(2,1)S(1)}, u32[]{:S(2)}, u32[]{:S(2)}) collective-permute-start(bf16[112,256]{1,0:T(8,128)(2,1)S(1)} %get-tuple-element.62), channel_id=1, source_target_pairs={{1,2},{2,1},{3,0},{0,3},{5,6},{6,5},{7,4},{4,7},{9,10},{10,9},{11,... | collective-permute-start | bytes 172040 | tf_op jit(solution)/shard_map/ppermute | solution.py:710
  37.2 1.7 %ahead_back.1.zmain_ref = f32[3,10,32,256]{3,2,1,0:T(8,128)S(1)} custom-call(bf16[8,32,1024]{2,1,0:T(8,128)(2,1)S(1)} %get-tuple-element.54.g_ref.g2_ref, bf16[2304,1024]{1,0:T(8,128)(2,1)S(1)} %load.1.w_ref, bf16[9,32,256]{2,1,0:T(8,128)(2,1)S(1)} %collective-permute-done.4.near_r, bf16[9,32,256]{2,1,0:T(8,128)(2,1)S(1)} %collective-permute-done.5.far_r), custom_call_target="tpu_custom_call" | custom-call | flops 2000000000 | bytes 5537792 | tf_op jit(solution)/shard_map/ahead_back/pallas_call | solution.py:691
  39.1 1.3 %collective-permute-done.7.far_c = bf16[112,256]{1,0:T(8,128)(2,1)S(1)} collective-permute-done((bf16[112,256]{1,0:T(8,128)(2,1)S(1)}, bf16[112,256]{1,0:T(8,128)(2,1)S(1)}, u32[]{:S(2)}, u32[]{:S(2)}) %collective-permute-start.7) | collective-permute-done | bytes 57376 | tf_op jit(solution)/shard_map/ppermute | solution.py:710
  40.4 7.7 %backward.1 = (bf16[8,32,1024]{2,1,0:T(8,128)(2,1)S(1)}, bf16[8,32,1024]{2,1,0:T(8,128)(2,1)S(1)}, f32[1,8,32,256]{3,2,1,0:T(8,128)}, f32[1,8,32,256]{3,2,1,0:T(...) custom-call(s32[1]{0:T(128)S(6)} %copy.11.count_ref, ...), custom_call_target="tpu_custom_call" | custom-call | flops 4000000000 | bytes 9797636 | tf_op jit(solution)/shard_map/backward/pallas_call | solution.py:691
  48.0 2.5 %collective-permute-start.10 = (bf16[4,32,256]{2,1,0:T(8,128)(2,1)S(1)}, bf16[4,32,256]{2,1,0:T(8,128)(2,1)S(1)}, u32[]{:S(2)}, u32[]{:S(2)}) collective-permute-start(bf16[4,32,256]{2,1,0:T(8,128)(2,1)S(1)} %get-tuple-element.65), channel_id=1, source_target_pairs={{4,8},{8,4},{12,16},{16,12},{20,24},{24,20},{28,0},{0,28},{5,9},{9... | collective-permute-start | bytes 196616 | tf_op jit(solution)/shard_map/ppermute | solution.py:706
  50.5 2.4 %own_sum.1.own_ref = f32[512,2304]{1,0:T(8,128)S(1)} custom-call(bf16[512,768]{1,0:T(8,128)(2,1)S(1)} %get-tuple-element.68.mine_ref, bf16[768,2304]{1,0:T(8,128)(2,1)S(1)} %bitcast.9), custom_call_target="tpu_custom_call" | custom-call | flops 2000000000 | bytes 4325376 | tf_op jit(solution)/shard_map/own_sum/pallas_call | solution.py:691
  53.0 2.2 %chip_sum.1 = (bf16[256,1152]{1,0:T(8,128)(2,1)S(1)}, bf16[256,1152]{1,0:T(8,128)(2,1)S(1)}, bf16[256,1152]{1,0:T(8,128)(2,1)S(1)}, bf16[256,1152]{1,0:T(8,128)(2,1)S(1)}) custom-call(bf16[512,768]{1,0:T(8,128)(2,1)S(1)} %collective-permute-done.8.got_ref, bf16[768,2304]{1,0:T(8,128)(2,1)S(1)} %collective-permute-done.11.p_ref, f32[512,2304]{1,0:T(8,128)S(1)} %own_sum.1.own_ref), custom_call_target="tpu_custom_call" | custom-call | flops 2000000000 | bytes 9043968 | tf_op jit(solution)/shard_map/chip_sum/pallas_call | solution.py:691
  55.2 2.0 %collective-permute-start.12 = (bf16[256,1152]{1,0:T(8,128)(2,1)S(1)}, bf16[256,1152]{1,0:T(8,128)(2,1)S(1)}, u32[]{:S(2)}, u32[]{:S(2)}) collective-permute-start(bf16[256,1152]{1,0:T(8,128)(2,1)S(1)} %get-tuple-element.70), channel_id=1, source_target_pairs={{0,32},{4,100},{32,0},{36,68},{64,96},{68,36},{96,64},{100,4},{1,3... | collective-permute-start | bytes 1769480 | tf_op jit(solution)/shard_map/ppermute | solution.py:716
  57.3 0.8 collective-permute-start.14
  58.1 2.2 %collective-permute-start.15 = (bf16[48,256]{1,0:T(8,128)(2,1)S(1)}, bf16[48,256]{1,0:T(8,128)(2,1)S(1)}, u32[]{:S(2)}, u32[]{:S(2)}) collective-permute-start(bf16[48,256]{1,0:T(8,128)(2,1)S(1)} %get-tuple-element.76), channel_id=1, source_target_pairs={{1,2},{2,1},{3,0},{0,3},{5,6},{6,5},{7,4},{4,7},{9,10},{10,9},{11,... | collective-permute-start | bytes 73736 | tf_op jit(solution)/shard_map/ppermute | solution.py:710
  60.3 0.9 collective-permute-done.14.near_c
  61.2 1.9 %collective-permute-done.15.far_c = bf16[48,256]{1,0:T(8,128)(2,1)S(1)} collective-permute-done((bf16[48,256]{1,0:T(8,128)(2,1)S(1)}, bf16[48,256]{1,0:T(8,128)(2,1)S(1)}, u32[]{:S(2)}, u32[]{:S(2)}) %collective-permute-start.15) | collective-permute-done | bytes 24608 | tf_op jit(solution)/shard_map/ppermute | solution.py:710
  63.1 2.0 %collective-permute-done.12.came0 = bf16[256,1152]{1,0:T(8,128)(2,1)S(1)} collective-permute-done((bf16[256,1152]{1,0:T(8,128)(2,1)S(1)}, bf16[256,1152]{1,0:T(8,128)(2,1)S(1)}, u32[]{:S(2)}, u32[]{:S(2)}) %collective-permute-start.12) | collective-permute-done | bytes 589856 | tf_op jit(solution)/shard_map/ppermute | solution.py:716
  65.1 1.9 %collective-permute-done.13.came1 = bf16[256,1152]{1,0:T(8,128)(2,1)S(1)} collective-permute-done((bf16[256,1152]{1,0:T(8,128)(2,1)S(1)}, bf16[256,1152]{1,0:T(8,128)(2,1)S(1)}, u32[]{:S(2)}, u32[]{:S(2)}) %collective-permute-start.13) | collective-permute-done | bytes 589856 | tf_op jit(solution)/shard_map/ppermute | solution.py:716
  67.6 2.9 %last.1 = bf16[1,8,32,256]{3,2,1,0:T(8,128)(2,1)} custom-call(bf16[8,32,1024]{2,1,0:T(8,128)(2,1)S(1)} %get-tuple-element.72.g_ref, bf16[2304,1024]{1,0:T(8,128)(2,1)S(1)} %load.1.w_ref, bf16[4,32,256]{2,1,0:T(8,128)(2,1)S(1)} %collective-permute-done.9.near_r, bf16[4,32,256]{2,1,0:T(8,128)(2,1)S(1)} %collective-permute-done.10.far_r, ...), custom_call_target="tpu_custom_call" | custom-call | flops 2000000000 | bytes 5423104 | tf_op jit(solution)/shard_map/last/pallas_call | solution.py:691
  70.5 3.6 %collective-permute-done.16.came0 = bf16[128,1152]{1,0:T(8,128)(2,1)S(1)} collective-permute-done((bf16[128,1152]{1,0:T(8,128)(2,1)S(1)}, bf16[128,1152]{1,0:T(8,128)(2,1)S(1)}, u32[]{:S(2)}, u32[]{:S(2)}) %collective-permute-start.16) | collective-permute-done | bytes 294944 | tf_op jit(solution)/shard_map/ppermute | solution.py:716
  74.2 0.9 quarter.1
  75.2 7.0 %all-to-all-start = ((bf16[16,8,2304]{2,1,0:T(8,128)(2,1)}), bf16[16,8,2304]{2,1,0:T(8,128)(2,1)S(1)}, u32[]{:S(2)}, u32[]{:S(2)}) async-start(bf16[16,8,2304]{2,1,0:T(8,128)(2,1)} %bitcast.1), calls=%async_computation | async-start | bytes 1179648 | tf_op jit(solution)/shard_map/all_to_all | solution.py:880
  82.2 1.3 %maximum_bitcast_fusion = bf16[1,3,8,32,1024]{4,3,2,1,0:T(8,128)(2,1)} fusion(bf16[1,8,32,1024]{3,2,1,0:T(8,128)(2,1)S(1)} %bitcast.11, bf16[1,8,32,1024]{3,2,1,0:T(8,128)(2,1)S(1)} %bitcast.12, bf16[1,8,32,1024]{3,2,1,0:T(8,128)(2,1)S(1)} %bitcast.10), kind=kLoop, calls=%fused_computation | loop fusion | flops 1572864 | bytes 3145728 | tf_op jit(solution)/shard_map/broadcast_in_dim | solution.py:883
  83.5 11.2 %all-to-all-done.parts_ref = bf16[16,8,2304]{2,1,0:T(8,128)(2,1)S(1)} async-done(((bf16[16,8,2304]{2,1,0:T(8,128)(2,1)}), bf16[16,8,2304]{2,1,0:T(8,128)(2,1)S(1)}, u32[]{:S(2)}, u32[]{:S(2)}) %all-to-all-start) | async-done | bytes 589856 | tf_op jit(solution)/shard_map/all_to_all | solution.py:880
  94.8 0.8 total.1
  (30 shorter events, 2.0 us)
Async XLA Ops:
  2.0 6.2 %collective-permute-start = (bf16[18,32,256]{2,1,0:T(8,128)(2,1)S(1)}, bf16[18,32,256]{2,1,0:T(8,128)(2,1)S(1)}, u32[]{:S(2)}, u32[]{:S(2)}) collective-permute-start(bf16[18,32,256]{2,1,0:T(8,128)(2,1)S(1)} %get-tuple-element.48), channel_id=1, source_target_pairs={{0,4},{4,0},{8,12},{12,8},{16,20},{20,16},{24,28},{28,24},{1,5},{5... | collective-permute-start | bytes 884744 | tf_op jit(solution)/shard_map/ppermute | solution.py:706
  2.1 7.5 %copy-start = (bf16[1,3,8,32,1024]{4,3,2,1,0:T(8,128)(2,1)S(1)}, bf16[1,3,8,32,1024]{4,3,2,1,0:T(8,128)(2,1)}, u32[]{:S(2)}) copy-start(bf16[1,3,8,32,1024]{4,3,2,1,0:T(8,128)(2,1)} %x_ref.5) | copy-start | bytes 4718596
  2.1 7.5 %copy-start.1 = (bf16[1,3,8,32,256]{4,3,2,1,0:T(8,128)(2,1)S(1)}, bf16[1,3,8,32,256]{4,3,2,1,0:T(8,128)(2,1)}, u32[]{:S(2)}) copy-start(bf16[1,3,8,32,256]{4,3,2,1,0:T(8,128)(2,1)} %t0_ref.1) | copy-start | bytes 1179652
  2.1 7.5 %copy-start.2 = (f32[1,8,32,256]{3,2,1,0:T(8,128)S(1)}, f32[1,8,32,256]{3,2,1,0:T(8,128)}, u32[]{:S(2)}) copy-start(f32[1,8,32,256]{3,2,1,0:T(8,128)} %c_ref.5) | copy-start | bytes 786436
  2.1 7.5 %copy-start.3 = (bf16[1,8,32,256]{3,2,1,0:T(8,128)(2,1)S(1)}, bf16[1,8,32,256]{3,2,1,0:T(8,128)(2,1)}, u32[]{:S(2)}) copy-start(bf16[1,8,32,256]{3,2,1,0:T(8,128)(2,1)} %h_ref.7) | copy-start | bytes 393220
  2.1 7.4 %collective-permute-start.1 = (bf16[18,32,256]{2,1,0:T(8,128)(2,1)S(1)}, bf16[18,32,256]{2,1,0:T(8,128)(2,1)S(1)}, u32[]{:S(2)}, u32[]{:S(2)}) collective-permute-start(bf16[18,32,256]{2,1,0:T(8,128)(2,1)S(1)} %get-tuple-element.50), channel_id=1, source_target_pairs={{4,8},{8,4},{12,16},{16,12},{20,24},{24,20},{28,0},{0,28},{5,9},{9... | collective-permute-start | bytes 884744 | tf_op jit(solution)/shard_map/ppermute | solution.py:706
  9.8 6.3 %collective-permute-start.2 = (bf16[224,256]{1,0:T(8,128)(2,1)S(1)}, bf16[224,256]{1,0:T(8,128)(2,1)S(1)}, u32[]{:S(2)}, u32[]{:S(2)}) collective-permute-start(bf16[224,256]{1,0:T(8,128)(2,1)S(1)} %get-tuple-element.51), channel_id=1, source_target_pairs={{0,1},{1,0},{2,3},{3,2},{4,5},{5,4},{6,7},{7,6},{8,9},{9,8},{10,11... | collective-permute-start | bytes 344072 | tf_op jit(solution)/shard_map/ppermute | solution.py:710
  11.6 6.0 %collective-permute-start.3 = (bf16[224,256]{1,0:T(8,128)(2,1)S(1)}, bf16[224,256]{1,0:T(8,128)(2,1)S(1)}, u32[]{:S(2)}, u32[]{:S(2)}) collective-permute-start(bf16[224,256]{1,0:T(8,128)(2,1)S(1)} %get-tuple-element.52), channel_id=1, source_target_pairs={{1,2},{2,1},{3,0},{0,3},{5,6},{6,5},{7,4},{4,7},{9,10},{10,9},{11,... | collective-permute-start | bytes 344072 | tf_op jit(solution)/shard_map/ppermute | solution.py:710
  28.3 24.7 %collective-permute-start.11 = (bf16[768,2304]{1,0:T(8,128)(2,1)S(1)}, bf16[768,2304]{1,0:T(8,128)(2,1)S(1)}, u32[]{:S(2)}, u32[]{:S(2)}) collective-permute-start(bf16[768,2304]{1,0:T(8,128)(2,1)S(1)} %bitcast.8), channel_id=1, source_target_pairs={{0,4},{4,0},{1,5},{5,1},{2,6},{6,2},{3,7},{7,3},{8,12},{12,8},{9,1... | collective-permute-start | bytes 10616840 | tf_op jit(solution)/shard_map/ppermute | solution.py:808
  28.3 6.4 %collective-permute-start.4 = (bf16[9,32,256]{2,1,0:T(8,128)(2,1)S(1)}, bf16[9,32,256]{2,1,0:T(8,128)(2,1)S(1)}, u32[]{:S(2)}, u32[]{:S(2)}) collective-permute-start(bf16[9,32,256]{2,1,0:T(8,128)(2,1)S(1)} %get-tuple-element.55), channel_id=1, source_target_pairs={{0,4},{4,0},{8,12},{12,8},{16,20},{20,16},{24,28},{28,24},{1,5},{5... | collective-permute-start | bytes 442376 | tf_op jit(solution)/shard_map/ppermute | solution.py:706
  28.8 5.9 %collective-permute-start.5 = (bf16[9,32,256]{2,1,0:T(8,128)(2,1)S(1)}, bf16[9,32,256]{2,1,0:T(8,128)(2,1)S(1)}, u32[]{:S(2)}, u32[]{:S(2)}) collective-permute-start(bf16[9,32,256]{2,1,0:T(8,128)(2,1)S(1)} %get-tuple-element.56), channel_id=1, source_target_pairs={{4,8},{8,4},{12,16},{16,12},{20,24},{24,20},{28,0},{0,28},{5,9},{9... | collective-permute-start | bytes 442376 | tf_op jit(solution)/shard_map/ppermute | solution.py:706
  34.8 4.3 %collective-permute-start.6 = (bf16[112,256]{1,0:T(8,128)(2,1)S(1)}, bf16[112,256]{1,0:T(8,128)(2,1)S(1)}, u32[]{:S(2)}, u32[]{:S(2)}) collective-permute-start(bf16[112,256]{1,0:T(8,128)(2,1)S(1)} %get-tuple-element.61), channel_id=1, source_target_pairs={{0,1},{1,0},{2,3},{3,2},{4,5},{5,4},{6,7},{7,6},{8,9},{9,8},{10,11... | collective-permute-start | bytes 172040 | tf_op jit(solution)/shard_map/ppermute | solution.py:710
  34.9 5.5 %collective-permute-start.7 = (bf16[112,256]{1,0:T(8,128)(2,1)S(1)}, bf16[112,256]{1,0:T(8,128)(2,1)S(1)}, u32[]{:S(2)}, u32[]{:S(2)}) collective-permute-start(bf16[112,256]{1,0:T(8,128)(2,1)S(1)} %get-tuple-element.62), channel_id=1, source_target_pairs={{1,2},{2,1},{3,0},{0,3},{5,6},{6,5},{7,4},{4,7},{9,10},{10,9},{11,... | collective-permute-start | bytes 172040 | tf_op jit(solution)/shard_map/ppermute | solution.py:710
  48.0 4.9 %collective-permute-start.8 = (bf16[512,768]{1,0:T(8,128)(2,1)S(1)}, bf16[512,768]{1,0:T(8,128)(2,1)S(1)}, u32[]{:S(2)}, u32[]{:S(2)}) collective-permute-start(bf16[512,768]{1,0:T(8,128)(2,1)S(1)} %get-tuple-element.63), channel_id=1, source_target_pairs={{0,4},{4,0},{1,5},{5,1},{2,6},{6,2},{3,7},{7,3},{8,12},{12,8},{9,1... | collective-permute-start | bytes 2359304 | tf_op jit(solution)/shard_map/ppermute | solution.py:842
  48.0 4.9 %collective-permute-start.10 = (bf16[4,32,256]{2,1,0:T(8,128)(2,1)S(1)}, bf16[4,32,256]{2,1,0:T(8,128)(2,1)S(1)}, u32[]{:S(2)}, u32[]{:S(2)}) collective-permute-start(bf16[4,32,256]{2,1,0:T(8,128)(2,1)S(1)} %get-tuple-element.65), channel_id=1, source_target_pairs={{4,8},{8,4},{12,16},{16,12},{20,24},{24,20},{28,0},{0,28},{5,9},{9... | collective-permute-start | bytes 196616 | tf_op jit(solution)/shard_map/ppermute | solution.py:706
  50.5 2.4 %collective-permute-start.9 = (bf16[4,32,256]{2,1,0:T(8,128)(2,1)S(1)}, bf16[4,32,256]{2,1,0:T(8,128)(2,1)S(1)}, u32[]{:S(2)}, u32[]{:S(2)}) collective-permute-start(bf16[4,32,256]{2,1,0:T(8,128)(2,1)S(1)} %get-tuple-element.64), channel_id=1, source_target_pairs={{0,4},{4,0},{8,12},{12,8},{16,20},{20,16},{24,28},{28,24},{1,5},{5... | collective-permute-start | bytes 196616 | tf_op jit(solution)/shard_map/ppermute | solution.py:706
  55.2 10.0 %collective-permute-start.12 = (bf16[256,1152]{1,0:T(8,128)(2,1)S(1)}, bf16[256,1152]{1,0:T(8,128)(2,1)S(1)}, u32[]{:S(2)}, u32[]{:S(2)}) collective-permute-start(bf16[256,1152]{1,0:T(8,128)(2,1)S(1)} %get-tuple-element.70), channel_id=1, source_target_pairs={{0,32},{4,100},{32,0},{36,68},{64,96},{68,36},{96,64},{100,4},{1,3... | collective-permute-start | bytes 1769480 | tf_op jit(solution)/shard_map/ppermute | solution.py:716
  57.2 9.9 %collective-permute-start.13 = (bf16[256,1152]{1,0:T(8,128)(2,1)S(1)}, bf16[256,1152]{1,0:T(8,128)(2,1)S(1)}, u32[]{:S(2)}, u32[]{:S(2)}) collective-permute-start(bf16[256,1152]{1,0:T(8,128)(2,1)S(1)} %get-tuple-element.71), channel_id=1, source_target_pairs={{0,8},{4,28},{8,0},{12,20},{16,24},{20,12},{24,16},{28,4},{1,9},{5... | collective-permute-start | bytes 1769480 | tf_op jit(solution)/shard_map/ppermute | solution.py:716
  57.3 3.9 %collective-permute-start.14 = (bf16[48,256]{1,0:T(8,128)(2,1)S(1)}, bf16[48,256]{1,0:T(8,128)(2,1)S(1)}, u32[]{:S(2)}, u32[]{:S(2)}) collective-permute-start(bf16[48,256]{1,0:T(8,128)(2,1)S(1)} %get-tuple-element.75), channel_id=1, source_target_pairs={{0,1},{1,0},{2,3},{3,2},{4,5},{5,4},{6,7},{7,6},{8,9},{9,8},{10,11... | collective-permute-start | bytes 73736 | tf_op jit(solution)/shard_map/ppermute | solution.py:710
  58.1 5.0 %collective-permute-start.15 = (bf16[48,256]{1,0:T(8,128)(2,1)S(1)}, bf16[48,256]{1,0:T(8,128)(2,1)S(1)}, u32[]{:S(2)}, u32[]{:S(2)}) collective-permute-start(bf16[48,256]{1,0:T(8,128)(2,1)S(1)} %get-tuple-element.76), channel_id=1, source_target_pairs={{1,2},{2,1},{3,0},{0,3},{5,6},{6,5},{7,4},{4,7},{9,10},{10,9},{11,... | collective-permute-start | bytes 73736 | tf_op jit(solution)/shard_map/ppermute | solution.py:710
  67.3 6.8 %collective-permute-start.16 = (bf16[128,1152]{1,0:T(8,128)(2,1)S(1)}, bf16[128,1152]{1,0:T(8,128)(2,1)S(1)}, u32[]{:S(2)}, u32[]{:S(2)}) collective-permute-start(bf16[128,1152]{1,0:T(8,128)(2,1)S(1)} %get-tuple-element.81), channel_id=1, source_target_pairs={{0,8},{4,28},{8,0},{12,20},{16,24},{20,12},{24,16},{28,4},{1,9},{5... | collective-permute-start | bytes 884744 | tf_op jit(solution)/shard_map/ppermute | solution.py:716
  67.4 6.8 %collective-permute-start.17 = (bf16[128,1152]{1,0:T(8,128)(2,1)S(1)}, bf16[128,1152]{1,0:T(8,128)(2,1)S(1)}, u32[]{:S(2)}, u32[]{:S(2)}) collective-permute-start(bf16[128,1152]{1,0:T(8,128)(2,1)S(1)} %get-tuple-element.82), channel_id=1, source_target_pairs={{0,32},{4,100},{32,0},{36,68},{64,96},{68,36},{96,64},{100,4},{1,3... | collective-permute-start | bytes 884744 | tf_op jit(solution)/shard_map/ppermute | solution.py:716
  75.2 19.6 %all-to-all-start = ((bf16[16,8,2304]{2,1,0:T(8,128)(2,1)}), bf16[16,8,2304]{2,1,0:T(8,128)(2,1)S(1)}, u32[]{:S(2)}, u32[]{:S(2)}) async-start(bf16[16,8,2304]{2,1,0:T(8,128)(2,1)} %bitcast.1), calls=%async_computation | async-start | bytes 1179648 | tf_op jit(solution)/shard_map/all_to_all | solution.py:880

commit v7 on v6

--- a/solution.py
+++ b/solution.py
@@ -841,7 +841,6 @@
     near_r, far_r = swap_rows(near_c_rows, far_c_rows)
     got = lax.ppermute(theirs, "core", CORES)
     (own_sum,) = call(own_sum_kernel, (mine, flat_patches), [out((512, 9 * C), F32)], [], name="own_sum", flops=2 * 10**9)
-    got, near_r, far_r = lax.optimization_barrier((got, near_r, far_r))
     sent = call(
         chip_sum_kernel,
         (got, other_patches, own_sum),
@@ -858,11 +857,15 @@
         [vmem((4, L, C), BF)] * 2 + [vmem((col_units_c, C), F32)] * 2,
         name="cols_c",
     )
-    near_c, far_c = swap_cols(near, far)
     came = first_partner(sent[1], "dp"), first_partner(sent[3], "x")
-    *came, near_c, far_c = lax.optimization_barrier((*came, near_c, far_c))
+    near, far, *came = lax.optimization_barrier((near, far, *came))
     sent = call(halve_kernel, (sent[0], came[0], sent[2], came[1]), [out((128, HALF), BF)] * 4, [], name="halve")
     came = first_partner(sent[1], "x"), first_partner(sent[3], "dp")
+    near_c, far_c = swap_cols(near, far)
+    *came, near_c, far_c = lax.optimization_barrier((*came, near_c, far_c))
+    (blocks,) = call(
+        quarter_kernel, (sent[0], came[0], sent[2], came[1]), [out((128, 9 * C), BF)], [], name="quarter"
+    )
     (hidden_grad,) = call(
         last_kernel,
         (g0, recur_weight, near_r, far_r, near_c, far_c),
@@ -872,10 +875,6 @@
         + [vmem(((R + 2) * W, 4 * C), BF), vmem((3, R, 64, C), F32)],
         name="last",
         flops=2 * 10**9,
-    )
-    *came, hidden_grad = lax.optimization_barrier((*came, hidden_grad))
-    (blocks,) = call(
-        quarter_kernel, (sent[0], came[0], sent[2], came[1]), [out((128, 9 * C), BF)], [], name="quarter"
     )
     parts = lax.all_to_all(blocks, AXES, 0, 0, tiled=True, axis_index_groups=owner_groups())
     (total,) = call(total_kernel, (parts.reshape(16, 8, 9 * C),), [out((8, 9 * C), F32)], [], name="total")

time: 95.9 us -> 95.2 us (level)
  waiting for transfers between devices: 29.8 us -> 26 us
  local copies, waits for them, and re-layouts: 0.03 us -> 2.37 us
    ppermute x3, waiting for transfers between devices: 1.45 us -> 9.21 us  [swap_rows(): lax.ppermute(far, axis, ring_pairs(8, 1))]
    ppermute x4, waiting for transfers between devices: 7.66 us -> 0.87 us  [first_partner(): return lax.ppermute(value, (axis, 'core'), pairs)]
    all_to_all x1, waiting for transfers between devices: 11.2 us -> 6 us  [body(): lax.all_to_all(blocks, AXES, 0, 0, tiled=True, axis_index_groups=owner_gr...]
    ppermute x3, starting transfers between devices: 0.6 us -> 4.29 us  [swap_rows(): lax.ppermute(near, axis, ring_pairs(8, 0))]
    unnamed x8 -> x12, local copies, waits for them, and re-layouts: 0.03 us -> 2.37 us
    ppermute x3, starting transfers between devices: 7.69 us -> 5.7 us  [swap_rows(): lax.ppermute(far, axis, ring_pairs(8, 1))]
    all_to_all x1, starting transfers between devices: 7.01 us -> 5.39 us  [body(): lax.all_to_all(blocks, AXES, 0, 0, tiled=True, axis_index_groups=owner_gr...]
  transfers between devices with their start and end apart: 19 -> 19, of which waited for: 13 -> 12; matrix products, arithmetic and copies ran while one was open for 1% -> 1% of each run, Pallas kernels for 21% -> 21%
where the time goes in v7:
time: 95.2 us; the launch traced here: 94.8 us
  Pallas kernels  36.1 us (38%)
  starting transfers between devices  27.6 us (29%)
  waiting for transfers between devices  26 us (27%)
  local copies, waits for them, and re-layouts  2.37 us (2%)
  between operations  1.5 us (2%)
  other arithmetic  1.31 us (1%)
    pallas_call x15, Pallas kernels, call(): pl.pallas_call(kernel, grid=(1,), in_specs=specs, out_specs=[whole(out.sh...  36.1 us
    ppermute x3, waiting for transfers between devices, swap_rows(): lax.ppermute(far, axis, ring_pairs(8, 1))  9.21 us
    ppermute x3, starting transfers between devices, swap_cols(): lax.ppermute(far, 'sx', ring_pairs(4, 1))  6.63 us
    all_to_all x1, waiting for transfers between devices, body(): lax.all_to_all(blocks, AXES, 0, 0, tiled=True, axis_index_groups=owner_gr...  6 us
    ppermute x3, starting transfers between devices, swap_rows(): lax.ppermute(far, axis, ring_pairs(8, 1))  5.7 us
    all_to_all x1, starting transfers between devices, body(): lax.all_to_all(blocks, AXES, 0, 0, tiled=True, axis_index_groups=owner_gr...  5.39 us
    ppermute x3, waiting for transfers between devices, swap_cols(): lax.ppermute(far, 'sx', ring_pairs(4, 1))  4.67 us
    ppermute x3, starting transfers between devices, swap_rows(): lax.ppermute(near, axis, ring_pairs(8, 0))  4.29 us
  transfers between devices with their start and end apart: 19, of which 12 were waited for; matrix products, arithmetic and copies ran while one was open for 1% of the time, Pallas kernels for 21%

profile of v7, /device:TPU:0, one launch (start us, length us, event | category | flops | bytes accessed | tf_op | source)
XLA Modules:
  0.0 94.8 jit_solution(11296141649701219261)
XLA Ops:
  0.6 1.4 %rows_a.1 = (bf16[18,32,256]{2,1,0:T(8,128)(2,1)S(1)}, bf16[18,32,256]{2,1,0:T(8,128)(2,1)S(1)}) custom-call(bf16[1,8,32,256]{3,2,1,0:T(8,128)(2,1)} %h_ref.7, f32[1,8,32,256]{3,2,1,0:T(8,128)} %c_ref.5, bf16[1,3,8,32,1024]{4,3,2,1,0:T(8,128)(2,1)} %x_ref.5, bf16[1,3,8,32,256]{4,3,2,1,0:T(8,128)(2,1)} %t0_ref.1), custom_call_target="tpu_custom_call" | custom-call | bytes 2359296 | tf_op jit(solution)/shard_map/rows_a/pallas_call | solution.py:691
  2.1 3.0 %collective-permute-start.1 = (bf16[18,32,256]{2,1,0:T(8,128)(2,1)S(1)}, bf16[18,32,256]{2,1,0:T(8,128)(2,1)S(1)}, u32[]{:S(2)}, u32[]{:S(2)}) collective-permute-start(bf16[18,32,256]{2,1,0:T(8,128)(2,1)S(1)} %get-tuple-element.48), channel_id=1, source_target_pairs={{4,8},{8,4},{12,16},{16,12},{20,24},{24,20},{28,0},{0,28},{5,9},{9... | collective-permute-start | bytes 884744 | tf_op jit(solution)/shard_map/ppermute | solution.py:706
  5.2 2.4 %load.1.w_ref = bf16[2304,1024]{1,0:T(8,128)(2,1)S(1)} custom-call(bf16[2304,1024]{1,0:T(8,128)(2,1)} %w_hbm), custom_call_target="tpu_custom_call" | custom-call | bytes 4718592 | tf_op jit(solution)/shard_map/load/pallas_call | solution.py:691
  8.2 1.4 %collective-permute-done.1.far_r = bf16[18,32,256]{2,1,0:T(8,128)(2,1)S(1)} collective-permute-done((bf16[18,32,256]{2,1,0:T(8,128)(2,1)S(1)}, bf16[18,32,256]{2,1,0:T(8,128)(2,1)S(1)}, u32[]{:S(2)}, u32[]{:S(2)}) %collective-permute-start.1) | collective-permute-done | bytes 294944 | tf_op jit(solution)/shard_map/ppermute | solution.py:706
  9.8 1.8 %collective-permute-start.2 = (bf16[224,256]{1,0:T(8,128)(2,1)S(1)}, bf16[224,256]{1,0:T(8,128)(2,1)S(1)}, u32[]{:S(2)}, u32[]{:S(2)}) collective-permute-start(bf16[224,256]{1,0:T(8,128)(2,1)S(1)} %get-tuple-element.49), channel_id=1, source_target_pairs={{0,1},{1,0},{2,3},{3,2},{4,5},{5,4},{6,7},{7,6},{8,9},{9,8},{10,11... | collective-permute-start | bytes 344072 | tf_op jit(solution)/shard_map/ppermute | solution.py:710
  11.6 2.2 %collective-permute-start.3 = (bf16[224,256]{1,0:T(8,128)(2,1)S(1)}, bf16[224,256]{1,0:T(8,128)(2,1)S(1)}, u32[]{:S(2)}, u32[]{:S(2)}) collective-permute-start(bf16[224,256]{1,0:T(8,128)(2,1)S(1)} %get-tuple-element.50), channel_id=1, source_target_pairs={{1,2},{2,1},{3,0},{0,3},{5,6},{6,5},{7,4},{4,7},{9,10},{10,9},{11,... | collective-permute-start | bytes 344072 | tf_op jit(solution)/shard_map/ppermute | solution.py:710
  13.8 2.4 %ahead.1.main_ref = f32[384,1024]{1,0:T(8,128)S(1)} custom-call(bf16[1,8,32,256]{3,2,1,0:T(8,128)(2,1)S(1)} %copy-done.5, bf16[2304,1024]{1,0:T(8,128)(2,1)S(1)} %load.1.w_ref, bf16[18,32,256]{2,1,0:T(8,128)(2,1)S(1)} %collective-permute-done.near_r, bf16[18,32,256]{2,1,0:T(8,128)(2,1)S(1)} %collective-permute-done.1.far_r), custom_call_target="tpu_custom_call" | custom-call | flops 2000000000 | bytes 5439488 | tf_op jit(solution)/shard_map/ahead/pallas_call | solution.py:691
  16.2 1.4 %collective-permute-done.3.far_c = bf16[224,256]{1,0:T(8,128)(2,1)S(1)} collective-permute-done((bf16[224,256]{1,0:T(8,128)(2,1)S(1)}, bf16[224,256]{1,0:T(8,128)(2,1)S(1)}, u32[]{:S(2)}, u32[]{:S(2)}) %collective-permute-start.3) | collective-permute-done | bytes 114720 | tf_op jit(solution)/shard_map/ppermute | solution.py:710
  17.6 10.6 %forward.1 = (bf16[1,3,8,32,256]{4,3,2,1,0:T(8,128)(2,1)}, bf16[3,256,2304]{2,1,0:T(8,128)(2,1)S(1)}, bf16[6,10,48,256]{3,2,1,0:T(8,128)(2,1)S(1)}, bf16[6,8,32,...) custom-call(s32[1]{0:T(128)S(6)} %copy.11.count_ref, ...), custom_call_target="tpu_custom_call" | custom-call | flops 6000000000 | bytes 9469956 | tf_op jit(solution)/shard_map/forward/pallas_call | solution.py:691
  28.8 2.2 %collective-permute-start.5 = (bf16[9,32,256]{2,1,0:T(8,128)(2,1)S(1)}, bf16[9,32,256]{2,1,0:T(8,128)(2,1)S(1)}, u32[]{:S(2)}, u32[]{:S(2)}) collective-permute-start(bf16[9,32,256]{2,1,0:T(8,128)(2,1)S(1)} %get-tuple-element.54), channel_id=1, source_target_pairs={{4,8},{8,4},{12,16},{16,12},{20,24},{24,20},{28,0},{0,28},{5,9},{9... | collective-permute-start | bytes 442376 | tf_op jit(solution)/shard_map/ppermute | solution.py:706
  31.0 3.7 %collective-permute-done.4.near_r = bf16[9,32,256]{2,1,0:T(8,128)(2,1)S(1)} collective-permute-done((bf16[9,32,256]{2,1,0:T(8,128)(2,1)S(1)}, bf16[9,32,256]{2,1,0:T(8,128)(2,1)S(1)}, u32[]{:S(2)}, u32[]{:S(2)}) %collective-permute-start.4) | collective-permute-done | bytes 147488 | tf_op jit(solution)/shard_map/ppermute | solution.py:706
  34.9 2.3 %collective-permute-start.7 = (bf16[112,256]{1,0:T(8,128)(2,1)S(1)}, bf16[112,256]{1,0:T(8,128)(2,1)S(1)}, u32[]{:S(2)}, u32[]{:S(2)}) collective-permute-start(bf16[112,256]{1,0:T(8,128)(2,1)S(1)} %get-tuple-element.60), channel_id=1, source_target_pairs={{1,2},{2,1},{3,0},{0,3},{5,6},{6,5},{7,4},{4,7},{9,10},{10,9},{11,... | collective-permute-start | bytes 172040 | tf_op jit(solution)/shard_map/ppermute | solution.py:710
  37.2 1.7 %ahead_back.1.zmain_ref = f32[3,10,32,256]{3,2,1,0:T(8,128)S(1)} custom-call(bf16[8,32,1024]{2,1,0:T(8,128)(2,1)S(1)} %get-tuple-element.52.g_ref.g2_ref, bf16[2304,1024]{1,0:T(8,128)(2,1)S(1)} %load.1.w_ref, bf16[9,32,256]{2,1,0:T(8,128)(2,1)S(1)} %collective-permute-done.4.near_r, bf16[9,32,256]{2,1,0:T(8,128)(2,1)S(1)} %collective-permute-done.5.far_r), custom_call_target="tpu_custom_call" | custom-call | flops 2000000000 | bytes 5537792 | tf_op jit(solution)/shard_map/ahead_back/pallas_call | solution.py:691
  39.1 1.3 %collective-permute-done.7.far_c = bf16[112,256]{1,0:T(8,128)(2,1)S(1)} collective-permute-done((bf16[112,256]{1,0:T(8,128)(2,1)S(1)}, bf16[112,256]{1,0:T(8,128)(2,1)S(1)}, u32[]{:S(2)}, u32[]{:S(2)}) %collective-permute-start.7) | collective-permute-done | bytes 57376 | tf_op jit(solution)/shard_map/ppermute | solution.py:710
  40.4 7.7 %backward.1 = (bf16[8,32,1024]{2,1,0:T(8,128)(2,1)S(1)}, bf16[8,32,1024]{2,1,0:T(8,128)(2,1)S(1)}, f32[1,8,32,256]{3,2,1,0:T(8,128)}, f32[1,8,32,256]{3,2,1,0:T(...) custom-call(s32[1]{0:T(128)S(6)} %copy.11.count_ref, ...), custom_call_target="tpu_custom_call" | custom-call | flops 4000000000 | bytes 9797636 | tf_op jit(solution)/shard_map/backward/pallas_call | solution.py:691
  48.1 2.4 %own_sum.1.own_ref = f32[512,2304]{1,0:T(8,128)S(1)} custom-call(bf16[512,768]{1,0:T(8,128)(2,1)S(1)} %get-tuple-element.63.mine_ref, bf16[768,2304]{1,0:T(8,128)(2,1)S(1)} %bitcast.9), custom_call_target="tpu_custom_call" | custom-call | flops 2000000000 | bytes 4325376 | tf_op jit(solution)/shard_map/own_sum/pallas_call | solution.py:691
  50.4 2.2 %chip_sum.1 = (bf16[256,1152]{1,0:T(8,128)(2,1)S(1)}, bf16[256,1152]{1,0:T(8,128)(2,1)S(1)}, bf16[256,1152]{1,0:T(8,128)(2,1)S(1)}, bf16[256,1152]{1,0:T(8,128)(2,1)S(1)}) custom-call(bf16[512,768]{1,0:T(8,128)(2,1)S(1)} %collective-permute-done.8.got_ref, bf16[768,2304]{1,0:T(8,128)(2,1)S(1)} %collective-permute-done.9.p_ref, f32[512,2304]{1,0:T(8,128)S(1)} %own_sum.1.own_ref), custom_call_target="tpu_custom_call" | custom-call | flops 2000000000 | bytes 9043968 | tf_op jit(solution)/shard_map/chip_sum/pallas_call | solution.py:691
  52.7 2.0 %collective-permute-start.12 = (bf16[256,1152]{1,0:T(8,128)(2,1)S(1)}, bf16[256,1152]{1,0:T(8,128)(2,1)S(1)}, u32[]{:S(2)}, u32[]{:S(2)}) collective-permute-start(bf16[256,1152]{1,0:T(8,128)(2,1)S(1)} %get-tuple-element.70), channel_id=1, source_target_pairs={{0,32},{4,100},{32,0},{36,68},{64,96},{68,36},{96,64},{100,4},{1,3... | collective-permute-start | bytes 1769480 | tf_op jit(solution)/shard_map/ppermute | solution.py:716
  55.4 3.7 %collective-permute-start.10 = (bf16[4,32,256]{2,1,0:T(8,128)(2,1)S(1)}, bf16[4,32,256]{2,1,0:T(8,128)(2,1)S(1)}, u32[]{:S(2)}, u32[]{:S(2)}) collective-permute-start(bf16[4,32,256]{2,1,0:T(8,128)(2,1)S(1)} %get-tuple-element.66), channel_id=1, source_target_pairs={{0,4},{4,0},{8,12},{12,8},{16,20},{20,16},{24,28},{28,24},{1,5},{5... | collective-permute-start | bytes 196616 | tf_op jit(solution)/shard_map/ppermute | solution.py:706
  60.0 7.8 %collective-permute-done.11.far_r = bf16[4,32,256]{2,1,0:T(8,128)(2,1)S(1)} collective-permute-done((bf16[4,32,256]{2,1,0:T(8,128)(2,1)S(1)}, bf16[4,32,256]{2,1,0:T(8,128)(2,1)S(1)}, u32[]{:S(2)}, u32[]{:S(2)}) %collective-permute-start.11) | collective-permute-done | bytes 65568 | tf_op jit(solution)/shard_map/ppermute | solution.py:706
  68.4 0.8 collective-permute-start.16
  69.2 2.2 %collective-permute-start.17 = (bf16[48,256]{1,0:T(8,128)(2,1)S(1)}, bf16[48,256]{1,0:T(8,128)(2,1)S(1)}, u32[]{:S(2)}, u32[]{:S(2)}) collective-permute-start(bf16[48,256]{1,0:T(8,128)(2,1)S(1)} %get-tuple-element.79), channel_id=1, source_target_pairs={{1,2},{2,1},{3,0},{0,3},{5,6},{6,5},{7,4},{4,7},{9,10},{10,9},{11,... | collective-permute-start | bytes 73736 | tf_op jit(solution)/shard_map/ppermute | solution.py:710
  71.4 0.9 collective-permute-done.16.near_c
  72.3 1.9 %collective-permute-done.17.far_c = bf16[48,256]{1,0:T(8,128)(2,1)S(1)} collective-permute-done((bf16[48,256]{1,0:T(8,128)(2,1)S(1)}, bf16[48,256]{1,0:T(8,128)(2,1)S(1)}, u32[]{:S(2)}, u32[]{:S(2)}) %collective-permute-start.17) | collective-permute-done | bytes 24608 | tf_op jit(solution)/shard_map/ppermute | solution.py:710
  74.2 0.8 collective-permute-done.14.came0
  75.1 1.0 %quarter.1 = bf16[128,2304]{1,0:T(8,128)(2,1)} custom-call(bf16[128,1152]{1,0:T(8,128)(2,1)S(1)} %get-tuple-element.75.kept0, bf16[128,1152]{1,0:T(8,128)(2,1)S(1)} %collective-permute-done.14.came0, bf16[128,1152]{1,0:T(8,128)(2,1)S(1)} %get-tuple-element.81.kept1, bf16[128,1152]{1,0:T(8,128)(2,1)S(1)} %collective-permute-done.15.came1), custom_call_target="tpu_custom_call" | custom-call | bytes 1179648 | tf_op jit(solution)/shard_map/quarter/pallas_call | solution.py:691
  76.1 5.4 %all-to-all-start = ((bf16[16,8,2304]{2,1,0:T(8,128)(2,1)}), bf16[16,8,2304]{2,1,0:T(8,128)(2,1)S(1)}, u32[]{:S(2)}, u32[]{:S(2)}) async-start(bf16[16,8,2304]{2,1,0:T(8,128)(2,1)} %bitcast.1), calls=%async_computation | async-start | bytes 1179648 | tf_op jit(solution)/shard_map/all_to_all | solution.py:879
  81.5 1.3 %maximum_bitcast_fusion = bf16[1,3,8,32,1024]{4,3,2,1,0:T(8,128)(2,1)} fusion(bf16[1,8,32,1024]{3,2,1,0:T(8,128)(2,1)S(1)} %bitcast.11, bf16[1,8,32,1024]{3,2,1,0:T(8,128)(2,1)S(1)} %bitcast.12, bf16[1,8,32,1024]{3,2,1,0:T(8,128)(2,1)S(1)} %bitcast.10), kind=kLoop, calls=%fused_computation | loop fusion | flops 1572864 | bytes 3145728 | tf_op jit(solution)/shard_map/broadcast_in_dim | solution.py:882
  82.8 2.3 %copy-done.2 = bf16[2304,1024]{1,0:T(8,128)(2,1)S(1)} copy-done((bf16[2304,1024]{1,0:T(8,128)(2,1)S(1)}, bf16[2304,1024]{1,0:T(8,128)(2,1)}, u32[]{:S(2)}) %copy-start.2) | copy-done | bytes 4718616
  85.1 2.9 %last.1 = bf16[1,8,32,256]{3,2,1,0:T(8,128)(2,1)} custom-call(bf16[8,32,1024]{2,1,0:T(8,128)(2,1)S(1)} %get-tuple-element.65.g_ref, bf16[2304,1024]{1,0:T(8,128)(2,1)S(1)} %copy-done.2, bf16[4,32,256]{2,1,0:T(8,128)(2,1)S(1)} %collective-permute-done.10.near_r, bf16[4,32,256]{2,1,0:T(8,128)(2,1)S(1)} %collective-permute-done.11.far_r, ...), custom_call_target="tpu_custom_call" | custom-call | flops 2000000000 | bytes 5423104 | tf_op jit(solution)/shard_map/last/pallas_call | solution.py:691
  88.0 6.0 %all-to-all-done.parts_ref = bf16[16,8,2304]{2,1,0:T(8,128)(2,1)S(1)} async-done(((bf16[16,8,2304]{2,1,0:T(8,128)(2,1)}), bf16[16,8,2304]{2,1,0:T(8,128)(2,1)S(1)}, u32[]{:S(2)}, u32[]{:S(2)}) %all-to-all-start) | async-done | bytes 589856 | tf_op jit(solution)/shard_map/all_to_all | solution.py:879
  94.0 0.8 total.1
  (34 shorter events, 3.4 us)
Async XLA Ops:
  2.0 6.2 %collective-permute-start = (bf16[18,32,256]{2,1,0:T(8,128)(2,1)S(1)}, bf16[18,32,256]{2,1,0:T(8,128)(2,1)S(1)}, u32[]{:S(2)}, u32[]{:S(2)}) collective-permute-start(bf16[18,32,256]{2,1,0:T(8,128)(2,1)S(1)} %get-tuple-element.46), channel_id=1, source_target_pairs={{0,4},{4,0},{8,12},{12,8},{16,20},{20,16},{24,28},{28,24},{1,5},{5... | collective-permute-start | bytes 884744 | tf_op jit(solution)/shard_map/ppermute | solution.py:706
  2.1 7.5 %copy-start = (bf16[1,3,8,32,1024]{4,3,2,1,0:T(8,128)(2,1)S(1)}, bf16[1,3,8,32,1024]{4,3,2,1,0:T(8,128)(2,1)}, u32[]{:S(2)}) copy-start(bf16[1,3,8,32,1024]{4,3,2,1,0:T(8,128)(2,1)} %x_ref.5) | copy-start | bytes 4718596
  2.1 7.5 %copy-start.3 = (bf16[1,3,8,32,256]{4,3,2,1,0:T(8,128)(2,1)S(1)}, bf16[1,3,8,32,256]{4,3,2,1,0:T(8,128)(2,1)}, u32[]{:S(2)}) copy-start(bf16[1,3,8,32,256]{4,3,2,1,0:T(8,128)(2,1)} %t0_ref.1) | copy-start | bytes 1179652
  2.1 7.5 %copy-start.4 = (f32[1,8,32,256]{3,2,1,0:T(8,128)S(1)}, f32[1,8,32,256]{3,2,1,0:T(8,128)}, u32[]{:S(2)}) copy-start(f32[1,8,32,256]{3,2,1,0:T(8,128)} %c_ref.5) | copy-start | bytes 786436
  2.1 7.5 %copy-start.5 = (bf16[1,8,32,256]{3,2,1,0:T(8,128)(2,1)S(1)}, bf16[1,8,32,256]{3,2,1,0:T(8,128)(2,1)}, u32[]{:S(2)}) copy-start(bf16[1,8,32,256]{3,2,1,0:T(8,128)(2,1)} %h_ref.7) | copy-start | bytes 393220
  2.1 7.4 %collective-permute-start.1 = (bf16[18,32,256]{2,1,0:T(8,128)(2,1)S(1)}, bf16[18,32,256]{2,1,0:T(8,128)(2,1)S(1)}, u32[]{:S(2)}, u32[]{:S(2)}) collective-permute-start(bf16[18,32,256]{2,1,0:T(8,128)(2,1)S(1)} %get-tuple-element.48), channel_id=1, source_target_pairs={{4,8},{8,4},{12,16},{16,12},{20,24},{24,20},{28,0},{0,28},{5,9},{9... | collective-permute-start | bytes 884744 | tf_op jit(solution)/shard_map/ppermute | solution.py:706
  7.6 32.8 %copy-start.1 = (bf16[2304,1024]{1,0:T(8,128)(2,1)}, bf16[2304,1024]{1,0:T(8,128)(2,1)S(1)}, u32[]{:S(2)}) copy-start(bf16[2304,1024]{1,0:T(8,128)(2,1)S(1)} %load.1.w_ref) | copy-start | bytes 14155780
  9.8 6.3 %collective-permute-start.2 = (bf16[224,256]{1,0:T(8,128)(2,1)S(1)}, bf16[224,256]{1,0:T(8,128)(2,1)S(1)}, u32[]{:S(2)}, u32[]{:S(2)}) collective-permute-start(bf16[224,256]{1,0:T(8,128)(2,1)S(1)} %get-tuple-element.49), channel_id=1, source_target_pairs={{0,1},{1,0},{2,3},{3,2},{4,5},{5,4},{6,7},{7,6},{8,9},{9,8},{10,11... | collective-permute-start | bytes 344072 | tf_op jit(solution)/shard_map/ppermute | solution.py:710
  11.6 6.0 %collective-permute-start.3 = (bf16[224,256]{1,0:T(8,128)(2,1)S(1)}, bf16[224,256]{1,0:T(8,128)(2,1)S(1)}, u32[]{:S(2)}, u32[]{:S(2)}) collective-permute-start(bf16[224,256]{1,0:T(8,128)(2,1)S(1)} %get-tuple-element.50), channel_id=1, source_target_pairs={{1,2},{2,1},{3,0},{0,3},{5,6},{6,5},{7,4},{4,7},{9,10},{10,9},{11,... | collective-permute-start | bytes 344072 | tf_op jit(solution)/shard_map/ppermute | solution.py:710
  28.3 22.2 %collective-permute-start.9 = (bf16[768,2304]{1,0:T(8,128)(2,1)S(1)}, bf16[768,2304]{1,0:T(8,128)(2,1)S(1)}, u32[]{:S(2)}, u32[]{:S(2)}) collective-permute-start(bf16[768,2304]{1,0:T(8,128)(2,1)S(1)} %bitcast.8), channel_id=1, source_target_pairs={{0,4},{4,0},{1,5},{5,1},{2,6},{6,2},{3,7},{7,3},{8,12},{12,8},{9,1... | collective-permute-start | bytes 10616840 | tf_op jit(solution)/shard_map/ppermute | solution.py:808
  28.3 6.4 %collective-permute-start.4 = (bf16[9,32,256]{2,1,0:T(8,128)(2,1)S(1)}, bf16[9,32,256]{2,1,0:T(8,128)(2,1)S(1)}, u32[]{:S(2)}, u32[]{:S(2)}) collective-permute-start(bf16[9,32,256]{2,1,0:T(8,128)(2,1)S(1)} %get-tuple-element.53), channel_id=1, source_target_pairs={{0,4},{4,0},{8,12},{12,8},{16,20},{20,16},{24,28},{28,24},{1,5},{5... | collective-permute-start | bytes 442376 | tf_op jit(solution)/shard_map/ppermute | solution.py:706
  28.8 5.9 %collective-permute-start.5 = (bf16[9,32,256]{2,1,0:T(8,128)(2,1)S(1)}, bf16[9,32,256]{2,1,0:T(8,128)(2,1)S(1)}, u32[]{:S(2)}, u32[]{:S(2)}) collective-permute-start(bf16[9,32,256]{2,1,0:T(8,128)(2,1)S(1)} %get-tuple-element.54), channel_id=1, source_target_pairs={{4,8},{8,4},{12,16},{16,12},{20,24},{24,20},{28,0},{0,28},{5,9},{9... | collective-permute-start | bytes 442376 | tf_op jit(solution)/shard_map/ppermute | solution.py:706
  34.8 4.3 %collective-permute-start.6 = (bf16[112,256]{1,0:T(8,128)(2,1)S(1)}, bf16[112,256]{1,0:T(8,128)(2,1)S(1)}, u32[]{:S(2)}, u32[]{:S(2)}) collective-permute-start(bf16[112,256]{1,0:T(8,128)(2,1)S(1)} %get-tuple-element.59), channel_id=1, source_target_pairs={{0,1},{1,0},{2,3},{3,2},{4,5},{5,4},{6,7},{7,6},{8,9},{9,8},{10,11... | collective-permute-start | bytes 172040 | tf_op jit(solution)/shard_map/ppermute | solution.py:710
  34.9 5.5 %collective-permute-start.7 = (bf16[112,256]{1,0:T(8,128)(2,1)S(1)}, bf16[112,256]{1,0:T(8,128)(2,1)S(1)}, u32[]{:S(2)}, u32[]{:S(2)}) collective-permute-start(bf16[112,256]{1,0:T(8,128)(2,1)S(1)} %get-tuple-element.60), channel_id=1, source_target_pairs={{1,2},{2,1},{3,0},{0,3},{5,6},{6,5},{7,4},{4,7},{9,10},{10,9},{11,... | collective-permute-start | bytes 172040 | tf_op jit(solution)/shard_map/ppermute | solution.py:710
  48.0 2.4 %collective-permute-start.8 = (bf16[512,768]{1,0:T(8,128)(2,1)S(1)}, bf16[512,768]{1,0:T(8,128)(2,1)S(1)}, u32[]{:S(2)}, u32[]{:S(2)}) collective-permute-start(bf16[512,768]{1,0:T(8,128)(2,1)S(1)} %get-tuple-element.61), channel_id=1, source_target_pairs={{0,4},{4,0},{1,5},{5,1},{2,6},{6,2},{3,7},{7,3},{8,12},{12,8},{9,1... | collective-permute-start | bytes 2359304 | tf_op jit(solution)/shard_map/ppermute | solution.py:842
  52.7 15.2 %collective-permute-start.12 = (bf16[256,1152]{1,0:T(8,128)(2,1)S(1)}, bf16[256,1152]{1,0:T(8,128)(2,1)S(1)}, u32[]{:S(2)}, u32[]{:S(2)}) collective-permute-start(bf16[256,1152]{1,0:T(8,128)(2,1)S(1)} %get-tuple-element.70), channel_id=1, source_target_pairs={{0,32},{4,100},{32,0},{36,68},{64,96},{68,36},{96,64},{100,4},{1,3... | collective-permute-start | bytes 1769480 | tf_op jit(solution)/shard_map/ppermute | solution.py:716
  54.7 13.3 %collective-permute-start.13 = (bf16[256,1152]{1,0:T(8,128)(2,1)S(1)}, bf16[256,1152]{1,0:T(8,128)(2,1)S(1)}, u32[]{:S(2)}, u32[]{:S(2)}) collective-permute-start(bf16[256,1152]{1,0:T(8,128)(2,1)S(1)} %get-tuple-element.71), channel_id=1, source_target_pairs={{0,8},{4,28},{8,0},{12,20},{16,24},{20,12},{24,16},{28,4},{1,9},{5... | collective-permute-start | bytes 1769480 | tf_op jit(solution)/shard_map/ppermute | solution.py:716
  55.4 4.6 %collective-permute-start.10 = (bf16[4,32,256]{2,1,0:T(8,128)(2,1)S(1)}, bf16[4,32,256]{2,1,0:T(8,128)(2,1)S(1)}, u32[]{:S(2)}, u32[]{:S(2)}) collective-permute-start(bf16[4,32,256]{2,1,0:T(8,128)(2,1)S(1)} %get-tuple-element.66), channel_id=1, source_target_pairs={{0,4},{4,0},{8,12},{12,8},{16,20},{20,16},{24,28},{28,24},{1,5},{5... | collective-permute-start | bytes 196616 | tf_op jit(solution)/shard_map/ppermute | solution.py:706
  59.1 8.7 %collective-permute-start.11 = (bf16[4,32,256]{2,1,0:T(8,128)(2,1)S(1)}, bf16[4,32,256]{2,1,0:T(8,128)(2,1)S(1)}, u32[]{:S(2)}, u32[]{:S(2)}) collective-permute-start(bf16[4,32,256]{2,1,0:T(8,128)(2,1)S(1)} %get-tuple-element.67), channel_id=1, source_target_pairs={{4,8},{8,4},{12,16},{16,12},{20,24},{24,20},{28,0},{0,28},{5,9},{9... | collective-permute-start | bytes 196616 | tf_op jit(solution)/shard_map/ppermute | solution.py:706
  68.2 6.8 %collective-permute-start.14 = (bf16[128,1152]{1,0:T(8,128)(2,1)S(1)}, bf16[128,1152]{1,0:T(8,128)(2,1)S(1)}, u32[]{:S(2)}, u32[]{:S(2)}) collective-permute-start(bf16[128,1152]{1,0:T(8,128)(2,1)S(1)} %get-tuple-element.76), channel_id=1, source_target_pairs={{0,8},{4,28},{8,0},{12,20},{16,24},{20,12},{24,16},{28,4},{1,9},{5... | collective-permute-start | bytes 884744 | tf_op jit(solution)/shard_map/ppermute | solution.py:716
  68.3 6.8 %collective-permute-start.15 = (bf16[128,1152]{1,0:T(8,128)(2,1)S(1)}, bf16[128,1152]{1,0:T(8,128)(2,1)S(1)}, u32[]{:S(2)}, u32[]{:S(2)}) collective-permute-start(bf16[128,1152]{1,0:T(8,128)(2,1)S(1)} %get-tuple-element.77), channel_id=1, source_target_pairs={{0,32},{4,100},{32,0},{36,68},{64,96},{68,36},{96,64},{100,4},{1,3... | collective-permute-start | bytes 884744 | tf_op jit(solution)/shard_map/ppermute | solution.py:716
  68.4 3.9 %collective-permute-start.16 = (bf16[48,256]{1,0:T(8,128)(2,1)S(1)}, bf16[48,256]{1,0:T(8,128)(2,1)S(1)}, u32[]{:S(2)}, u32[]{:S(2)}) collective-permute-start(bf16[48,256]{1,0:T(8,128)(2,1)S(1)} %get-tuple-element.78), channel_id=1, source_target_pairs={{0,1},{1,0},{2,3},{3,2},{4,5},{5,4},{6,7},{7,6},{8,9},{9,8},{10,11... | collective-permute-start | bytes 73736 | tf_op jit(solution)/shard_map/ppermute | solution.py:710
  69.2 5.0 %collective-permute-start.17 = (bf16[48,256]{1,0:T(8,128)(2,1)S(1)}, bf16[48,256]{1,0:T(8,128)(2,1)S(1)}, u32[]{:S(2)}, u32[]{:S(2)}) collective-permute-start(bf16[48,256]{1,0:T(8,128)(2,1)S(1)} %get-tuple-element.79), channel_id=1, source_target_pairs={{1,2},{2,1},{3,0},{0,3},{5,6},{6,5},{7,4},{4,7},{9,10},{10,9},{11,... | collective-permute-start | bytes 73736 | tf_op jit(solution)/shard_map/ppermute | solution.py:710
  76.1 18.0 %all-to-all-start = ((bf16[16,8,2304]{2,1,0:T(8,128)(2,1)}), bf16[16,8,2304]{2,1,0:T(8,128)(2,1)S(1)}, u32[]{:S(2)}, u32[]{:S(2)}) async-start(bf16[16,8,2304]{2,1,0:T(8,128)(2,1)} %bitcast.1), calls=%async_computation | async-start | bytes 1179648 | tf_op jit(solution)/shard_map/all_to_all | solution.py:879
  82.8 2.3 %copy-start.2 = (bf16[2304,1024]{1,0:T(8,128)(2,1)S(1)}, bf16[2304,1024]{1,0:T(8,128)(2,1)}, u32[]{:S(2)}) copy-start(bf16[2304,1024]{1,0:T(8,128)(2,1)} %copy-done.1) | copy-start | bytes 14155780
